TPU v7x, 768 devices: a whole 4x8x12 slice. The times are simulated.
768 devices in a mesh: dp: 32 (over y, x), expert: 12 (over z), tensor: 2 (over core).
Axes of the slice: x: 4, y: 8, z: 12, core: 2. Of those that a mesh axis runs over, the one named last changes fastest.
Arguments:
- tokens: bfloat16 [49152, 2048], P(('dp', 'expert'), 'tensor'), may hold values from -6 to 6
- expert_ids: int32 [49152, 8], P(('dp', 'expert')), may hold values from 0 to 127, as said below
- route_weight: float32 [49152, 8], P(('dp', 'expert')), may hold values from 0.2 to 1
- gate_weight: bfloat16 [12, 2048, 768], P('expert', None, 'tensor'), may hold values from -0.125 to 0.125
- up_weight: bfloat16 [12, 2048, 768], P('expert', None, 'tensor'), may hold values from -0.125 to 0.125
- down_weight: bfloat16 [12, 768, 2048], P('expert', 'tensor'), may hold values from -0.21875 to 0.21875
- cotangent: bfloat16 [49152, 2048], P(('dp', 'expert'), 'tensor'), may hold values from -6 to 6
Outputs:
- mixed: bfloat16 [49152, 2048], P(('dp', 'expert'), 'tensor')
- token_grad: bfloat16 [49152, 2048], P(('dp', 'expert'), 'tensor')
- down_grad: bfloat16 [12, 768, 2048], P('expert', 'tensor', 'dp')
Inputs may be any that keep to these rules, and one draw needn't show every extreme that they name: `expert_ids`: among the rows of one device, at most 12 pairs choose the same expert; in every replica some expert below 12 is chosen by exactly 12 pairs on each of the replica's 12 devices; a token's choices are distinct.
All inputs are finite; a program needn't handle non-finite values.
Results may differ from a plain program's by a relative error of at most 0.017.
Values may be sent and summed in bfloat16 or wider, within the bound.
No kernel may reach another device: no remote copies, remote signals or barrier semaphores. Data moves between devices by JAX's collectives and lax.ppermute only.
A program may use at most 32 MiB of HBM per device.

v0:
```python
import functools
import math

import jax
import jax.numpy as jnp
from jax import lax
from jax.experimental import pallas as pl
from jax.experimental.pallas import tpu as pltpu
from jax.sharding import PartitionSpec as P

EXPERTS = 128
NX = 4
B16 = jnp.bfloat16
F32 = jnp.float32
ROWS0 = (((0,), (0,)), ((), ()))
COLS1 = (((1,), (1,)), ((), ()))


def dot(a, b, dims=None):
    if dims is None:
        dims = (((1,), (0,)), ((), ()))
    return lax.dot_general(a, b, dims, preferred_element_type=F32)


def hbm(v):
    return pltpu.with_memory_space_constraint(v, pltpu.HBM)


def fused(kernel, outs, *args, scalars=0, flops=0, mib=8):
    specs = [pl.BlockSpec(memory_space=pltpu.SMEM)] * scalars
    specs += [pl.BlockSpec(memory_space=pltpu.VMEM)] * (len(args) - scalars)
    nbytes = sum(math.prod(a.shape) * a.dtype.itemsize for a in list(args) + list(outs))
    return pl.pallas_call(
        kernel,
        out_shape=outs,
        in_specs=specs,
        out_specs=[pl.BlockSpec(memory_space=pltpu.VMEM)] * len(outs),
        compiler_params=pltpu.CompilerParams(vmem_limit_bytes=mib << 20),
        cost_estimate=pl.CostEstimate(flops=flops, bytes_accessed=nbytes, transcendentals=0),
    )(*args)


def routing(ids_ref, w_ref, owners, cap):
    choose, toks = ids_ref.shape
    expert = lax.broadcasted_iota(jnp.int32, (owners, toks), 0)
    mask = jnp.zeros((owners, toks), F32)
    weight = jnp.zeros((owners, toks), F32)
    for k in range(choose):
        hit = ids_ref[k : k + 1, :] == expert
        mask = mask + jnp.where(hit, 1.0, 0.0)
        weight = weight + jnp.where(hit, w_ref[k : k + 1, :], 0.0)
    earlier = lax.broadcasted_iota(jnp.int32, (toks, toks), 0) < lax.broadcasted_iota(
        jnp.int32, (toks, toks), 1
    )
    rank = dot(mask.astype(B16), jnp.where(earlier, 1.0, 0.0).astype(B16))
    code = jnp.where(mask > 0.0, rank, -100.0)
    shape = (owners, 2 * cap, toks)
    code = jnp.broadcast_to(code[:, None, :], shape)
    weight = jnp.broadcast_to(weight[:, None, :], shape)
    row = lax.broadcasted_iota(jnp.int32, shape, 1).astype(F32)
    flat = (owners * 2 * cap, toks)
    left = jnp.where(code == row, 1.0, 0.0).reshape(flat)
    right = jnp.where(code == row - float(cap), 1.0, 0.0).reshape(flat)
    return left, right, weight.reshape(flat)


def dispatch_kernel(owners, cap, ids_ref, w_ref, tok_ref, cot_ref, out_ref):
    left, right, weight = routing(ids_ref, w_ref, owners, cap)
    scale = jnp.sum(right * weight, axis=1, keepdims=True)
    rows = dot(left.astype(B16), tok_ref[...]) + dot(right.astype(B16), cot_ref[...]) * scale
    out_ref[...] = rows.astype(B16)


def plan_kernel(owners, cap, ids_ref, w_ref, high_ref, low_ref, right_ref):
    left, right, weight = routing(ids_ref, w_ref, owners, cap)
    left = (left * weight).T
    high = left.astype(B16)
    high_ref[...] = high
    low_ref[...] = (left - high.astype(F32)).astype(B16)
    right_ref[...] = right.T.astype(B16)


def combine_kernel(high_ref, low_ref, right_ref, rows_ref, mixed_ref, grad_ref):
    rows = rows_ref[...]
    mixed_ref[...] = (dot(high_ref[...], rows) + dot(low_ref[...], rows)).astype(B16)
    grad_ref[...] = dot(right_ref[...], rows).astype(B16)


def pick(shape, axis, cap, shift):
    compact = lax.broadcasted_iota(jnp.int32, shape, axis).astype(F32)
    chunk = lax.broadcasted_iota(jnp.int32, shape, 1 - axis).astype(F32)
    block = jnp.floor((compact + 0.5) * (1.0 / cap))
    return jnp.where(chunk == compact + cap * block + shift, 1.0, 0.0).astype(B16)


def halves(side_ref, half):
    side = side_ref[0]
    here = pl.ds(pl.multiple_of(side * half, half), half)
    there = pl.ds(pl.multiple_of((1 - side) * half, half), half)
    return side, here, there


def forward_kernel(cap, side_ref, own_ref, oth_ref, wg_ref, wu_ref, gate_ref, up_ref, pack_ref):
    rows, half = own_ref.shape
    slots = rows // 2
    side, here, there = halves(side_ref, half)
    own, oth = own_ref[...], oth_ref[...]
    to_x = pick((slots, rows), 0, cap, 0)
    x_own, x_oth = dot(to_x, own).astype(B16), dot(to_x, oth).astype(B16)
    gate = dot(x_own, wg_ref[here, :]) + dot(x_oth, wg_ref[there, :])
    up = dot(x_own, wu_ref[here, :]) + dot(x_oth, wu_ref[there, :])
    hidden = (gate * (1.0 / (1.0 + jnp.exp(-gate))) * up).astype(B16)
    gate_ref[...] = gate
    up_ref[...] = up
    to_g = pick((slots, rows), 0, cap, cap)
    wide = half // 2
    nyh = half // (64 * NX)
    for s, rows_in in ((side, own), (1 - side, oth)):
        g = dot(to_g, rows_in).astype(B16)
        for xd in range(NX):
            for par in range(2):
                cols = jnp.concatenate(
                    [g[:, (y * NX + xd) * 64 : (y * NX + xd) * 64 + 64] for y in range(par, nyh, 2)],
                    axis=1,
                )
                n = cols.shape[1]
                pack_ref[xd, :, pl.ds(pl.multiple_of(par * (wide // 2) + s * n, 128), n)] = cols
    for xd in range(NX):
        pack_ref[xd, :, wide:] = hidden


def backward_kernel(
    cap, side_ref, own_ref, oth_ref, gate_ref, up_ref, wg_ref, wu_ref, wd_ref, keep_ref, give_ref
):
    rows, half = own_ref.shape
    slots = rows // 2
    _, here, there = halves(side_ref, half)
    to_g = pick((slots, rows), 0, cap, cap)
    g_own, g_oth = dot(to_g, own_ref[...]).astype(B16), dot(to_g, oth_ref[...]).astype(B16)
    gate, up = gate_ref[...], up_ref[...]
    sig = 1.0 / (1.0 + jnp.exp(-gate))
    act = gate * sig
    hidden = (act * up).astype(B16)
    hidden_grad = dot(g_own, wd_ref[:, here], COLS1) + dot(g_oth, wd_ref[:, there], COLS1)
    gate_term = (hidden_grad * up * sig * (1.0 + gate * (1.0 - sig))).astype(B16)
    up_term = (hidden_grad * act).astype(B16)
    from_x = pick((rows, slots), 1, cap, 0)
    from_g = pick((rows, slots), 1, cap, cap)
    for part, out in ((there, give_ref), (here, keep_ref)):
        out_rows = dot(hidden, wd_ref[:, part]).astype(B16)
        row_grad = dot(gate_term, wg_ref[part, :], COLS1) + dot(up_term, wu_ref[part, :], COLS1)
        out[...] = (dot(from_x, out_rows) + dot(from_g, row_grad.astype(B16))).astype(B16)


def down_kernel(part_ref, packs_ref, out_ref):
    n = out_ref.shape[0]
    cols = pl.ds(pl.multiple_of(part_ref[0] * n, n), n)
    total = None
    for k in range(NX):
        part = dot(packs_ref[k, :, cols], packs_ref[k, :, 2 * n :], ROWS0)
        total = part if total is None else total + part
    out_ref[...] = total.astype(B16)


def spread_kernel(where_ref, a_ref, b_ref, own_ref, s1_ref, s2_ref, s3_ref):
    q = where_ref[0]
    n = own_ref.shape[0]
    for k, out in enumerate((own_ref, s1_ref, s2_ref, s3_ref)):
        rows = pl.ds(pl.multiple_of(lax.rem(q + k, 4) * n, n), n)
        out[...] = (a_ref[rows, :].astype(F32) + b_ref[rows, :].astype(F32)).astype(B16)


def per_device(tokens, expert_ids, route_weight, gate_weight, up_weight, down_weight, cotangent):
    owners = lax.axis_size("expert")
    ny = lax.axis_size("y")
    tok_rows, choose = expert_ids.shape
    cap = 3 * tok_rows * choose // (2 * EXPERTS)
    half = tokens.shape[1]
    slots = owners * cap
    ff = gate_weight.shape[2]
    bf = lambda *shape: jax.ShapeDtypeStruct(shape, B16)
    side = lax.axis_index("tensor").astype(jnp.int32).reshape(1)
    y = lax.axis_index("y").astype(jnp.int32).reshape(1)
    ids_t, w_t = expert_ids.T, route_weight.T
    (send,) = fused(
        functools.partial(dispatch_kernel, owners, cap),
        [bf(2 * slots, half)],
        hbm(ids_t),
        hbm(w_t),
        hbm(tokens),
        hbm(cotangent),
        flops=4 * slots * tok_rows * half * 2,
    )
    high, low, right = fused(
        functools.partial(plan_kernel, owners, cap),
        [bf(tok_rows, 2 * slots)] * 3,
        hbm(ids_t),
        hbm(w_t),
        flops=tok_rows**3,
    )

    def trade(rows, axis, *shape):
        return lax.all_to_all(rows.reshape(shape), axis, split_axis=0, concat_axis=0, tiled=True)

    def swap(v):
        return lax.ppermute(v, "tensor", [(0, 1), (1, 0)])

    def to_y(v, move):
        return lax.ppermute(v, "y", [(b, move(b)) for b in range(ny)])

    chunks = (owners, 2 * cap, half)
    own = trade(send, "expert", *chunks).reshape(2 * slots, half)
    oth = swap(own)
    gate, up, pack = fused(
        functools.partial(forward_kernel, cap),
        [pltpu.HBM((slots, ff), F32)] * 2
        + [pltpu.HBM((NX, slots, half // 2 + ff), B16)],
        side,
        own,
        oth,
        gate_weight[0],
        hbm(up_weight[0]),
        scalars=1,
        flops=slots * half * 2 * ff * 4 + slots * 2 * slots * half * 8,
        mib=20,
    )
    packs = trade(pack, "x", *pack.shape)
    keep, give = fused(
        functools.partial(backward_kernel, cap),
        [bf(2 * slots, half)] * 2,
        side,
        own,
        oth,
        gate,
        up,
        hbm(gate_weight[0]),
        hbm(up_weight[0]),
        hbm(down_weight[0]),
        scalars=1,
        flops=slots * half * 2 * ff * 8 + slots * 2 * slots * half * 12,
        mib=24,
    )
    total = (keep.astype(F32) + swap(give).astype(F32)).astype(B16)
    back = trade(total, "expert", *chunks).reshape(2 * slots, half)
    mixed, token_grad = fused(
        combine_kernel,
        [bf(tok_rows, half)] * 2,
        high,
        low,
        right,
        back,
        flops=tok_rows * 2 * slots * half * 6,
    )
    down = functools.partial(
        fused, down_kernel, [bf(half // 4, ff)], scalars=1, flops=half // 4 * ff * slots * 2 * NX
    )
    (down_give,) = down(1 - y % 2, packs)
    down_got = to_y(down_give, lambda b: b ^ 1)
    (down_keep,) = down(y % 2, packs)
    mine, *sends = fused(
        spread_kernel, [bf(half // 16, ff)] * 4, y // 2, down_keep, down_got, scalars=1
    )
    total_down = mine.astype(F32)
    for k, s in enumerate(sends, 1):
        total_down = total_down + to_y(s, lambda b, k=k: (b + 2 * k) % ny).astype(F32)
    return mixed, token_grad, total_down.astype(B16).T[None]


def solution(mesh):
    dp, owners, tensor = (mesh.shape[a] for a in ("dp", "expert", "tensor"))
    mesh = jax.sharding.Mesh(
        mesh.devices.reshape(dp // NX, NX, owners, tensor), ("y", "x", "expert", "tensor")
    )
    blocks = ("y", "x", "expert")
    placed = (
        P(blocks, "tensor"),
        P(blocks, None),
        P(blocks, None),
        P("expert", None, "tensor"),
        P("expert", None, "tensor"),
        P("expert", "tensor", None),
        P(blocks, "tensor"),
    )

    return jax.shard_map(
        per_device,
        mesh=mesh,
        in_specs=placed,
        out_specs=(P(blocks, "tensor"), P(blocks, "tensor"), P("expert", "tensor", ("y", "x"))),
        check_vma=False,
    )
```

profile of v0, /device:TPU:48, one launch (start us, length us, event | category | flops | bytes accessed | tf_op | source)
XLA Modules:
  0.0 113.2 jit_solution(2517270138143104142)
XLA Ops:
  0.6 1.8 %shard_map.95 = bf16[288,1024]{1,0:T(8,128)(2,1)S(1)} custom-call(s32[8,128]{1,0:T(8,128)} %bitcast.25, f32[8,128]{1,0:T(8,128)} %bitcast.27, bf16[128,1024]{1,0:T(8,128)(2,1)} %tok_ref.1, bf16[128,1024]{1,0:T(8,128)(2,1)} %cot_ref.1), custom_call_target="tpu_custom_call" | custom-call | flops 150994944 | bytes 1122304 | tf_op jit(solution)/shard_map/pallas_call | solution.py:33
  2.4 41.8 %all_to_all.15 = bf16[12,24,1024]{2,1,0:T(8,128)(2,1)S(1)} all-to-all(bf16[12,24,1024]{2,1,0:T(8,128)(2,1)S(1)} %bitcast.21), channel_id=1, replica_groups=mesh['y'=8,'x'=4,'expert'=12,'tensor'=2] {'expert'}, dimensions={0} | all-to-all | bytes 1179648 | tf_op jit(solution)/shard_map/all_to_all | solution.py:203
  44.3 1.9 %collective-permute-start = (bf16[288,1024]{1,0:T(8,128)(2,1)S(1)}, bf16[288,1024]{1,0:T(8,128)(2,1)S(1)}, u32[]{:S(2)}, u32[]{:S(2)}) collective-permute-start(bf16[288,1024]{1,0:T(8,128)(2,1)S(1)} %bitcast.17), channel_id=1, source_target_pairs={{0,1},{1,0},{2,3},{3,2},{4,5},{5,4},{6,7},{7,6},{8,9},{9,8},{10,11... | collective-permute-start | bytes 1769480 | tf_op jit(solution)/shard_map/ppermute | solution.py:206
  46.2 2.0 %collective-permute-done.oth_ref = bf16[288,1024]{1,0:T(8,128)(2,1)S(1)} collective-permute-done((bf16[288,1024]{1,0:T(8,128)(2,1)S(1)}, bf16[288,1024]{1,0:T(8,128)(2,1)S(1)}, u32[]{:S(2)}, u32[]{:S(2)}) %collective-permute-start) | collective-permute-done | bytes 589856 | tf_op jit(solution)/shard_map/ppermute | solution.py:206
  48.2 3.9 %shard_map.96 = (f32[144,384]{1,0:T(8,128)}, f32[144,384]{1,0:T(8,128)}, bf16[4,144,896]{2,1,0:T(8,128)(2,1)}) custom-call(s32[1]{0:T(128)} %bitcast.2.side_ref, bf16[288,1024]{1,0:T(8,128)(2,1)S(1)} %bitcast.18, bf16[288,1024]{1,0:T(8,128)(2,1)S(1)} %collective-permute-done.oth_ref, bf16[2048,384]{1,0:T(8,128)(2,1)S(1)} %bitcast.16, bf16[2048,384]{1,0:T(8,128)(2,1)} %bitcast.22), custom_call_target="tpu_custom_call" | custom-call | flops 792723456 | bytes 5799940 | tf_op jit(solution)/shard_map/pallas_call | solution.py:33
  52.1 0.9 copy-done.1
  53.0 0.9 copy-done.2
  53.9 5.2 %shard_map.97 = (bf16[288,1024]{1,0:T(8,128)(2,1)S(1)}, bf16[288,1024]{1,0:T(8,128)(2,1)}) custom-call(s32[1]{0:T(128)} %bitcast.2.side_ref, bf16[288,1024]{1,0:T(8,128)(2,1)S(1)} %bitcast.19, bf16[288,1024]{1,0:T(8,128)(2,1)S(1)} %collective-permute-done.oth_ref, f32[144,384]{1,0:T(8,128)S(1)} %copy-done.1, f32[144,384]{1,0:T(8,128)S(1)} %copy-done.2, ...), custom_call_target="tpu_custom_call" | custom-call | flops 1415577600 | bytes 7520260 | tf_op jit(solution)/shard_map/pallas_call | solution.py:33
  59.2 2.0 %collective-permute-start.1 = (bf16[288,1024]{1,0:T(8,128)(2,1)}, bf16[288,1024]{1,0:T(8,128)(2,1)S(1)}, u32[]{:S(2)}, u32[]{:S(2)}) collective-permute-start(bf16[288,1024]{1,0:T(8,128)(2,1)} %get-tuple-element.23), channel_id=1, source_target_pairs={{0,1},{1,0},{2,3},{3,2},{4,5},{5,4},{6,7},{7,6},{8,9},{9,8},{10,11... | collective-permute-start | bytes 1769480 | tf_op jit(solution)/shard_map/ppermute | solution.py:206
  61.2 4.3 %all-to-all-start.2 = ((bf16[4,144,896]{2,1,0:T(8,128)(2,1)}), bf16[4,144,896]{2,1,0:T(8,128)(2,1)S(1)}, u32[]{:S(2)}, u32[]{:S(2)}) async-start(bf16[4,144,896]{2,1,0:T(8,128)(2,1)} %get-tuple-element.26), calls=%async_computation.2 | async-start | bytes 2064384 | tf_op jit(solution)/shard_map/all_to_all | solution.py:203
  65.5 1.1 add_convert_fusion
  66.6 14.4 %all-to-all-done.2.packs_ref = bf16[4,144,896]{2,1,0:T(8,128)(2,1)S(1)} async-done(((bf16[4,144,896]{2,1,0:T(8,128)(2,1)}), bf16[4,144,896]{2,1,0:T(8,128)(2,1)S(1)}, u32[]{:S(2)}, u32[]{:S(2)}) %all-to-all-start.2) | async-done | bytes 1032224 | tf_op jit(solution)/shard_map/all_to_all | solution.py:203
  81.0 3.6 %all-to-all-start.1 = ((bf16[12,24,1024]{2,1,0:T(8,128)(2,1)}), bf16[12,24,1024]{2,1,0:T(8,128)(2,1)S(1)}, u32[]{:S(2)}, u32[]{:S(2)}) async-start(bf16[12,24,1024]{2,1,0:T(8,128)(2,1)} %bitcast.8), calls=%async_computation.1 | async-start | bytes 1179648 | tf_op jit(solution)/shard_map/all_to_all | solution.py:203
  84.6 0.5 shard_map.100
  85.1 2.6 %collective-permute-start.2 = (bf16[256,384]{1,0:T(8,128)(2,1)S(1)}, bf16[256,384]{1,0:T(8,128)(2,1)S(1)}, u32[]{:S(2)}, u32[]{:S(2)}) collective-permute-start(bf16[256,384]{1,0:T(8,128)(2,1)S(1)} %shard_map.100), channel_id=1, source_target_pairs={{0,96},{96,0},{192,288},{288,192},{384,480},{480,384},{576,672},{6... | collective-permute-start | bytes 589832 | tf_op jit(solution)/shard_map/ppermute | solution.py:209
  87.7 0.5 shard_map.99.a_ref
  88.2 4.8 %collective-permute-done.2.b_ref = bf16[256,384]{1,0:T(8,128)(2,1)S(1)} collective-permute-done((bf16[256,384]{1,0:T(8,128)(2,1)S(1)}, bf16[256,384]{1,0:T(8,128)(2,1)S(1)}, u32[]{:S(2)}, u32[]{:S(2)}) %collective-permute-start.2) | collective-permute-done | bytes 196640 | tf_op jit(solution)/shard_map/ppermute | solution.py:209
  93.1 1.9 %collective-permute-start.3 = (bf16[64,384]{1,0:T(8,128)(2,1)S(1)}, bf16[64,384]{1,0:T(8,128)(2,1)S(1)}, u32[]{:S(2)}, u32[]{:S(2)}) collective-permute-start(bf16[64,384]{1,0:T(8,128)(2,1)S(1)} %get-tuple-element.28), channel_id=1, source_target_pairs={{0,192},{96,288},{192,384},{288,480},{384,576},{480,672},{576,0},{... | collective-permute-start | bytes 147464 | tf_op jit(solution)/shard_map/ppermute | solution.py:209
  95.0 7.6 %collective-permute-start.4 = (bf16[64,384]{1,0:T(8,128)(2,1)S(1)}, bf16[64,384]{1,0:T(8,128)(2,1)S(1)}, u32[]{:S(2)}, u32[]{:S(2)}) collective-permute-start(bf16[64,384]{1,0:T(8,128)(2,1)S(1)} %get-tuple-element.29), channel_id=1, source_target_pairs={{0,384},{96,480},{192,576},{288,672},{384,0},{480,96},{576,192},{6... | collective-permute-start | bytes 147464 | tf_op jit(solution)/shard_map/ppermute | solution.py:209
  102.7 1.9 %collective-permute-start.5 = (bf16[64,384]{1,0:T(8,128)(2,1)S(1)}, bf16[64,384]{1,0:T(8,128)(2,1)S(1)}, u32[]{:S(2)}, u32[]{:S(2)}) collective-permute-start(bf16[64,384]{1,0:T(8,128)(2,1)S(1)} %get-tuple-element.30), channel_id=1, source_target_pairs={{0,576},{96,672},{192,0},{288,96},{384,192},{480,288},{576,384},{6... | collective-permute-start | bytes 147464 | tf_op jit(solution)/shard_map/ppermute | solution.py:209
  104.6 1.0 shard_map.94
  105.6 5.7 %collective-permute-done.5 = bf16[64,384]{1,0:T(8,128)(2,1)S(1)} collective-permute-done((bf16[64,384]{1,0:T(8,128)(2,1)S(1)}, bf16[64,384]{1,0:T(8,128)(2,1)S(1)}, u32[]{:S(2)}, u32[]{:S(2)}) %collective-permute-start.5) | collective-permute-done | bytes 49184 | tf_op jit(solution)/shard_map/ppermute | solution.py:209
  111.3 0.6 fusion
  111.9 1.3 %shard_map.98 = (bf16[128,1024]{1,0:T(8,128)(2,1)}, bf16[128,1024]{1,0:T(8,128)(2,1)}) custom-call(bf16[128,288]{1,0:T(8,128)(2,1)S(1)} %get-tuple-element.17.high_ref, bf16[128,288]{1,0:T(8,128)(2,1)S(1)} %get-tuple-element.18.low_ref, bf16[128,288]{1,0:T(8,128)(2,1)S(1)} %get-tuple-element.19.right_ref, bf16[288,1024]{1,0:T(8,128)(2,1)S(1)} %bitcast.20), custom_call_target="tpu_custom_call" | custom-call | flops 226492416 | bytes 1335296 | tf_op jit(solution)/shard_map/pallas_call | solution.py:33
  (9 shorter events, 0.1 us)
Async XLA Ops:
  0.6 47.5 %copy-start = (bf16[1,2048,384]{2,1,0:T(8,128)(2,1)S(1)}, bf16[1,2048,384]{2,1,0:T(8,128)(2,1)}, u32[]{:S(2)}) copy-start(bf16[1,2048,384]{2,1,0:T(8,128)(2,1)} %param.10) | copy-start | bytes 4718596
  44.3 3.9 %collective-permute-start = (bf16[288,1024]{1,0:T(8,128)(2,1)S(1)}, bf16[288,1024]{1,0:T(8,128)(2,1)S(1)}, u32[]{:S(2)}, u32[]{:S(2)}) collective-permute-start(bf16[288,1024]{1,0:T(8,128)(2,1)S(1)} %bitcast.17), channel_id=1, source_target_pairs={{0,1},{1,0},{2,3},{3,2},{4,5},{5,4},{6,7},{7,6},{8,9},{9,8},{10,11... | collective-permute-start | bytes 1769480 | tf_op jit(solution)/shard_map/ppermute | solution.py:206
  52.1 0.9 copy-start.1
  53.0 0.9 copy-start.2
  59.2 6.4 %collective-permute-start.1 = (bf16[288,1024]{1,0:T(8,128)(2,1)}, bf16[288,1024]{1,0:T(8,128)(2,1)S(1)}, u32[]{:S(2)}, u32[]{:S(2)}) collective-permute-start(bf16[288,1024]{1,0:T(8,128)(2,1)} %get-tuple-element.23), channel_id=1, source_target_pairs={{0,1},{1,0},{2,3},{3,2},{4,5},{5,4},{6,7},{7,6},{8,9},{9,8},{10,11... | collective-permute-start | bytes 1769480 | tf_op jit(solution)/shard_map/ppermute | solution.py:206
  61.2 19.8 %all-to-all-start.2 = ((bf16[4,144,896]{2,1,0:T(8,128)(2,1)}), bf16[4,144,896]{2,1,0:T(8,128)(2,1)S(1)}, u32[]{:S(2)}, u32[]{:S(2)}) async-start(bf16[4,144,896]{2,1,0:T(8,128)(2,1)} %get-tuple-element.26), calls=%async_computation.2 | async-start | bytes 2064384 | tf_op jit(solution)/shard_map/all_to_all | solution.py:203
  81.0 30.9 %all-to-all-start.1 = ((bf16[12,24,1024]{2,1,0:T(8,128)(2,1)}), bf16[12,24,1024]{2,1,0:T(8,128)(2,1)S(1)}, u32[]{:S(2)}, u32[]{:S(2)}) async-start(bf16[12,24,1024]{2,1,0:T(8,128)(2,1)} %bitcast.8), calls=%async_computation.1 | async-start | bytes 1179648 | tf_op jit(solution)/shard_map/all_to_all | solution.py:203
  85.1 7.9 %collective-permute-start.2 = (bf16[256,384]{1,0:T(8,128)(2,1)S(1)}, bf16[256,384]{1,0:T(8,128)(2,1)S(1)}, u32[]{:S(2)}, u32[]{:S(2)}) collective-permute-start(bf16[256,384]{1,0:T(8,128)(2,1)S(1)} %shard_map.100), channel_id=1, source_target_pairs={{0,96},{96,0},{192,288},{288,192},{384,480},{480,384},{576,672},{6... | collective-permute-start | bytes 589832 | tf_op jit(solution)/shard_map/ppermute | solution.py:209
  93.1 12.5 %collective-permute-start.3 = (bf16[64,384]{1,0:T(8,128)(2,1)S(1)}, bf16[64,384]{1,0:T(8,128)(2,1)S(1)}, u32[]{:S(2)}, u32[]{:S(2)}) collective-permute-start(bf16[64,384]{1,0:T(8,128)(2,1)S(1)} %get-tuple-element.28), channel_id=1, source_target_pairs={{0,192},{96,288},{192,384},{288,480},{384,576},{480,672},{576,0},{... | collective-permute-start | bytes 147464 | tf_op jit(solution)/shard_map/ppermute | solution.py:209
  95.0 10.6 %collective-permute-start.4 = (bf16[64,384]{1,0:T(8,128)(2,1)S(1)}, bf16[64,384]{1,0:T(8,128)(2,1)S(1)}, u32[]{:S(2)}, u32[]{:S(2)}) collective-permute-start(bf16[64,384]{1,0:T(8,128)(2,1)S(1)} %get-tuple-element.29), channel_id=1, source_target_pairs={{0,384},{96,480},{192,576},{288,672},{384,0},{480,96},{576,192},{6... | collective-permute-start | bytes 147464 | tf_op jit(solution)/shard_map/ppermute | solution.py:209
  102.7 8.6 %collective-permute-start.5 = (bf16[64,384]{1,0:T(8,128)(2,1)S(1)}, bf16[64,384]{1,0:T(8,128)(2,1)S(1)}, u32[]{:S(2)}, u32[]{:S(2)}) collective-permute-start(bf16[64,384]{1,0:T(8,128)(2,1)S(1)} %get-tuple-element.30), channel_id=1, source_target_pairs={{0,576},{96,672},{192,0},{288,96},{384,192},{480,288},{576,384},{6... | collective-permute-start | bytes 147464 | tf_op jit(solution)/shard_map/ppermute | solution.py:209
where the time goes:
time: 114 us; the launch traced here: 113 us
  blocking collectives  41.8 us (37%)
  waiting for transfers between devices  26.8 us (24%)
  starting transfers between devices  25.9 us (23%)
  Pallas kernels  14.3 us (13%)
  local copies, waits for them, and re-layouts  1.88 us (2%)
  other arithmetic  1.71 us (2%)
    all_to_all x1, blocking collectives, trade(): lax.all_to_all(rows.reshape(shape), axis, split_axis=0, concat_axis=0, ti...  41.8 us
    all_to_all x2, waiting for transfers between devices, trade(): lax.all_to_all(rows.reshape(shape), axis, split_axis=0, concat_axis=0, ti...  14.4 us
    pallas_call x8, Pallas kernels, fused(): pl.pallas_call(kernel, out_shape=outs, in_specs=specs, out_specs=[pl.Bloc...  14.3 us
    ppermute x4, starting transfers between devices, to_y(): return lax.ppermute(v, 'y', [(b, move(b)) for b in range(ny)])  14 us
    ppermute x4, waiting for transfers between devices, to_y(): return lax.ppermute(v, 'y', [(b, move(b)) for b in range(ny)])  10.5 us
    all_to_all x2, starting transfers between devices, trade(): lax.all_to_all(rows.reshape(shape), axis, split_axis=0, concat_axis=0, ti...  7.92 us
    ppermute x2, starting transfers between devices, swap(): return lax.ppermute(v, 'tensor', [(0, 1), (1, 0)])  3.95 us
  transfers between devices with their start and end apart: 8, of which 4 were waited for; matrix products, arithmetic and copies ran while one was open for 2% of the time, Pallas kernels for 2%

commit v1 on v0

--- a/solution.py
+++ b/solution.py
@@ -103,7 +103,7 @@
 def forward_kernel(cap, side_ref, own_ref, oth_ref, wg_ref, wu_ref, gate_ref, up_ref, pack_ref):
     rows, half = own_ref.shape
     slots = rows // 2
-    side, here, there = halves(side_ref, half)
+    _, here, there = halves(side_ref, half)
     own, oth = own_ref[...], oth_ref[...]
     to_x = pick((slots, rows), 0, cap, 0)
     x_own, x_oth = dot(to_x, own).astype(B16), dot(to_x, oth).astype(B16)
@@ -112,20 +112,13 @@
     hidden = (gate * (1.0 / (1.0 + jnp.exp(-gate))) * up).astype(B16)
     gate_ref[...] = gate
     up_ref[...] = up
-    to_g = pick((slots, rows), 0, cap, cap)
-    wide = half // 2
-    nyh = half // (64 * NX)
-    for s, rows_in in ((side, own), (1 - side, oth)):
-        g = dot(to_g, rows_in).astype(B16)
-        for xd in range(NX):
-            for par in range(2):
-                cols = jnp.concatenate(
-                    [g[:, (y * NX + xd) * 64 : (y * NX + xd) * 64 + 64] for y in range(par, nyh, 2)],
-                    axis=1,
-                )
-                n = cols.shape[1]
-                pack_ref[xd, :, pl.ds(pl.multiple_of(par * (wide // 2) + s * n, 128), n)] = cols
+    g = dot(pick((slots, rows), 0, cap, cap), own).astype(B16)
+    wide = half // NX
+    nyh = wide // 64
     for xd in range(NX):
+        cols = [g[:, (y * NX + xd) * 64 : (y * NX + xd) * 64 + 64] for y in range(nyh)]
+        pack_ref[xd, :, 0 : wide // 2] = jnp.concatenate(cols[0::2], axis=1)
+        pack_ref[xd, :, wide // 2 : wide] = jnp.concatenate(cols[1::2], axis=1)
         pack_ref[xd, :, wide:] = hidden
 
 
@@ -152,22 +145,27 @@
         out[...] = (dot(from_x, out_rows) + dot(from_g, row_grad.astype(B16))).astype(B16)
 
 
-def down_kernel(part_ref, packs_ref, out_ref):
-    n = out_ref.shape[0]
-    cols = pl.ds(pl.multiple_of(part_ref[0] * n, n), n)
-    total = None
-    for k in range(NX):
-        part = dot(packs_ref[k, :, cols], packs_ref[k, :, 2 * n :], ROWS0)
-        total = part if total is None else total + part
-    out_ref[...] = total.astype(B16)
-
-
-def spread_kernel(where_ref, a_ref, b_ref, own_ref, s1_ref, s2_ref, s3_ref):
-    q = where_ref[0]
-    n = own_ref.shape[0]
-    for k, out in enumerate((own_ref, s1_ref, s2_ref, s3_ref)):
-        rows = pl.ds(pl.multiple_of(lax.rem(q + k, 4) * n, n), n)
-        out[...] = (a_ref[rows, :].astype(F32) + b_ref[rows, :].astype(F32)).astype(B16)
+def down_kernel(bit_ref, side_ref, packs_ref, oth_ref, out_ref):
+    n = out_ref.shape[0] // 2
+    wide = oth_ref.shape[2]
+    cols = pl.ds(pl.multiple_of(bit_ref[0] * n, n), n)
+    side = side_ref[0]
+    for ref, place in ((packs_ref, side), (oth_ref, 1 - side)):
+        total = None
+        for k in range(NX):
+            part = dot(ref[k, :, cols], packs_ref[k, :, wide:], ROWS0)
+            total = part if total is None else total + part
+        out_ref[pl.ds(pl.multiple_of(place * n, n), n), :] = total.astype(B16)
+
+
+def halve_kernel(blocks, bit_ref, a_ref, b_ref, keep_ref, give_ref):
+    n = keep_ref.shape[0] // blocks
+    bit = bit_ref[0]
+    for at, out in ((1 - bit, give_ref), (bit, keep_ref)):
+        for k in range(blocks):
+            rows = pl.ds(pl.multiple_of((2 * k + at) * n, n), n)
+            both = a_ref[rows, :].astype(F32) + b_ref[rows, :].astype(F32)
+            out[k * n : (k + 1) * n, :] = both.astype(B16)
 
 
 def per_device(tokens, expert_ids, route_weight, gate_weight, up_weight, down_weight, cotangent):
@@ -214,7 +212,7 @@
     gate, up, pack = fused(
         functools.partial(forward_kernel, cap),
         [pltpu.HBM((slots, ff), F32)] * 2
-        + [pltpu.HBM((NX, slots, half // 2 + ff), B16)],
+        + [pltpu.HBM((NX, slots, half // NX + ff), B16)],
         side,
         own,
         oth,
@@ -251,19 +249,27 @@
         back,
         flops=tok_rows * 2 * slots * half * 6,
     )
+    cols_oth = swap(packs[:, :, : half // NX])
     down = functools.partial(
-        fused, down_kernel, [bf(half // 4, ff)], scalars=1, flops=half // 4 * ff * slots * 2 * NX
-    )
-    (down_give,) = down(1 - y % 2, packs)
-    down_got = to_y(down_give, lambda b: b ^ 1)
-    (down_keep,) = down(y % 2, packs)
-    mine, *sends = fused(
-        spread_kernel, [bf(half // 16, ff)] * 4, y // 2, down_keep, down_got, scalars=1
-    )
-    total_down = mine.astype(F32)
-    for k, s in enumerate(sends, 1):
-        total_down = total_down + to_y(s, lambda b, k=k: (b + 2 * k) % ny).astype(F32)
-    return mixed, token_grad, total_down.astype(B16).T[None]
+        fused, down_kernel, [bf(half // 4, ff)], scalars=2, flops=half // 4 * ff * slots * 2 * NX
+    )
+    bits = [y % 2, y // 2 % 2, y // 4]
+    (give,) = down(1 - bits[0], side, packs, cols_oth)
+    got = to_y(give, lambda b: b ^ 1)
+    (keep,) = down(bits[0], side, packs, cols_oth)
+    for step, blocks in ((1, 2), (2, 1)):
+        rows = keep.shape[0] // 2
+        keep, give = fused(
+            functools.partial(halve_kernel, blocks),
+            [bf(rows, ff)] * 2,
+            bits[step],
+            keep,
+            got,
+            scalars=1,
+        )
+        got = to_y(give, lambda b, step=step: b ^ (1 << step))
+    down_grad = (keep.astype(F32) + got.astype(F32)).astype(B16)
+    return mixed, token_grad, down_grad.T[None]
 
 
 def solution(mesh):

time: 114 us -> 115 us (level)
  the two profiles are of different devices: /device:TPU:48 before, /device:TPU:56 now
where the time goes in v1:
time: 115 us
  blocking collectives  41.8 us (36%)
  waiting for transfers between devices  29 us (25%)
  starting transfers between devices  25.6 us (22%)
  Pallas kernels  14 us (12%)
  local copies, waits for them, and re-layouts  1.9 us (2%)
  other arithmetic  1.69 us (1%)
    all_to_all x1, blocking collectives, trade(): lax.all_to_all(rows.reshape(shape), axis, split_axis=0, concat_axis=0, ti...  41.8 us
    ppermute x3, waiting for transfers between devices, to_y(): return lax.ppermute(v, 'y', [(b, move(b)) for b in range(ny)])  14.2 us
    pallas_call x9, Pallas kernels, fused(): pl.pallas_call(kernel, out_shape=outs, in_specs=specs, out_specs=[pl.Bloc...  14 us
    ppermute x3, starting transfers between devices, to_y(): return lax.ppermute(v, 'y', [(b, move(b)) for b in range(ny)])  11.8 us
    all_to_all x2, waiting for transfers between devices, trade(): lax.all_to_all(rows.reshape(shape), axis, split_axis=0, concat_axis=0, ti...  11.2 us
    all_to_all x2, starting transfers between devices, trade(): lax.all_to_all(rows.reshape(shape), axis, split_axis=0, concat_axis=0, ti...  7.91 us
    ppermute x3, starting transfers between devices, swap(): return lax.ppermute(v, 'tensor', [(0, 1), (1, 0)])  5.88 us
    ppermute x3, waiting for transfers between devices, swap(): return lax.ppermute(v, 'tensor', [(0, 1), (1, 0)])  3.5 us
  transfers between devices with their start and end apart: 8, of which 6 were waited for; matrix products, arithmetic and copies ran while one was open for 1% of the time, Pallas kernels for 2%

profile of v1, /device:TPU:56, one launch (start us, length us, event | category | flops | bytes accessed | tf_op | source)
XLA Modules:
  0.0 114.8 jit_solution(6738678710375996112)
XLA Ops:
  0.6 1.8 %shard_map.95 = bf16[288,1024]{1,0:T(8,128)(2,1)S(1)} custom-call(s32[8,128]{1,0:T(8,128)} %bitcast.25, f32[8,128]{1,0:T(8,128)} %bitcast.27, bf16[128,1024]{1,0:T(8,128)(2,1)} %tok_ref.1, bf16[128,1024]{1,0:T(8,128)(2,1)} %cot_ref.1), custom_call_target="tpu_custom_call" | custom-call | flops 150994944 | bytes 1122304 | tf_op jit(solution)/shard_map/pallas_call | solution.py:33
  2.4 41.8 %all_to_all.15 = bf16[12,24,1024]{2,1,0:T(8,128)(2,1)S(1)} all-to-all(bf16[12,24,1024]{2,1,0:T(8,128)(2,1)S(1)} %bitcast.21), channel_id=1, replica_groups=mesh['y'=8,'x'=4,'expert'=12,'tensor'=2] {'expert'}, dimensions={0} | all-to-all | bytes 1179648 | tf_op jit(solution)/shard_map/all_to_all | solution.py:201
  44.3 1.9 %collective-permute-start = (bf16[288,1024]{1,0:T(8,128)(2,1)S(1)}, bf16[288,1024]{1,0:T(8,128)(2,1)S(1)}, u32[]{:S(2)}, u32[]{:S(2)}) collective-permute-start(bf16[288,1024]{1,0:T(8,128)(2,1)S(1)} %bitcast.17), channel_id=1, source_target_pairs={{0,1},{1,0},{2,3},{3,2},{4,5},{5,4},{6,7},{7,6},{8,9},{9,8},{10,11... | collective-permute-start | bytes 1769480 | tf_op jit(solution)/shard_map/ppermute | solution.py:204
  46.2 2.0 %collective-permute-done.oth_ref = bf16[288,1024]{1,0:T(8,128)(2,1)S(1)} collective-permute-done((bf16[288,1024]{1,0:T(8,128)(2,1)S(1)}, bf16[288,1024]{1,0:T(8,128)(2,1)S(1)}, u32[]{:S(2)}, u32[]{:S(2)}) %collective-permute-start) | collective-permute-done | bytes 589856 | tf_op jit(solution)/shard_map/ppermute | solution.py:204
  48.2 3.6 %shard_map.96 = (f32[144,384]{1,0:T(8,128)}, f32[144,384]{1,0:T(8,128)}, bf16[4,144,640]{2,1,0:T(8,128)(2,1)}) custom-call(s32[1]{0:T(128)} %bitcast.2.side_ref, bf16[288,1024]{1,0:T(8,128)(2,1)S(1)} %bitcast.18, bf16[288,1024]{1,0:T(8,128)(2,1)S(1)} %collective-permute-done.oth_ref, bf16[2048,384]{1,0:T(8,128)(2,1)S(1)} %bitcast.16, bf16[2048,384]{1,0:T(8,128)(2,1)} %bitcast.22), custom_call_target="tpu_custom_call" | custom-call | flops 792723456 | bytes 5505028 | tf_op jit(solution)/shard_map/pallas_call | solution.py:33
  51.8 0.9 copy-done.1
  52.7 0.9 copy-done.2
  53.7 5.2 %shard_map.97 = (bf16[288,1024]{1,0:T(8,128)(2,1)S(1)}, bf16[288,1024]{1,0:T(8,128)(2,1)S(1)}) custom-call(s32[1]{0:T(128)} %bitcast.2.side_ref, bf16[288,1024]{1,0:T(8,128)(2,1)S(1)} %bitcast.19, bf16[288,1024]{1,0:T(8,128)(2,1)S(1)} %collective-permute-done.oth_ref, f32[144,384]{1,0:T(8,128)S(1)} %copy-done.1, f32[144,384]{1,0:T(8,128)S(1)} %copy-done.2, ...), custom_call_target="tpu_custom_call" | custom-call | flops 1415577600 | bytes 7520260 | tf_op jit(solution)/shard_map/pallas_call | solution.py:33
  58.9 2.0 %collective-permute-start.1 = (bf16[288,1024]{1,0:T(8,128)(2,1)S(1)}, bf16[288,1024]{1,0:T(8,128)(2,1)S(1)}, u32[]{:S(2)}, u32[]{:S(2)}) collective-permute-start(bf16[288,1024]{1,0:T(8,128)(2,1)S(1)} %get-tuple-element.23), channel_id=1, source_target_pairs={{0,1},{1,0},{2,3},{3,2},{4,5},{5,4},{6,7},{7,6},{8,9},{9,8},{10,11... | collective-permute-start | bytes 1769480 | tf_op jit(solution)/shard_map/ppermute | solution.py:204
  61.0 4.3 %all-to-all-start.2 = ((bf16[4,144,640]{2,1,0:T(8,128)(2,1)}), bf16[4,144,640]{2,1,0:T(8,128)(2,1)S(1)}, u32[]{:S(2)}, u32[]{:S(2)}) async-start(bf16[4,144,640]{2,1,0:T(8,128)(2,1)} %get-tuple-element.26), calls=%async_computation.2 | async-start | bytes 1474560 | tf_op jit(solution)/shard_map/all_to_all | solution.py:201
  65.3 1.1 add_convert_fusion
  66.3 11.2 %all-to-all-done.2.packs_ref = bf16[4,144,640]{2,1,0:T(8,128)(2,1)S(1)} async-done(((bf16[4,144,640]{2,1,0:T(8,128)(2,1)}), bf16[4,144,640]{2,1,0:T(8,128)(2,1)S(1)}, u32[]{:S(2)}, u32[]{:S(2)}) %all-to-all-start.2) | async-done | bytes 737312 | tf_op jit(solution)/shard_map/all_to_all | solution.py:201
  77.6 3.6 %all-to-all-start.1 = ((bf16[12,24,1024]{2,1,0:T(8,128)(2,1)}), bf16[12,24,1024]{2,1,0:T(8,128)(2,1)S(1)}, u32[]{:S(2)}, u32[]{:S(2)}) async-start(bf16[12,24,1024]{2,1,0:T(8,128)(2,1)} %bitcast.8), calls=%async_computation.1 | async-start | bytes 1179648 | tf_op jit(solution)/shard_map/all_to_all | solution.py:201
  81.2 1.9 %collective-permute-start.2 = (bf16[4,144,256]{2,1,0:T(8,128)(2,1)S(1)}, bf16[4,144,256]{2,1,0:T(8,128)(2,1)S(1)}, u32[]{:S(2)}, u32[]{:S(2)}) collective-permute-start(bf16[4,144,256]{2,1,0:T(8,128)(2,1)S(1)} %slice.4), channel_id=1, source_target_pairs={{0,1},{1,0},{2,3},{3,2},{4,5},{5,4},{6,7},{7,6},{8,9},{9,8},{10,11... | collective-permute-start | bytes 884744 | tf_op jit(solution)/shard_map/ppermute | solution.py:204
  83.2 1.5 %collective-permute-done.2.oth_ref = bf16[4,144,256]{2,1,0:T(8,128)(2,1)S(1)} collective-permute-done((bf16[4,144,256]{2,1,0:T(8,128)(2,1)S(1)}, bf16[4,144,256]{2,1,0:T(8,128)(2,1)S(1)}, u32[]{:S(2)}, u32[]{:S(2)}) %collective-permute-start.2) | collective-permute-done | bytes 294944 | tf_op jit(solution)/shard_map/ppermute | solution.py:204
  85.2 3.3 %collective-permute-start.3 = (bf16[256,384]{1,0:T(8,128)(2,1)S(1)}, bf16[256,384]{1,0:T(8,128)(2,1)S(1)}, u32[]{:S(2)}, u32[]{:S(2)}) collective-permute-start(bf16[256,384]{1,0:T(8,128)(2,1)S(1)} %shard_map.100), channel_id=1, source_target_pairs={{0,96},{96,0},{192,288},{288,192},{384,480},{480,384},{576,672},{6... | collective-permute-start | bytes 589832 | tf_op jit(solution)/shard_map/ppermute | solution.py:207
  89.0 5.1 %collective-permute-done.3.b_ref = bf16[256,384]{1,0:T(8,128)(2,1)S(1)} collective-permute-done((bf16[256,384]{1,0:T(8,128)(2,1)S(1)}, bf16[256,384]{1,0:T(8,128)(2,1)S(1)}, u32[]{:S(2)}, u32[]{:S(2)}) %collective-permute-start.3) | collective-permute-done | bytes 196640 | tf_op jit(solution)/shard_map/ppermute | solution.py:207
  94.1 4.0 %collective-permute-start.4 = (bf16[128,384]{1,0:T(8,128)(2,1)S(1)}, bf16[128,384]{1,0:T(8,128)(2,1)S(1)}, u32[]{:S(2)}, u32[]{:S(2)}) collective-permute-start(bf16[128,384]{1,0:T(8,128)(2,1)S(1)} %get-tuple-element.28), channel_id=1, source_target_pairs={{0,192},{96,288},{192,0},{288,96},{384,576},{480,672},{576,384},{6... | collective-permute-start | bytes 294920 | tf_op jit(solution)/shard_map/ppermute | solution.py:207
  98.1 4.9 %collective-permute-done.4.b_ref = bf16[128,384]{1,0:T(8,128)(2,1)S(1)} collective-permute-done((bf16[128,384]{1,0:T(8,128)(2,1)S(1)}, bf16[128,384]{1,0:T(8,128)(2,1)S(1)}, u32[]{:S(2)}, u32[]{:S(2)}) %collective-permute-start.4) | collective-permute-done | bytes 98336 | tf_op jit(solution)/shard_map/ppermute | solution.py:207
  103.0 4.5 %collective-permute-start.5 = (bf16[64,384]{1,0:T(8,128)(2,1)S(1)}, bf16[64,384]{1,0:T(8,128)(2,1)S(1)}, u32[]{:S(2)}, u32[]{:S(2)}) collective-permute-start(bf16[64,384]{1,0:T(8,128)(2,1)S(1)} %get-tuple-element.30), channel_id=1, source_target_pairs={{0,384},{96,480},{192,576},{288,672},{384,0},{480,96},{576,192},{6... | collective-permute-start | bytes 147464 | tf_op jit(solution)/shard_map/ppermute | solution.py:207
  107.6 1.0 shard_map.94
  108.6 4.3 %collective-permute-done.5 = bf16[64,384]{1,0:T(8,128)(2,1)S(1)} collective-permute-done((bf16[64,384]{1,0:T(8,128)(2,1)S(1)}, bf16[64,384]{1,0:T(8,128)(2,1)S(1)}, u32[]{:S(2)}, u32[]{:S(2)}) %collective-permute-start.5) | collective-permute-done | bytes 49184 | tf_op jit(solution)/shard_map/ppermute | solution.py:207
  112.9 0.6 fusion
  113.5 1.3 %shard_map.98 = (bf16[128,1024]{1,0:T(8,128)(2,1)}, bf16[128,1024]{1,0:T(8,128)(2,1)}) custom-call(bf16[128,288]{1,0:T(8,128)(2,1)S(1)} %get-tuple-element.17.high_ref, bf16[128,288]{1,0:T(8,128)(2,1)S(1)} %get-tuple-element.18.low_ref, bf16[128,288]{1,0:T(8,128)(2,1)S(1)} %get-tuple-element.19.right_ref, bf16[288,1024]{1,0:T(8,128)(2,1)S(1)} %bitcast.20), custom_call_target="tpu_custom_call" | custom-call | flops 226492416 | bytes 1335296 | tf_op jit(solution)/shard_map/pallas_call | solution.py:33
  (11 shorter events, 1.1 us)
Async XLA Ops:
  0.6 47.5 %copy-start = (bf16[1,2048,384]{2,1,0:T(8,128)(2,1)S(1)}, bf16[1,2048,384]{2,1,0:T(8,128)(2,1)}, u32[]{:S(2)}) copy-start(bf16[1,2048,384]{2,1,0:T(8,128)(2,1)} %param.10) | copy-start | bytes 4718596
  44.3 3.9 %collective-permute-start = (bf16[288,1024]{1,0:T(8,128)(2,1)S(1)}, bf16[288,1024]{1,0:T(8,128)(2,1)S(1)}, u32[]{:S(2)}, u32[]{:S(2)}) collective-permute-start(bf16[288,1024]{1,0:T(8,128)(2,1)S(1)} %bitcast.17), channel_id=1, source_target_pairs={{0,1},{1,0},{2,3},{3,2},{4,5},{5,4},{6,7},{7,6},{8,9},{9,8},{10,11... | collective-permute-start | bytes 1769480 | tf_op jit(solution)/shard_map/ppermute | solution.py:204
  51.8 0.9 copy-start.1
  52.7 0.9 copy-start.2
  58.9 6.4 %collective-permute-start.1 = (bf16[288,1024]{1,0:T(8,128)(2,1)S(1)}, bf16[288,1024]{1,0:T(8,128)(2,1)S(1)}, u32[]{:S(2)}, u32[]{:S(2)}) collective-permute-start(bf16[288,1024]{1,0:T(8,128)(2,1)S(1)} %get-tuple-element.23), channel_id=1, source_target_pairs={{0,1},{1,0},{2,3},{3,2},{4,5},{5,4},{6,7},{7,6},{8,9},{9,8},{10,11... | collective-permute-start | bytes 1769480 | tf_op jit(solution)/shard_map/ppermute | solution.py:204
  61.0 16.6 %all-to-all-start.2 = ((bf16[4,144,640]{2,1,0:T(8,128)(2,1)}), bf16[4,144,640]{2,1,0:T(8,128)(2,1)S(1)}, u32[]{:S(2)}, u32[]{:S(2)}) async-start(bf16[4,144,640]{2,1,0:T(8,128)(2,1)} %get-tuple-element.26), calls=%async_computation.2 | async-start | bytes 1474560 | tf_op jit(solution)/shard_map/all_to_all | solution.py:201
  77.6 36.0 %all-to-all-start.1 = ((bf16[12,24,1024]{2,1,0:T(8,128)(2,1)}), bf16[12,24,1024]{2,1,0:T(8,128)(2,1)S(1)}, u32[]{:S(2)}, u32[]{:S(2)}) async-start(bf16[12,24,1024]{2,1,0:T(8,128)(2,1)} %bitcast.8), calls=%async_computation.1 | async-start | bytes 1179648 | tf_op jit(solution)/shard_map/all_to_all | solution.py:201
  81.2 3.5 %collective-permute-start.2 = (bf16[4,144,256]{2,1,0:T(8,128)(2,1)S(1)}, bf16[4,144,256]{2,1,0:T(8,128)(2,1)S(1)}, u32[]{:S(2)}, u32[]{:S(2)}) collective-permute-start(bf16[4,144,256]{2,1,0:T(8,128)(2,1)S(1)} %slice.4), channel_id=1, source_target_pairs={{0,1},{1,0},{2,3},{3,2},{4,5},{5,4},{6,7},{7,6},{8,9},{9,8},{10,11... | collective-permute-start | bytes 884744 | tf_op jit(solution)/shard_map/ppermute | solution.py:204
  85.2 8.9 %collective-permute-start.3 = (bf16[256,384]{1,0:T(8,128)(2,1)S(1)}, bf16[256,384]{1,0:T(8,128)(2,1)S(1)}, u32[]{:S(2)}, u32[]{:S(2)}) collective-permute-start(bf16[256,384]{1,0:T(8,128)(2,1)S(1)} %shard_map.100), channel_id=1, source_target_pairs={{0,96},{96,0},{192,288},{288,192},{384,480},{480,384},{576,672},{6... | collective-permute-start | bytes 589832 | tf_op jit(solution)/shard_map/ppermute | solution.py:207
  94.1 8.9 %collective-permute-start.4 = (bf16[128,384]{1,0:T(8,128)(2,1)S(1)}, bf16[128,384]{1,0:T(8,128)(2,1)S(1)}, u32[]{:S(2)}, u32[]{:S(2)}) collective-permute-start(bf16[128,384]{1,0:T(8,128)(2,1)S(1)} %get-tuple-element.28), channel_id=1, source_target_pairs={{0,192},{96,288},{192,0},{288,96},{384,576},{480,672},{576,384},{6... | collective-permute-start | bytes 294920 | tf_op jit(solution)/shard_map/ppermute | solution.py:207
  103.0 9.9 %collective-permute-start.5 = (bf16[64,384]{1,0:T(8,128)(2,1)S(1)}, bf16[64,384]{1,0:T(8,128)(2,1)S(1)}, u32[]{:S(2)}, u32[]{:S(2)}) collective-permute-start(bf16[64,384]{1,0:T(8,128)(2,1)S(1)} %get-tuple-element.30), channel_id=1, source_target_pairs={{0,384},{96,480},{192,576},{288,672},{384,0},{480,96},{576,192},{6... | collective-permute-start | bytes 147464 | tf_op jit(solution)/shard_map/ppermute | solution.py:207

commit v2 on v1

--- a/solution.py
+++ b/solution.py
@@ -145,32 +145,45 @@
         out[...] = (dot(from_x, out_rows) + dot(from_g, row_grad.astype(B16))).astype(B16)
 
 
-def down_kernel(bit_ref, side_ref, packs_ref, oth_ref, out_ref):
-    n = out_ref.shape[0] // 2
-    wide = oth_ref.shape[2]
-    cols = pl.ds(pl.multiple_of(bit_ref[0] * n, n), n)
-    side = side_ref[0]
-    for ref, place in ((packs_ref, side), (oth_ref, 1 - side)):
-        total = None
-        for k in range(NX):
-            part = dot(ref[k, :, cols], packs_ref[k, :, wide:], ROWS0)
-            total = part if total is None else total + part
-        out_ref[pl.ds(pl.multiple_of(place * n, n), n), :] = total.astype(B16)
-
-
-def halve_kernel(blocks, bit_ref, a_ref, b_ref, keep_ref, give_ref):
+def down_kernel(bit_ref, packs_ref, cols_ref, keep_ref, give_ref):
+    n = keep_ref.shape[0] // 2
+    slots = packs_ref.shape[1]
+    wide = cols_ref.shape[2]
+    bit = bit_ref[0]
+    for at, out in ((1 - bit, give_ref), (bit, keep_ref)):
+        cols = pl.ds(pl.multiple_of(at * n, n), n)
+        for h in range(2):
+            total = None
+            for k in range(NX):
+                rows = cols_ref[k, h * slots : (h + 1) * slots, cols]
+                part = dot(rows, packs_ref[k, :, wide:], ROWS0)
+                total = part if total is None else total + part
+            out[h * n : (h + 1) * n, :] = total.astype(B16)
+
+
+def partner_row(bit_ref, pair_ref, at, n):
+    start = (1 - bit_ref[0]) * (pair_ref.shape[0] // 2) + at
+    return pair_ref[pl.ds(pl.multiple_of(start, n), n), :].astype(F32)
+
+
+def halve_kernel(blocks, last_ref, bit_ref, mine_ref, pair_ref, keep_ref, give_ref):
     n = keep_ref.shape[0] // blocks
     bit = bit_ref[0]
-    for at, out in ((1 - bit, give_ref), (bit, keep_ref)):
+    for side, out in ((1 - bit, give_ref), (bit, keep_ref)):
         for k in range(blocks):
-            rows = pl.ds(pl.multiple_of((2 * k + at) * n, n), n)
-            both = a_ref[rows, :].astype(F32) + b_ref[rows, :].astype(F32)
+            at = (2 * k + side) * n
+            mine = mine_ref[pl.ds(pl.multiple_of(at, n), n), :].astype(F32)
+            both = mine + partner_row(last_ref, pair_ref, at, n)
             out[k * n : (k + 1) * n, :] = both.astype(B16)
+
+
+def finish_kernel(last_ref, mine_ref, pair_ref, out_ref):
+    n = out_ref.shape[0]
+    out_ref[...] = (mine_ref[...].astype(F32) + partner_row(last_ref, pair_ref, 0, n)).astype(B16)
 
 
 def per_device(tokens, expert_ids, route_weight, gate_weight, up_weight, down_weight, cotangent):
     owners = lax.axis_size("expert")
-    ny = lax.axis_size("y")
     tok_rows, choose = expert_ids.shape
     cap = 3 * tok_rows * choose // (2 * EXPERTS)
     half = tokens.shape[1]
@@ -178,7 +191,7 @@
     ff = gate_weight.shape[2]
     bf = lambda *shape: jax.ShapeDtypeStruct(shape, B16)
     side = lax.axis_index("tensor").astype(jnp.int32).reshape(1)
-    y = lax.axis_index("y").astype(jnp.int32).reshape(1)
+    bits = [lax.axis_index(a).astype(jnp.int32).reshape(1) for a in ("y1", "y2", "y4")]
     ids_t, w_t = expert_ids.T, route_weight.T
     (send,) = fused(
         functools.partial(dispatch_kernel, owners, cap),
@@ -203,8 +216,8 @@
     def swap(v):
         return lax.ppermute(v, "tensor", [(0, 1), (1, 0)])
 
-    def to_y(v, move):
-        return lax.ppermute(v, "y", [(b, move(b)) for b in range(ny)])
+    def pair(v, axis, dim=0):
+        return lax.all_gather(v, axis, axis=dim, tiled=True)
 
     chunks = (owners, 2 * cap, half)
     own = trade(send, "expert", *chunks).reshape(2 * slots, half)
@@ -249,35 +262,40 @@
         back,
         flops=tok_rows * 2 * slots * half * 6,
     )
-    cols_oth = swap(packs[:, :, : half // NX])
-    down = functools.partial(
-        fused, down_kernel, [bf(half // 4, ff)], scalars=2, flops=half // 4 * ff * slots * 2 * NX
-    )
-    bits = [y % 2, y // 2 % 2, y // 4]
-    (give,) = down(1 - bits[0], side, packs, cols_oth)
-    got = to_y(give, lambda b: b ^ 1)
-    (keep,) = down(bits[0], side, packs, cols_oth)
+    keep, give = fused(
+        down_kernel,
+        [bf(half // 4, ff)] * 2,
+        bits[0],
+        packs,
+        pair(packs[:, :, : half // NX], "tensor", 1),
+        scalars=1,
+        flops=half // 2 * ff * slots * 2 * NX,
+    )
     for step, blocks in ((1, 2), (2, 1)):
         rows = keep.shape[0] // 2
         keep, give = fused(
             functools.partial(halve_kernel, blocks),
             [bf(rows, ff)] * 2,
+            bits[step - 1],
             bits[step],
             keep,
-            got,
-            scalars=1,
+            pair(give, ("y1", "y2")[step - 1]),
+            scalars=2,
         )
-        got = to_y(give, lambda b, step=step: b ^ (1 << step))
-    down_grad = (keep.astype(F32) + got.astype(F32)).astype(B16)
+    (down_grad,) = fused(
+        finish_kernel, [bf(*keep.shape)], bits[2], keep, pair(give, "y4"), scalars=1
+    )
     return mixed, token_grad, down_grad.T[None]
 
 
 def solution(mesh):
     dp, owners, tensor = (mesh.shape[a] for a in ("dp", "expert", "tensor"))
     mesh = jax.sharding.Mesh(
-        mesh.devices.reshape(dp // NX, NX, owners, tensor), ("y", "x", "expert", "tensor")
-    )
-    blocks = ("y", "x", "expert")
+        mesh.devices.reshape(2, 2, dp // (4 * NX), NX, owners, tensor),
+        ("y4", "y2", "y1", "x", "expert", "tensor"),
+    )
+    ways = ("y4", "y2", "y1", "x")
+    blocks = (*ways, "expert")
     placed = (
         P(blocks, "tensor"),
         P(blocks, None),
@@ -292,6 +310,6 @@
         per_device,
         mesh=mesh,
         in_specs=placed,
-        out_specs=(P(blocks, "tensor"), P(blocks, "tensor"), P("expert", "tensor", ("y", "x"))),
+        out_specs=(P(blocks, "tensor"), P(blocks, "tensor"), P("expert", "tensor", ways)),
         check_vma=False,
     )

time: 115 us -> 112 us (0.974)
  the two profiles are of different devices: /device:TPU:56 before, /device:TPU:32 now
where the time goes in v2:
time: 112 us; the launch traced here: 111 us
  blocking collectives  68 us (61%)
  Pallas kernels  14.4 us (13%)
  waiting for transfers between devices  13.2 us (12%)
  starting transfers between devices  11.9 us (11%)
  local copies, waits for them, and re-layouts  1.9 us (2%)
    all_to_all x1, blocking collectives, trade(): lax.all_to_all(rows.reshape(shape), axis, split_axis=0, concat_axis=0, ti...  41.8 us
    all_gather x4, blocking collectives, pair(): return lax.all_gather(v, axis, axis=dim, tiled=True)  26.2 us
    pallas_call x9, Pallas kernels, fused(): pl.pallas_call(kernel, out_shape=outs, in_specs=specs, out_specs=[pl.Bloc...  14.4 us
    all_to_all x2, waiting for transfers between devices, trade(): lax.all_to_all(rows.reshape(shape), axis, split_axis=0, concat_axis=0, ti...  11.2 us
    all_to_all x2, starting transfers between devices, trade(): lax.all_to_all(rows.reshape(shape), axis, split_axis=0, concat_axis=0, ti...  7.92 us
    ppermute x2, starting transfers between devices, swap(): return lax.ppermute(v, 'tensor', [(0, 1), (1, 0)])  3.95 us
  transfers between devices with their start and end apart: 4, of which 2 were waited for; matrix products, arithmetic and copies ran while one was open for 1% of the time, Pallas kernels for 2%

profile of v2, /device:TPU:32, one launch (start us, length us, event | category | flops | bytes accessed | tf_op | source)
XLA Modules:
  0.0 111.1 jit_solution(8018420589394469665)
XLA Ops:
  0.6 0.0 copy-start
  0.6 1.8 %shard_map.95 = bf16[288,1024]{1,0:T(8,128)(2,1)S(1)} custom-call(s32[8,128]{1,0:T(8,128)} %bitcast.27, f32[8,128]{1,0:T(8,128)} %bitcast.29, bf16[128,1024]{1,0:T(8,128)(2,1)} %tok_ref.1, bf16[128,1024]{1,0:T(8,128)(2,1)} %cot_ref.1), custom_call_target="tpu_custom_call" | custom-call | flops 150994944 | bytes 1122304 | tf_op jit(solution)/shard_map/pallas_call | solution.py:33
  2.4 41.8 %all_to_all.15 = bf16[12,24,1024]{2,1,0:T(8,128)(2,1)S(1)} all-to-all(bf16[12,24,1024]{2,1,0:T(8,128)(2,1)S(1)} %bitcast.22), channel_id=1, replica_groups=mesh['y4'=2,'y2'=2,'y1'=2,'x'=4,'expert'=12,'tensor'=2] {'expert'}, dimensions={0} | all-to-all | bytes 1179648 | tf_op jit(solution)/shard_map/all_to_all | solution.py:214
  44.3 1.9 %collective-permute-start = (bf16[288,1024]{1,0:T(8,128)(2,1)S(1)}, bf16[288,1024]{1,0:T(8,128)(2,1)S(1)}, u32[]{:S(2)}, u32[]{:S(2)}) collective-permute-start(bf16[288,1024]{1,0:T(8,128)(2,1)S(1)} %bitcast.18), channel_id=1, source_target_pairs={{0,1},{1,0},{2,3},{3,2},{4,5},{5,4},{6,7},{7,6},{8,9},{9,8},{10,11... | collective-permute-start | bytes 1769480 | tf_op jit(solution)/shard_map/ppermute | solution.py:217
  46.2 2.0 %collective-permute-done.oth_ref = bf16[288,1024]{1,0:T(8,128)(2,1)S(1)} collective-permute-done((bf16[288,1024]{1,0:T(8,128)(2,1)S(1)}, bf16[288,1024]{1,0:T(8,128)(2,1)S(1)}, u32[]{:S(2)}, u32[]{:S(2)}) %collective-permute-start) | collective-permute-done | bytes 589856 | tf_op jit(solution)/shard_map/ppermute | solution.py:217
  48.2 3.6 %shard_map.96 = (f32[144,384]{1,0:T(8,128)}, f32[144,384]{1,0:T(8,128)}, bf16[4,144,640]{2,1,0:T(8,128)(2,1)}) custom-call(s32[1]{0:T(128)} %bitcast.2.side_ref, bf16[288,1024]{1,0:T(8,128)(2,1)S(1)} %bitcast.19, bf16[288,1024]{1,0:T(8,128)(2,1)S(1)} %collective-permute-done.oth_ref, bf16[2048,384]{1,0:T(8,128)(2,1)S(1)} %bitcast.17, bf16[2048,384]{1,0:T(8,128)(2,1)} %bitcast.23), custom_call_target="tpu_custom_call" | custom-call | flops 792723456 | bytes 5505028 | tf_op jit(solution)/shard_map/pallas_call | solution.py:33
  51.8 0.9 copy-done.1
  52.7 0.9 copy-done.2
  53.7 5.2 %shard_map.97 = (bf16[288,1024]{1,0:T(8,128)(2,1)S(1)}, bf16[288,1024]{1,0:T(8,128)(2,1)S(1)}) custom-call(s32[1]{0:T(128)} %bitcast.2.side_ref, bf16[288,1024]{1,0:T(8,128)(2,1)S(1)} %bitcast.20, bf16[288,1024]{1,0:T(8,128)(2,1)S(1)} %collective-permute-done.oth_ref, f32[144,384]{1,0:T(8,128)S(1)} %copy-done.1, f32[144,384]{1,0:T(8,128)S(1)} %copy-done.2, ...), custom_call_target="tpu_custom_call" | custom-call | flops 1415577600 | bytes 7520260 | tf_op jit(solution)/shard_map/pallas_call | solution.py:33
  58.9 2.0 %collective-permute-start.1 = (bf16[288,1024]{1,0:T(8,128)(2,1)S(1)}, bf16[288,1024]{1,0:T(8,128)(2,1)S(1)}, u32[]{:S(2)}, u32[]{:S(2)}) collective-permute-start(bf16[288,1024]{1,0:T(8,128)(2,1)S(1)} %get-tuple-element.25), channel_id=1, source_target_pairs={{0,1},{1,0},{2,3},{3,2},{4,5},{5,4},{6,7},{7,6},{8,9},{9,8},{10,11... | collective-permute-start | bytes 1769480 | tf_op jit(solution)/shard_map/ppermute | solution.py:217
  60.9 4.3 %all-to-all-start.2 = ((bf16[4,144,640]{2,1,0:T(8,128)(2,1)}), bf16[4,144,640]{2,1,0:T(8,128)(2,1)S(1)}, u32[]{:S(2)}, u32[]{:S(2)}) async-start(bf16[4,144,640]{2,1,0:T(8,128)(2,1)} %get-tuple-element.28), calls=%async_computation.2 | async-start | bytes 1474560 | tf_op jit(solution)/shard_map/all_to_all | solution.py:214
  65.2 0.0 collective-permute-done.1
  65.3 1.1 add_convert_fusion
  66.3 11.2 %all-to-all-done.2.packs_ref = bf16[4,144,640]{2,1,0:T(8,128)(2,1)S(1)} async-done(((bf16[4,144,640]{2,1,0:T(8,128)(2,1)}), bf16[4,144,640]{2,1,0:T(8,128)(2,1)S(1)}, u32[]{:S(2)}, u32[]{:S(2)}) %all-to-all-start.2) | async-done | bytes 737312 | tf_op jit(solution)/shard_map/all_to_all | solution.py:214
  77.5 3.6 %all-to-all-start.1 = ((bf16[12,24,1024]{2,1,0:T(8,128)(2,1)}), bf16[12,24,1024]{2,1,0:T(8,128)(2,1)S(1)}, u32[]{:S(2)}, u32[]{:S(2)}) async-start(bf16[12,24,1024]{2,1,0:T(8,128)(2,1)} %bitcast.8), calls=%async_computation.1 | async-start | bytes 1179648 | tf_op jit(solution)/shard_map/all_to_all | solution.py:214
  81.2 1.0 shard_map.94
  82.2 2.2 %all_gather.12.cols_ref = bf16[4,288,256]{2,1,0:T(8,128)(2,1)S(1)} all-gather(bf16[4,144,256]{2,1,0:T(8,128)(2,1)S(1)} %slice.4), channel_id=1, replica_groups=mesh['y4'=2,'y2'=2,'y1'=2,'x'=4,'expert'=12,'tensor'=2] {'tensor'}, dimensions={1}, use_global_device_ids=true | all-gather | bytes 884736 | tf_op jit(solution)/shard_map/all_gather | solution.py:220
  84.4 0.8 shard_map.99
  85.2 7.6 %all_gather.13.pair_ref = bf16[512,384]{1,0:T(8,128)(2,1)S(1)} all-gather(bf16[256,384]{1,0:T(8,128)(2,1)S(1)} %get-tuple-element.30), channel_id=1, replica_groups=mesh['y4'=2,'y2'=2,'y1'=2,'x'=4,'expert'=12,'tensor'=2] {'y1'}, dimensions={0}, use_global_device_ids=true | all-gather | bytes 589824 | tf_op jit(solution)/shard_map/all_gather | solution.py:220
  92.8 0.1 shard_map.100
  92.9 7.6 %all_gather.14.pair_ref = bf16[256,384]{1,0:T(8,128)(2,1)S(1)} all-gather(bf16[128,384]{1,0:T(8,128)(2,1)S(1)} %get-tuple-element.32), channel_id=1, replica_groups=mesh['y4'=2,'y2'=2,'y1'=2,'x'=4,'expert'=12,'tensor'=2] {'y2'}, dimensions={0}, use_global_device_ids=true | all-gather | bytes 294912 | tf_op jit(solution)/shard_map/all_gather | solution.py:220
  100.6 8.7 %all_gather.15.pair_ref = bf16[128,384]{1,0:T(8,128)(2,1)S(1)} all-gather(bf16[64,384]{1,0:T(8,128)(2,1)S(1)} %get-tuple-element.34), channel_id=1, replica_groups=mesh['y4'=2,'y2'=2,'y1'=2,'x'=4,'expert'=12,'tensor'=2] {'y4'}, dimensions={0}, use_global_device_ids=true | all-gather | bytes 147456 | tf_op jit(solution)/shard_map/all_gather | solution.py:220
  109.2 0.6 shard_map.102
  109.9 1.3 %shard_map.98 = (bf16[128,1024]{1,0:T(8,128)(2,1)}, bf16[128,1024]{1,0:T(8,128)(2,1)}) custom-call(bf16[128,288]{1,0:T(8,128)(2,1)S(1)} %get-tuple-element.19.high_ref, bf16[128,288]{1,0:T(8,128)(2,1)S(1)} %get-tuple-element.20.low_ref, bf16[128,288]{1,0:T(8,128)(2,1)S(1)} %get-tuple-element.21.right_ref, bf16[288,1024]{1,0:T(8,128)(2,1)S(1)} %bitcast.21), custom_call_target="tpu_custom_call" | custom-call | flops 226492416 | bytes 1335296 | tf_op jit(solution)/shard_map/pallas_call | solution.py:33
  (6 shorter events, 0.1 us)
Async XLA Ops:
  0.6 47.5 %copy-start = (bf16[1,2048,384]{2,1,0:T(8,128)(2,1)S(1)}, bf16[1,2048,384]{2,1,0:T(8,128)(2,1)}, u32[]{:S(2)}) copy-start(bf16[1,2048,384]{2,1,0:T(8,128)(2,1)} %param.10) | copy-start | bytes 4718596
  44.3 3.9 %collective-permute-start = (bf16[288,1024]{1,0:T(8,128)(2,1)S(1)}, bf16[288,1024]{1,0:T(8,128)(2,1)S(1)}, u32[]{:S(2)}, u32[]{:S(2)}) collective-permute-start(bf16[288,1024]{1,0:T(8,128)(2,1)S(1)} %bitcast.18), channel_id=1, source_target_pairs={{0,1},{1,0},{2,3},{3,2},{4,5},{5,4},{6,7},{7,6},{8,9},{9,8},{10,11... | collective-permute-start | bytes 1769480 | tf_op jit(solution)/shard_map/ppermute | solution.py:217
  51.8 0.9 copy-start.1
  52.7 0.9 copy-start.2
  58.9 6.4 %collective-permute-start.1 = (bf16[288,1024]{1,0:T(8,128)(2,1)S(1)}, bf16[288,1024]{1,0:T(8,128)(2,1)S(1)}, u32[]{:S(2)}, u32[]{:S(2)}) collective-permute-start(bf16[288,1024]{1,0:T(8,128)(2,1)S(1)} %get-tuple-element.25), channel_id=1, source_target_pairs={{0,1},{1,0},{2,3},{3,2},{4,5},{5,4},{6,7},{7,6},{8,9},{9,8},{10,11... | collective-permute-start | bytes 1769480 | tf_op jit(solution)/shard_map/ppermute | solution.py:217
  60.9 16.6 %all-to-all-start.2 = ((bf16[4,144,640]{2,1,0:T(8,128)(2,1)}), bf16[4,144,640]{2,1,0:T(8,128)(2,1)S(1)}, u32[]{:S(2)}, u32[]{:S(2)}) async-start(bf16[4,144,640]{2,1,0:T(8,128)(2,1)} %get-tuple-element.28), calls=%async_computation.2 | async-start | bytes 1474560 | tf_op jit(solution)/shard_map/all_to_all | solution.py:214
  77.5 32.3 %all-to-all-start.1 = ((bf16[12,24,1024]{2,1,0:T(8,128)(2,1)}), bf16[12,24,1024]{2,1,0:T(8,128)(2,1)S(1)}, u32[]{:S(2)}, u32[]{:S(2)}) async-start(bf16[12,24,1024]{2,1,0:T(8,128)(2,1)} %bitcast.8), calls=%async_computation.1 | async-start | bytes 1179648 | tf_op jit(solution)/shard_map/all_to_all | solution.py:214

commit v3 on v2

--- a/solution.py
+++ b/solution.py
@@ -26,18 +26,36 @@
     return pltpu.with_memory_space_constraint(v, pltpu.HBM)
 
 
-def fused(kernel, outs, *args, scalars=0, flops=0, mib=8):
-    specs = [pl.BlockSpec(memory_space=pltpu.SMEM)] * scalars
-    specs += [pl.BlockSpec(memory_space=pltpu.VMEM)] * (len(args) - scalars)
+def fused(kernel, outs, *args, scalars=0, flops=0, mib=8, far=(), scratch=()):
+    specs = [
+        pl.BlockSpec(
+            memory_space=pltpu.SMEM if i < scalars else pltpu.HBM if i in far else pltpu.VMEM
+        )
+        for i in range(len(args))
+    ]
     nbytes = sum(math.prod(a.shape) * a.dtype.itemsize for a in list(args) + list(outs))
     return pl.pallas_call(
         kernel,
         out_shape=outs,
         in_specs=specs,
         out_specs=[pl.BlockSpec(memory_space=pltpu.VMEM)] * len(outs),
+        scratch_shapes=scratch,
         compiler_params=pltpu.CompilerParams(vmem_limit_bytes=mib << 20),
         cost_estimate=pl.CostEstimate(flops=flops, bytes_accessed=nbytes, transcendentals=0),
     )(*args)
+
+
+def fetch(pairs, sems):
+    copies = [pltpu.make_async_copy(a, b, sems.at[i]) for i, (a, b) in enumerate(pairs)]
+    for c in copies:
+        c.start()
+    return copies
+
+
+def landing(*shapes):
+    return [pltpu.VMEM(v.shape, v.dtype) for v in shapes] + [
+        pltpu.SemaphoreType.DMA((len(shapes),))
+    ]
 
 
 def routing(ids_ref, w_ref, owners, cap):
@@ -64,11 +82,18 @@
     return left, right, weight.reshape(flat)
 
 
-def dispatch_kernel(owners, cap, ids_ref, w_ref, tok_ref, cot_ref, out_ref):
+def dispatch_kernel(owners, cap, *refs):
+    sources, out_ref, landed, sems = refs[:4], refs[4], refs[5:9], refs[9]
+    copies = fetch(list(zip(sources, landed, strict=True)), sems)
+    ids_ref, w_ref, tok_ref, cot_ref = landed
+    copies[0].wait()
+    copies[1].wait()
     left, right, weight = routing(ids_ref, w_ref, owners, cap)
     scale = jnp.sum(right * weight, axis=1, keepdims=True)
-    rows = dot(left.astype(B16), tok_ref[...]) + dot(right.astype(B16), cot_ref[...]) * scale
-    out_ref[...] = rows.astype(B16)
+    left, right = left.astype(B16), right.astype(B16)
+    copies[2].wait()
+    copies[3].wait()
+    out_ref[...] = (dot(left, tok_ref[...]) + dot(right, cot_ref[...]) * scale).astype(B16)
 
 
 def plan_kernel(owners, cap, ids_ref, w_ref, high_ref, low_ref, right_ref):
@@ -100,25 +125,43 @@
     return side, here, there
 
 
-def forward_kernel(cap, side_ref, own_ref, oth_ref, wg_ref, wu_ref, gate_ref, up_ref, pack_ref):
+def own_kernel(cap, side_ref, own_ref, wg_far, wu_far, gate_ref, up_ref, cols_ref, wg, wu, sems):
     rows, half = own_ref.shape
     slots = rows // 2
-    _, here, there = halves(side_ref, half)
-    own, oth = own_ref[...], oth_ref[...]
-    to_x = pick((slots, rows), 0, cap, 0)
-    x_own, x_oth = dot(to_x, own).astype(B16), dot(to_x, oth).astype(B16)
-    gate = dot(x_own, wg_ref[here, :]) + dot(x_oth, wg_ref[there, :])
-    up = dot(x_own, wu_ref[here, :]) + dot(x_oth, wu_ref[there, :])
+    _, here, _ = halves(side_ref, half)
+    copies = fetch([(wg_far.at[here], wg), (wu_far.at[here], wu)], sems)
+    own = own_ref[...]
+    x = dot(pick((slots, rows), 0, cap, 0), own).astype(B16)
+    g = dot(pick((slots, rows), 0, cap, cap), own).astype(B16)
+    wide = half // NX
+    for xd in range(NX):
+        cols = [g[:, (y * NX + xd) * 64 : (y * NX + xd) * 64 + 64] for y in range(wide // 64)]
+        cols_ref[xd, :, 0 : wide // 2] = jnp.concatenate(cols[0::2], axis=1)
+        cols_ref[xd, :, wide // 2 : wide] = jnp.concatenate(cols[1::2], axis=1)
+    copies[0].wait()
+    gate_ref[...] = dot(x, wg[...])
+    copies[1].wait()
+    up_ref[...] = dot(x, wu[...])
+
+
+def rest_kernel(
+    cap, side_ref, oth_ref, gate_in, up_in, cols_ref, wg_far, wu_far, gate_ref, up_ref, pack_ref, wg, wu, sems
+):
+    rows, half = oth_ref.shape
+    slots = rows // 2
+    _, _, there = halves(side_ref, half)
+    copies = fetch([(wg_far.at[there], wg), (wu_far.at[there], wu)], sems)
+    wide = cols_ref.shape[2]
+    x = dot(pick((slots, rows), 0, cap, 0), oth_ref[...]).astype(B16)
+    pack_ref[:, :, 0:wide] = cols_ref[...]
+    copies[0].wait()
+    gate = gate_in[...] + dot(x, wg[...])
+    copies[1].wait()
+    up = up_in[...] + dot(x, wu[...])
     hidden = (gate * (1.0 / (1.0 + jnp.exp(-gate))) * up).astype(B16)
     gate_ref[...] = gate
     up_ref[...] = up
-    g = dot(pick((slots, rows), 0, cap, cap), own).astype(B16)
-    wide = half // NX
-    nyh = wide // 64
     for xd in range(NX):
-        cols = [g[:, (y * NX + xd) * 64 : (y * NX + xd) * 64 + 64] for y in range(nyh)]
-        pack_ref[xd, :, 0 : wide // 2] = jnp.concatenate(cols[0::2], axis=1)
-        pack_ref[xd, :, wide // 2 : wide] = jnp.concatenate(cols[1::2], axis=1)
         pack_ref[xd, :, wide:] = hidden
 
 
@@ -201,6 +244,8 @@
         hbm(tokens),
         hbm(cotangent),
         flops=4 * slots * tok_rows * half * 2,
+        far=range(4),
+        scratch=landing(ids_t, w_t, tokens, cotangent),
     )
     high, low, right = fused(
         functools.partial(plan_kernel, owners, cap),
@@ -222,18 +267,36 @@
     chunks = (owners, 2 * cap, half)
     own = trade(send, "expert", *chunks).reshape(2 * slots, half)
     oth = swap(own)
-    gate, up, pack = fused(
-        functools.partial(forward_kernel, cap),
-        [pltpu.HBM((slots, ff), F32)] * 2
-        + [pltpu.HBM((NX, slots, half // NX + ff), B16)],
+    floats = jax.ShapeDtypeStruct((slots, ff), F32)
+    halfway = landing(bf(half, ff), bf(half, ff))
+    gate, up, cols = fused(
+        functools.partial(own_kernel, cap),
+        [floats, floats, bf(NX, slots, half // NX)],
         side,
         own,
-        oth,
-        gate_weight[0],
+        hbm(gate_weight[0]),
         hbm(up_weight[0]),
         scalars=1,
-        flops=slots * half * 2 * ff * 4 + slots * 2 * slots * half * 8,
-        mib=20,
+        flops=slots * half * 2 * ff * 2 + slots * 2 * slots * half * 4,
+        mib=12,
+        far=(2, 3),
+        scratch=halfway,
+    )
+    gate, up, pack = fused(
+        functools.partial(rest_kernel, cap),
+        [pltpu.HBM((slots, ff), F32)] * 2 + [pltpu.HBM((NX, slots, half // NX + ff), B16)],
+        side,
+        oth,
+        gate,
+        up,
+        cols,
+        hbm(gate_weight[0]),
+        hbm(up_weight[0]),
+        scalars=1,
+        flops=slots * half * 2 * ff * 2 + slots * 2 * slots * half * 2,
+        mib=12,
+        far=(5, 6),
+        scratch=halfway,
     )
     packs = trade(pack, "x", *pack.shape)
     keep, give = fused(

time: 112 us -> 111 us (level)
  the two profiles are of different devices: /device:TPU:32 before, /device:TPU:56 now
where the time goes in v3:
time: 111 us; the launch traced here: 110 us
  blocking collectives  68 us (61%)
  Pallas kernels  15.1 us (14%)
  starting transfers between devices  12.1 us (11%)
  waiting for transfers between devices  11.2 us (10%)
  local copies, waits for them, and re-layouts  1.89 us (2%)
    all_to_all x1, blocking collectives, trade(): lax.all_to_all(rows.reshape(shape), axis, split_axis=0, concat_axis=0, ti...  41.8 us
    all_gather x4, blocking collectives, pair(): return lax.all_gather(v, axis, axis=dim, tiled=True)  26.2 us
    pallas_call x10, Pallas kernels, fused(): pl.pallas_call(kernel, out_shape=outs, in_specs=specs, out_specs=[pl.Bloc...  15.1 us
    all_to_all x2, waiting for transfers between devices, trade(): lax.all_to_all(rows.reshape(shape), axis, split_axis=0, concat_axis=0, ti...  11 us
    all_to_all x2, starting transfers between devices, trade(): lax.all_to_all(rows.reshape(shape), axis, split_axis=0, concat_axis=0, ti...  7.93 us
    ppermute x2, starting transfers between devices, swap(): return lax.ppermute(v, 'tensor', [(0, 1), (1, 0)])  4.16 us
  transfers between devices with their start and end apart: 4, of which 2 were waited for; matrix products, arithmetic and copies ran while one was open for 1% of the time, Pallas kernels for 4%

profile of v3, /device:TPU:56, one launch (start us, length us, event | category | flops | bytes accessed | tf_op | source)
XLA Modules:
  0.0 110.1 jit_solution(17606293242033709704)
XLA Ops:
  0.6 1.6 %shard_map.95 = bf16[288,1024]{1,0:T(8,128)(2,1)S(1)} custom-call(s32[8,128]{1,0:T(8,128)} %bitcast.29, f32[8,128]{1,0:T(8,128)} %bitcast.31, bf16[128,1024]{1,0:T(8,128)(2,1)} %refs_2_.1, bf16[128,1024]{1,0:T(8,128)(2,1)} %refs_3_.1), custom_call_target="tpu_custom_call" | custom-call | flops 150994944 | bytes 1122304 | tf_op jit(solution)/shard_map/pallas_call | solution.py:37
  2.2 41.8 %all_to_all.15 = bf16[12,24,1024]{2,1,0:T(8,128)(2,1)S(1)} all-to-all(bf16[12,24,1024]{2,1,0:T(8,128)(2,1)S(1)} %bitcast.20), channel_id=1, replica_groups=mesh['y4'=2,'y2'=2,'y1'=2,'x'=4,'expert'=12,'tensor'=2] {'expert'}, dimensions={0} | all-to-all | bytes 1179648 | tf_op jit(solution)/shard_map/all_to_all | solution.py:259
  44.0 1.9 %collective-permute-start = (bf16[288,1024]{1,0:T(8,128)(2,1)S(1)}, bf16[288,1024]{1,0:T(8,128)(2,1)S(1)}, u32[]{:S(2)}, u32[]{:S(2)}) collective-permute-start(bf16[288,1024]{1,0:T(8,128)(2,1)S(1)} %bitcast.16), channel_id=1, source_target_pairs={{0,1},{1,0},{2,3},{3,2},{4,5},{5,4},{6,7},{7,6},{8,9},{9,8},{10,11... | collective-permute-start | bytes 1769480 | tf_op jit(solution)/shard_map/ppermute | solution.py:262
  46.0 1.8 %shard_map.96 = (f32[144,384]{1,0:T(8,128)S(1)}, f32[144,384]{1,0:T(8,128)S(1)}, bf16[4,144,256]{2,1,0:T(8,128)(2,1)S(1)}) custom-call(s32[1]{0:T(128)} %bitcast.2.side_ref, bf16[288,1024]{1,0:T(8,128)(2,1)S(1)} %bitcast.17, bf16[2048,384]{1,0:T(8,128)(2,1)} %bitcast.21, bf16[2048,384]{1,0:T(8,128)(2,1)} %bitcast.24), custom_call_target="tpu_custom_call" | custom-call | flops 396361728 | bytes 4472836 | tf_op jit(solution)/shard_map/pallas_call | solution.py:37
  47.8 0.2 collective-permute-done.oth_ref
  47.9 2.8 %shard_map.97 = (f32[144,384]{1,0:T(8,128)}, f32[144,384]{1,0:T(8,128)}, bf16[4,144,640]{2,1,0:T(8,128)(2,1)}) custom-call(s32[1]{0:T(128)} %bitcast.2.side_ref, bf16[288,1024]{1,0:T(8,128)(2,1)S(1)} %collective-permute-done.oth_ref, f32[144,384]{1,0:T(8,128)S(1)} %get-tuple-element.25.gate_in, f32[144,384]{1,0:T(8,128)S(1)} %get-tuple-element.26.up_in, ...), custom_call_target="tpu_custom_call" | custom-call | flops 311427072 | bytes 5652484 | tf_op jit(solution)/shard_map/pallas_call | solution.py:37
  50.7 0.0 copy-start
  50.7 0.9 copy-done
  51.6 0.9 copy-done.1
  52.6 5.2 %shard_map.98 = (bf16[288,1024]{1,0:T(8,128)(2,1)S(1)}, bf16[288,1024]{1,0:T(8,128)(2,1)S(1)}) custom-call(s32[1]{0:T(128)} %bitcast.2.side_ref, bf16[288,1024]{1,0:T(8,128)(2,1)S(1)} %bitcast.18, bf16[288,1024]{1,0:T(8,128)(2,1)S(1)} %collective-permute-done.oth_ref, f32[144,384]{1,0:T(8,128)S(1)} %copy-done, f32[144,384]{1,0:T(8,128)S(1)} %copy-done.1, ...), custom_call_target="tpu_custom_call" | custom-call | flops 1415577600 | bytes 7520260 | tf_op jit(solution)/shard_map/pallas_call | solution.py:37
  57.8 2.2 %collective-permute-start.1 = (bf16[288,1024]{1,0:T(8,128)(2,1)S(1)}, bf16[288,1024]{1,0:T(8,128)(2,1)S(1)}, u32[]{:S(2)}, u32[]{:S(2)}) collective-permute-start(bf16[288,1024]{1,0:T(8,128)(2,1)S(1)} %get-tuple-element.31), channel_id=1, source_target_pairs={{0,1},{1,0},{2,3},{3,2},{4,5},{5,4},{6,7},{7,6},{8,9},{9,8},{10,11... | collective-permute-start | bytes 1769480 | tf_op jit(solution)/shard_map/ppermute | solution.py:262
  60.1 4.3 %all-to-all-start.2 = ((bf16[4,144,640]{2,1,0:T(8,128)(2,1)}), bf16[4,144,640]{2,1,0:T(8,128)(2,1)S(1)}, u32[]{:S(2)}, u32[]{:S(2)}) async-start(bf16[4,144,640]{2,1,0:T(8,128)(2,1)} %get-tuple-element.34), calls=%async_computation.2 | async-start | bytes 1474560 | tf_op jit(solution)/shard_map/all_to_all | solution.py:259
  64.4 1.1 add_convert_fusion
  65.5 11.0 %all-to-all-done.2.packs_ref = bf16[4,144,640]{2,1,0:T(8,128)(2,1)S(1)} async-done(((bf16[4,144,640]{2,1,0:T(8,128)(2,1)}), bf16[4,144,640]{2,1,0:T(8,128)(2,1)S(1)}, u32[]{:S(2)}, u32[]{:S(2)}) %all-to-all-start.2) | async-done | bytes 737312 | tf_op jit(solution)/shard_map/all_to_all | solution.py:259
  76.5 3.6 %all-to-all-start.1 = ((bf16[12,24,1024]{2,1,0:T(8,128)(2,1)}), bf16[12,24,1024]{2,1,0:T(8,128)(2,1)S(1)}, u32[]{:S(2)}, u32[]{:S(2)}) async-start(bf16[12,24,1024]{2,1,0:T(8,128)(2,1)} %bitcast.8), calls=%async_computation.1 | async-start | bytes 1179648 | tf_op jit(solution)/shard_map/all_to_all | solution.py:259
  80.1 1.0 shard_map.94
  81.1 2.2 %all_gather.12.cols_ref = bf16[4,288,256]{2,1,0:T(8,128)(2,1)S(1)} all-gather(bf16[4,144,256]{2,1,0:T(8,128)(2,1)S(1)} %slice.4), channel_id=1, replica_groups=mesh['y4'=2,'y2'=2,'y1'=2,'x'=4,'expert'=12,'tensor'=2] {'tensor'}, dimensions={1}, use_global_device_ids=true | all-gather | bytes 884736 | tf_op jit(solution)/shard_map/all_gather | solution.py:265
  83.4 0.8 shard_map.100
  84.1 7.6 %all_gather.13.pair_ref = bf16[512,384]{1,0:T(8,128)(2,1)S(1)} all-gather(bf16[256,384]{1,0:T(8,128)(2,1)S(1)} %get-tuple-element.36), channel_id=1, replica_groups=mesh['y4'=2,'y2'=2,'y1'=2,'x'=4,'expert'=12,'tensor'=2] {'y1'}, dimensions={0}, use_global_device_ids=true | all-gather | bytes 589824 | tf_op jit(solution)/shard_map/all_gather | solution.py:265
  91.8 0.1 shard_map.101
  91.8 7.6 %all_gather.14.pair_ref = bf16[256,384]{1,0:T(8,128)(2,1)S(1)} all-gather(bf16[128,384]{1,0:T(8,128)(2,1)S(1)} %get-tuple-element.38), channel_id=1, replica_groups=mesh['y4'=2,'y2'=2,'y1'=2,'x'=4,'expert'=12,'tensor'=2] {'y2'}, dimensions={0}, use_global_device_ids=true | all-gather | bytes 294912 | tf_op jit(solution)/shard_map/all_gather | solution.py:265
  99.5 8.7 %all_gather.15.pair_ref = bf16[128,384]{1,0:T(8,128)(2,1)S(1)} all-gather(bf16[64,384]{1,0:T(8,128)(2,1)S(1)} %get-tuple-element.40), channel_id=1, replica_groups=mesh['y4'=2,'y2'=2,'y1'=2,'x'=4,'expert'=12,'tensor'=2] {'y4'}, dimensions={0}, use_global_device_ids=true | all-gather | bytes 147456 | tf_op jit(solution)/shard_map/all_gather | solution.py:265
  108.2 0.6 shard_map.103
  108.8 1.3 %shard_map.99 = (bf16[128,1024]{1,0:T(8,128)(2,1)}, bf16[128,1024]{1,0:T(8,128)(2,1)}) custom-call(bf16[128,288]{1,0:T(8,128)(2,1)S(1)} %get-tuple-element.22.high_ref, bf16[128,288]{1,0:T(8,128)(2,1)S(1)} %get-tuple-element.23.low_ref, bf16[128,288]{1,0:T(8,128)(2,1)S(1)} %get-tuple-element.24.right_ref, bf16[288,1024]{1,0:T(8,128)(2,1)S(1)} %bitcast.19), custom_call_target="tpu_custom_call" | custom-call | flops 226492416 | bytes 1335296 | tf_op jit(solution)/shard_map/pallas_call | solution.py:37
  (5 shorter events, 0.1 us)
Async XLA Ops:
  44.0 3.9 %collective-permute-start = (bf16[288,1024]{1,0:T(8,128)(2,1)S(1)}, bf16[288,1024]{1,0:T(8,128)(2,1)S(1)}, u32[]{:S(2)}, u32[]{:S(2)}) collective-permute-start(bf16[288,1024]{1,0:T(8,128)(2,1)S(1)} %bitcast.16), channel_id=1, source_target_pairs={{0,1},{1,0},{2,3},{3,2},{4,5},{5,4},{6,7},{7,6},{8,9},{9,8},{10,11... | collective-permute-start | bytes 1769480 | tf_op jit(solution)/shard_map/ppermute | solution.py:262
  50.7 0.9 copy-start
  51.6 0.9 copy-start.1
  57.8 6.6 %collective-permute-start.1 = (bf16[288,1024]{1,0:T(8,128)(2,1)S(1)}, bf16[288,1024]{1,0:T(8,128)(2,1)S(1)}, u32[]{:S(2)}, u32[]{:S(2)}) collective-permute-start(bf16[288,1024]{1,0:T(8,128)(2,1)S(1)} %get-tuple-element.31), channel_id=1, source_target_pairs={{0,1},{1,0},{2,3},{3,2},{4,5},{5,4},{6,7},{7,6},{8,9},{9,8},{10,11... | collective-permute-start | bytes 1769480 | tf_op jit(solution)/shard_map/ppermute | solution.py:262
  60.1 16.4 %all-to-all-start.2 = ((bf16[4,144,640]{2,1,0:T(8,128)(2,1)}), bf16[4,144,640]{2,1,0:T(8,128)(2,1)S(1)}, u32[]{:S(2)}, u32[]{:S(2)}) async-start(bf16[4,144,640]{2,1,0:T(8,128)(2,1)} %get-tuple-element.34), calls=%async_computation.2 | async-start | bytes 1474560 | tf_op jit(solution)/shard_map/all_to_all | solution.py:259
  76.5 32.3 %all-to-all-start.1 = ((bf16[12,24,1024]{2,1,0:T(8,128)(2,1)}), bf16[12,24,1024]{2,1,0:T(8,128)(2,1)S(1)}, u32[]{:S(2)}, u32[]{:S(2)}) async-start(bf16[12,24,1024]{2,1,0:T(8,128)(2,1)} %bitcast.8), calls=%async_computation.1 | async-start | bytes 1179648 | tf_op jit(solution)/shard_map/all_to_all | solution.py:259

commit v4 on v3

--- a/solution.py
+++ b/solution.py
@@ -105,7 +105,13 @@
     right_ref[...] = right.T.astype(B16)
 
 
-def combine_kernel(high_ref, low_ref, right_ref, rows_ref, mixed_ref, grad_ref):
+def combine_kernel(
+    bit_ref, high_ref, low_ref, right_ref, rows_ref, mine_ref, pair_ref, mixed_ref, grad_ref, down_ref
+):
+    n = mine_ref.shape[1]
+    for h in range(2):
+        both = mine_ref[h].astype(F32) + partner(bit_ref, pair_ref, h, 0, n)
+        down_ref[h * n : (h + 1) * n, :] = both.astype(B16)
     rows = rows_ref[...]
     mixed_ref[...] = (dot(high_ref[...], rows) + dot(low_ref[...], rows)).astype(B16)
     grad_ref[...] = dot(right_ref[...], rows).astype(B16)
@@ -125,11 +131,11 @@
     return side, here, there
 
 
-def own_kernel(cap, side_ref, own_ref, wg_far, wu_far, gate_ref, up_ref, cols_ref, wg, wu, sems):
+def own_kernel(cap, side_ref, own_ref, wg_ref, wu_far, gate_ref, up_ref, cols_ref, wu, sems):
     rows, half = own_ref.shape
     slots = rows // 2
     _, here, _ = halves(side_ref, half)
-    copies = fetch([(wg_far.at[here], wg), (wu_far.at[here], wu)], sems)
+    copies = fetch([(wu_far.at[here], wu)], sems)
     own = own_ref[...]
     x = dot(pick((slots, rows), 0, cap, 0), own).astype(B16)
     g = dot(pick((slots, rows), 0, cap, cap), own).astype(B16)
@@ -138,25 +144,23 @@
         cols = [g[:, (y * NX + xd) * 64 : (y * NX + xd) * 64 + 64] for y in range(wide // 64)]
         cols_ref[xd, :, 0 : wide // 2] = jnp.concatenate(cols[0::2], axis=1)
         cols_ref[xd, :, wide // 2 : wide] = jnp.concatenate(cols[1::2], axis=1)
+    gate_ref[...] = dot(x, wg_ref[here, :])
     copies[0].wait()
-    gate_ref[...] = dot(x, wg[...])
-    copies[1].wait()
     up_ref[...] = dot(x, wu[...])
 
 
 def rest_kernel(
-    cap, side_ref, oth_ref, gate_in, up_in, cols_ref, wg_far, wu_far, gate_ref, up_ref, pack_ref, wg, wu, sems
+    cap, side_ref, oth_ref, gate_in, up_in, cols_ref, wg_ref, wu_far, gate_ref, up_ref, pack_ref, wu, sems
 ):
     rows, half = oth_ref.shape
     slots = rows // 2
     _, _, there = halves(side_ref, half)
-    copies = fetch([(wg_far.at[there], wg), (wu_far.at[there], wu)], sems)
+    copies = fetch([(wu_far.at[there], wu)], sems)
     wide = cols_ref.shape[2]
     x = dot(pick((slots, rows), 0, cap, 0), oth_ref[...]).astype(B16)
     pack_ref[:, :, 0:wide] = cols_ref[...]
+    gate = gate_in[...] + dot(x, wg_ref[there, :])
     copies[0].wait()
-    gate = gate_in[...] + dot(x, wg[...])
-    copies[1].wait()
     up = up_in[...] + dot(x, wu[...])
     hidden = (gate * (1.0 / (1.0 + jnp.exp(-gate))) * up).astype(B16)
     gate_ref[...] = gate
@@ -189,7 +193,7 @@
 
 
 def down_kernel(bit_ref, packs_ref, cols_ref, keep_ref, give_ref):
-    n = keep_ref.shape[0] // 2
+    n = keep_ref.shape[1]
     slots = packs_ref.shape[1]
     wide = cols_ref.shape[2]
     bit = bit_ref[0]
@@ -201,28 +205,31 @@
                 rows = cols_ref[k, h * slots : (h + 1) * slots, cols]
                 part = dot(rows, packs_ref[k, :, wide:], ROWS0)
                 total = part if total is None else total + part
-            out[h * n : (h + 1) * n, :] = total.astype(B16)
-
-
-def partner_row(bit_ref, pair_ref, at, n):
-    start = (1 - bit_ref[0]) * (pair_ref.shape[0] // 2) + at
-    return pair_ref[pl.ds(pl.multiple_of(start, n), n), :].astype(F32)
-
-
-def halve_kernel(blocks, last_ref, bit_ref, mine_ref, pair_ref, keep_ref, give_ref):
-    n = keep_ref.shape[0] // blocks
+            out[h] = total.astype(B16)
+
+
+def partner(bit_ref, pair_ref, h, at, n):
+    start = (1 - bit_ref[0]) * (pair_ref.shape[1] // 2) + at
+    return pair_ref[h, pl.ds(pl.multiple_of(start, n), n), :].astype(F32)
+
+
+def halve_rows_kernel(last_ref, bit_ref, mine_ref, pair_ref, keep_ref, give_ref):
+    n = keep_ref.shape[1]
     bit = bit_ref[0]
     for side, out in ((1 - bit, give_ref), (bit, keep_ref)):
-        for k in range(blocks):
-            at = (2 * k + side) * n
-            mine = mine_ref[pl.ds(pl.multiple_of(at, n), n), :].astype(F32)
-            both = mine + partner_row(last_ref, pair_ref, at, n)
-            out[k * n : (k + 1) * n, :] = both.astype(B16)
-
-
-def finish_kernel(last_ref, mine_ref, pair_ref, out_ref):
-    n = out_ref.shape[0]
-    out_ref[...] = (mine_ref[...].astype(F32) + partner_row(last_ref, pair_ref, 0, n)).astype(B16)
+        for h in range(2):
+            mine = mine_ref[h, pl.ds(pl.multiple_of(side * n, n), n), :].astype(F32)
+            out[h] = (mine + partner(last_ref, pair_ref, h, side * n, n)).astype(B16)
+
+
+def halve_sides_kernel(last_ref, bit_ref, mine_ref, pair_ref, keep_ref, give_ref):
+    n = keep_ref.shape[1]
+    bit = bit_ref[0]
+    for side, out in ((1 - bit, give_ref), (bit, keep_ref)):
+        both = mine_ref[side].astype(F32) + partner(last_ref, pair_ref, side, 0, 2 * n)
+        both = both.astype(B16)
+        out[0] = both[0:n]
+        out[1] = both[n : 2 * n]
 
 
 def per_device(tokens, expert_ids, route_weight, gate_weight, up_weight, down_weight, cotangent):
@@ -261,25 +268,25 @@
     def swap(v):
         return lax.ppermute(v, "tensor", [(0, 1), (1, 0)])
 
-    def pair(v, axis, dim=0):
-        return lax.all_gather(v, axis, axis=dim, tiled=True)
+    def pair(v, axis):
+        return lax.all_gather(v, axis, axis=1, tiled=True)
 
     chunks = (owners, 2 * cap, half)
     own = trade(send, "expert", *chunks).reshape(2 * slots, half)
     oth = swap(own)
     floats = jax.ShapeDtypeStruct((slots, ff), F32)
-    halfway = landing(bf(half, ff), bf(half, ff))
+    halfway = landing(bf(half, ff))
     gate, up, cols = fused(
         functools.partial(own_kernel, cap),
         [floats, floats, bf(NX, slots, half // NX)],
         side,
         own,
-        hbm(gate_weight[0]),
+        gate_weight[0],
         hbm(up_weight[0]),
         scalars=1,
         flops=slots * half * 2 * ff * 2 + slots * 2 * slots * half * 4,
         mib=12,
-        far=(2, 3),
+        far=(3,),
         scratch=halfway,
     )
     gate, up, pack = fused(
@@ -290,12 +297,12 @@
         gate,
         up,
         cols,
-        hbm(gate_weight[0]),
+        gate_weight[0],
         hbm(up_weight[0]),
         scalars=1,
         flops=slots * half * 2 * ff * 2 + slots * 2 * slots * half * 2,
         mib=12,
-        far=(5, 6),
+        far=(6,),
         scratch=halfway,
     )
     packs = trade(pack, "x", *pack.shape)
@@ -316,37 +323,37 @@
     )
     total = (keep.astype(F32) + swap(give).astype(F32)).astype(B16)
     back = trade(total, "expert", *chunks).reshape(2 * slots, half)
-    mixed, token_grad = fused(
-        combine_kernel,
-        [bf(tok_rows, half)] * 2,
-        high,
-        low,
-        right,
-        back,
-        flops=tok_rows * 2 * slots * half * 6,
-    )
     keep, give = fused(
         down_kernel,
-        [bf(half // 4, ff)] * 2,
+        [bf(2, half // 8, ff)] * 2,
         bits[0],
         packs,
-        pair(packs[:, :, : half // NX], "tensor", 1),
+        pair(packs[:, :, : half // NX], "tensor"),
         scalars=1,
         flops=half // 2 * ff * slots * 2 * NX,
     )
-    for step, blocks in ((1, 2), (2, 1)):
-        rows = keep.shape[0] // 2
+    for step, kernel in ((1, halve_rows_kernel), (2, halve_sides_kernel)):
         keep, give = fused(
-            functools.partial(halve_kernel, blocks),
-            [bf(rows, ff)] * 2,
+            kernel,
+            [bf(2, keep.shape[1] // 2, ff)] * 2,
             bits[step - 1],
             bits[step],
             keep,
             pair(give, ("y1", "y2")[step - 1]),
             scalars=2,
         )
-    (down_grad,) = fused(
-        finish_kernel, [bf(*keep.shape)], bits[2], keep, pair(give, "y4"), scalars=1
+    mixed, token_grad, down_grad = fused(
+        combine_kernel,
+        [bf(tok_rows, half)] * 2 + [bf(half // 16, ff)],
+        bits[2],
+        high,
+        low,
+        right,
+        back,
+        keep,
+        pair(give, "y4"),
+        scalars=1,
+        flops=tok_rows * 2 * slots * half * 6,
     )
     return mixed, token_grad, down_grad.T[None]
 

time: 111 us -> 110 us (level)
  the two profiles are of different devices: /device:TPU:56 before, /device:TPU:32 now
where the time goes in v4:
time: 110 us
  blocking collectives  68 us (62%)
  Pallas kernels  14.8 us (13%)
  starting transfers between devices  12.2 us (11%)
  waiting for transfers between devices  10.9 us (10%)
  local copies, waits for them, and re-layouts  1.89 us (2%)
    all_to_all x1, blocking collectives, trade(): lax.all_to_all(rows.reshape(shape), axis, split_axis=0, concat_axis=0, ti...  41.8 us
    all_gather x4, blocking collectives, pair(): return lax.all_gather(v, axis, axis=1, tiled=True)  26.1 us
    pallas_call x9, Pallas kernels, fused(): pl.pallas_call(kernel, out_shape=outs, in_specs=specs, out_specs=[pl.Bloc...  14.8 us
    all_to_all x2, waiting for transfers between devices, trade(): lax.all_to_all(rows.reshape(shape), axis, split_axis=0, concat_axis=0, ti...  10.9 us
    all_to_all x2, starting transfers between devices, trade(): lax.all_to_all(rows.reshape(shape), axis, split_axis=0, concat_axis=0, ti...  7.92 us
    ppermute x2, starting transfers between devices, swap(): return lax.ppermute(v, 'tensor', [(0, 1), (1, 0)])  4.31 us
  transfers between devices with their start and end apart: 4, of which 1 were waited for; matrix products, arithmetic and copies ran while one was open for 1% of the time, Pallas kernels for 4%

profile of v4, /device:TPU:32, one launch (start us, length us, event | category | flops | bytes accessed | tf_op | source)
XLA Modules:
  0.0 109.6 jit_solution(5231235868757460381)
XLA Ops:
  0.6 0.0 copy-start
  0.6 1.7 %shard_map.95 = bf16[288,1024]{1,0:T(8,128)(2,1)S(1)} custom-call(s32[8,128]{1,0:T(8,128)} %bitcast.28, f32[8,128]{1,0:T(8,128)} %bitcast.30, bf16[128,1024]{1,0:T(8,128)(2,1)} %refs_2_.1, bf16[128,1024]{1,0:T(8,128)(2,1)} %refs_3_.1), custom_call_target="tpu_custom_call" | custom-call | flops 150994944 | bytes 1122304 | tf_op jit(solution)/shard_map/pallas_call | solution.py:37
  2.3 41.8 %all_to_all.15 = bf16[12,24,1024]{2,1,0:T(8,128)(2,1)S(1)} all-to-all(bf16[12,24,1024]{2,1,0:T(8,128)(2,1)S(1)} %bitcast.23), channel_id=1, replica_groups=mesh['y4'=2,'y2'=2,'y1'=2,'x'=4,'expert'=12,'tensor'=2] {'expert'}, dimensions={0} | all-to-all | bytes 1179648 | tf_op jit(solution)/shard_map/all_to_all | solution.py:266
  44.2 1.9 %collective-permute-start = (bf16[288,1024]{1,0:T(8,128)(2,1)S(1)}, bf16[288,1024]{1,0:T(8,128)(2,1)S(1)}, u32[]{:S(2)}, u32[]{:S(2)}) collective-permute-start(bf16[288,1024]{1,0:T(8,128)(2,1)S(1)} %bitcast.19), channel_id=1, source_target_pairs={{0,1},{1,0},{2,3},{3,2},{4,5},{5,4},{6,7},{7,6},{8,9},{9,8},{10,11... | collective-permute-start | bytes 1769480 | tf_op jit(solution)/shard_map/ppermute | solution.py:269
  46.1 2.0 %shard_map.96 = (f32[144,384]{1,0:T(8,128)S(1)}, f32[144,384]{1,0:T(8,128)S(1)}, bf16[4,144,256]{2,1,0:T(8,128)(2,1)S(1)}) custom-call(s32[1]{0:T(128)} %bitcast.3.side_ref, bf16[288,1024]{1,0:T(8,128)(2,1)S(1)} %bitcast.20, bf16[2048,384]{1,0:T(8,128)(2,1)S(1)} %bitcast.17, bf16[2048,384]{1,0:T(8,128)(2,1)} %bitcast.24), custom_call_target="tpu_custom_call" | custom-call | flops 396361728 | bytes 4472836 | tf_op jit(solution)/shard_map/pallas_call | solution.py:37
  48.1 2.7 %shard_map.97 = (f32[144,384]{1,0:T(8,128)}, f32[144,384]{1,0:T(8,128)}, bf16[4,144,640]{2,1,0:T(8,128)(2,1)}) custom-call(s32[1]{0:T(128)} %bitcast.3.side_ref, bf16[288,1024]{1,0:T(8,128)(2,1)S(1)} %collective-permute-done.oth_ref, f32[144,384]{1,0:T(8,128)S(1)} %get-tuple-element.26.gate_in, f32[144,384]{1,0:T(8,128)S(1)} %get-tuple-element.27.up_in, ...), custom_call_target="tpu_custom_call" | custom-call | flops 311427072 | bytes 5652484 | tf_op jit(solution)/shard_map/pallas_call | solution.py:37
  50.9 0.0 copy-start.1
  50.9 0.9 copy-done.1
  51.8 0.9 copy-done.2
  52.8 5.2 %shard_map.98 = (bf16[288,1024]{1,0:T(8,128)(2,1)S(1)}, bf16[288,1024]{1,0:T(8,128)(2,1)S(1)}) custom-call(s32[1]{0:T(128)} %bitcast.3.side_ref, bf16[288,1024]{1,0:T(8,128)(2,1)S(1)} %bitcast.21, bf16[288,1024]{1,0:T(8,128)(2,1)S(1)} %collective-permute-done.oth_ref, f32[144,384]{1,0:T(8,128)S(1)} %copy-done.1, f32[144,384]{1,0:T(8,128)S(1)} %copy-done.2, ...), custom_call_target="tpu_custom_call" | custom-call | flops 1415577600 | bytes 7520260 | tf_op jit(solution)/shard_map/pallas_call | solution.py:37
  58.0 2.4 %collective-permute-start.1 = (bf16[288,1024]{1,0:T(8,128)(2,1)S(1)}, bf16[288,1024]{1,0:T(8,128)(2,1)S(1)}, u32[]{:S(2)}, u32[]{:S(2)}) collective-permute-start(bf16[288,1024]{1,0:T(8,128)(2,1)S(1)} %get-tuple-element.32), channel_id=1, source_target_pairs={{0,1},{1,0},{2,3},{3,2},{4,5},{5,4},{6,7},{7,6},{8,9},{9,8},{10,11... | collective-permute-start | bytes 1769480 | tf_op jit(solution)/shard_map/ppermute | solution.py:269
  60.4 4.3 %all-to-all-start.2 = ((bf16[4,144,640]{2,1,0:T(8,128)(2,1)}), bf16[4,144,640]{2,1,0:T(8,128)(2,1)S(1)}, u32[]{:S(2)}, u32[]{:S(2)}) async-start(bf16[4,144,640]{2,1,0:T(8,128)(2,1)} %get-tuple-element.33), calls=%async_computation.2 | async-start | bytes 1474560 | tf_op jit(solution)/shard_map/all_to_all | solution.py:266
  64.7 0.0 collective-permute-done.1
  64.7 1.1 add_convert_fusion
  65.8 10.9 %all-to-all-done.2.packs_ref = bf16[4,144,640]{2,1,0:T(8,128)(2,1)S(1)} async-done(((bf16[4,144,640]{2,1,0:T(8,128)(2,1)}), bf16[4,144,640]{2,1,0:T(8,128)(2,1)S(1)}, u32[]{:S(2)}, u32[]{:S(2)}) %all-to-all-start.2) | async-done | bytes 737312 | tf_op jit(solution)/shard_map/all_to_all | solution.py:266
  76.7 3.6 %all-to-all-start.1 = ((bf16[12,24,1024]{2,1,0:T(8,128)(2,1)}), bf16[12,24,1024]{2,1,0:T(8,128)(2,1)S(1)}, u32[]{:S(2)}, u32[]{:S(2)}) async-start(bf16[12,24,1024]{2,1,0:T(8,128)(2,1)} %bitcast.9), calls=%async_computation.1 | async-start | bytes 1179648 | tf_op jit(solution)/shard_map/all_to_all | solution.py:266
  80.3 1.0 shard_map.94
  81.3 2.2 %all_gather.12.cols_ref = bf16[4,288,256]{2,1,0:T(8,128)(2,1)S(1)} all-gather(bf16[4,144,256]{2,1,0:T(8,128)(2,1)S(1)} %slice.4), channel_id=1, replica_groups=mesh['y4'=2,'y2'=2,'y1'=2,'x'=4,'expert'=12,'tensor'=2] {'tensor'}, dimensions={1}, use_global_device_ids=true | all-gather | bytes 884736 | tf_op jit(solution)/shard_map/all_gather | solution.py:272
  83.6 0.8 shard_map.99
  84.3 7.6 %all_gather.13.pair_ref = bf16[2,256,384]{2,1,0:T(8,128)(2,1)S(1)} all-gather(bf16[2,128,384]{2,1,0:T(8,128)(2,1)S(1)} %get-tuple-element.35), channel_id=1, replica_groups=mesh['y4'=2,'y2'=2,'y1'=2,'x'=4,'expert'=12,'tensor'=2] {'y1'}, dimensions={1}, use_global_device_ids=true | all-gather | bytes 589824 | tf_op jit(solution)/shard_map/all_gather | solution.py:272
  91.9 0.1 shard_map.100
  92.0 7.6 %all_gather.14.pair_ref = bf16[2,128,384]{2,1,0:T(8,128)(2,1)S(1)} all-gather(bf16[2,64,384]{2,1,0:T(8,128)(2,1)S(1)} %get-tuple-element.37), channel_id=1, replica_groups=mesh['y4'=2,'y2'=2,'y1'=2,'x'=4,'expert'=12,'tensor'=2] {'y2'}, dimensions={1}, use_global_device_ids=true | all-gather | bytes 294912 | tf_op jit(solution)/shard_map/all_gather | solution.py:272
  99.7 8.7 %all_gather.15.pair_ref = bf16[2,64,384]{2,1,0:T(8,128)(2,1)S(1)} all-gather(bf16[2,32,384]{2,1,0:T(8,128)(2,1)S(1)} %get-tuple-element.39), channel_id=1, replica_groups=mesh['y4'=2,'y2'=2,'y1'=2,'x'=4,'expert'=12,'tensor'=2] {'y4'}, dimensions={1}, use_global_device_ids=true | all-gather | bytes 147456 | tf_op jit(solution)/shard_map/all_gather | solution.py:272
  108.4 1.3 %shard_map.102 = (bf16[128,1024]{1,0:T(8,128)(2,1)}, bf16[128,1024]{1,0:T(8,128)(2,1)}, bf16[64,384]{1,0:T(8,128)(2,1)}) custom-call(s32[1]{0:T(128)} %bitcast.bit_ref, bf16[128,288]{1,0:T(8,128)(2,1)S(1)} %get-tuple-element.23.high_ref, bf16[128,288]{1,0:T(8,128)(2,1)S(1)} %get-tuple-element.24.low_ref, bf16[128,288]{1,0:T(8,128)(2,1)S(1)} %get-tuple-element.25.right_ref, ...), custom_call_target="tpu_custom_call" | custom-call | flops 226492416 | bytes 1531908 | tf_op jit(solution)/shard_map/pallas_call | solution.py:37
  (6 shorter events, 0.1 us)
Async XLA Ops:
  0.6 45.5 %copy-start = (bf16[1,2048,384]{2,1,0:T(8,128)(2,1)S(1)}, bf16[1,2048,384]{2,1,0:T(8,128)(2,1)}, u32[]{:S(2)}) copy-start(bf16[1,2048,384]{2,1,0:T(8,128)(2,1)} %param.10) | copy-start | bytes 4718596
  44.2 4.0 %collective-permute-start = (bf16[288,1024]{1,0:T(8,128)(2,1)S(1)}, bf16[288,1024]{1,0:T(8,128)(2,1)S(1)}, u32[]{:S(2)}, u32[]{:S(2)}) collective-permute-start(bf16[288,1024]{1,0:T(8,128)(2,1)S(1)} %bitcast.19), channel_id=1, source_target_pairs={{0,1},{1,0},{2,3},{3,2},{4,5},{5,4},{6,7},{7,6},{8,9},{9,8},{10,11... | collective-permute-start | bytes 1769480 | tf_op jit(solution)/shard_map/ppermute | solution.py:269
  50.9 0.9 copy-start.1
  51.8 0.9 copy-start.2
  58.0 6.7 %collective-permute-start.1 = (bf16[288,1024]{1,0:T(8,128)(2,1)S(1)}, bf16[288,1024]{1,0:T(8,128)(2,1)S(1)}, u32[]{:S(2)}, u32[]{:S(2)}) collective-permute-start(bf16[288,1024]{1,0:T(8,128)(2,1)S(1)} %get-tuple-element.32), channel_id=1, source_target_pairs={{0,1},{1,0},{2,3},{3,2},{4,5},{5,4},{6,7},{7,6},{8,9},{9,8},{10,11... | collective-permute-start | bytes 1769480 | tf_op jit(solution)/shard_map/ppermute | solution.py:269
  60.4 16.3 %all-to-all-start.2 = ((bf16[4,144,640]{2,1,0:T(8,128)(2,1)}), bf16[4,144,640]{2,1,0:T(8,128)(2,1)S(1)}, u32[]{:S(2)}, u32[]{:S(2)}) async-start(bf16[4,144,640]{2,1,0:T(8,128)(2,1)} %get-tuple-element.33), calls=%async_computation.2 | async-start | bytes 1474560 | tf_op jit(solution)/shard_map/all_to_all | solution.py:266
  76.7 31.7 %all-to-all-start.1 = ((bf16[12,24,1024]{2,1,0:T(8,128)(2,1)}), bf16[12,24,1024]{2,1,0:T(8,128)(2,1)S(1)}, u32[]{:S(2)}, u32[]{:S(2)}) async-start(bf16[12,24,1024]{2,1,0:T(8,128)(2,1)} %bitcast.9), calls=%async_computation.1 | async-start | bytes 1179648 | tf_op jit(solution)/shard_map/all_to_all | solution.py:266

commit v5 on v4

--- a/solution.py
+++ b/solution.py
@@ -26,7 +26,7 @@
     return pltpu.with_memory_space_constraint(v, pltpu.HBM)
 
 
-def fused(kernel, outs, *args, scalars=0, flops=0, mib=8, far=(), scratch=()):
+def fused(kernel, outs, *args, scalars=0, flops=0, mib=8, far=(), scratch=(), alias=None):
     specs = [
         pl.BlockSpec(
             memory_space=pltpu.SMEM if i < scalars else pltpu.HBM if i in far else pltpu.VMEM
@@ -40,6 +40,7 @@
         in_specs=specs,
         out_specs=[pl.BlockSpec(memory_space=pltpu.VMEM)] * len(outs),
         scratch_shapes=scratch,
+        input_output_aliases=alias or {},
         compiler_params=pltpu.CompilerParams(vmem_limit_bytes=mib << 20),
         cost_estimate=pl.CostEstimate(flops=flops, bytes_accessed=nbytes, transcendentals=0),
     )(*args)
@@ -169,27 +170,61 @@
         pack_ref[xd, :, wide:] = hidden
 
 
-def backward_kernel(
-    cap, side_ref, own_ref, oth_ref, gate_ref, up_ref, wg_ref, wu_ref, wd_ref, keep_ref, give_ref
+def results(cap, hidden, gate_term, up_term, wd, wg, wu):
+    slots = hidden.shape[0]
+    out_rows = dot(hidden, wd[...]).astype(B16)
+    row_grad = (dot(gate_term, wg[...], COLS1) + dot(up_term, wu[...], COLS1)).astype(B16)
+    from_x = pick((2 * slots, slots), 1, cap, 0)
+    from_g = pick((2 * slots, slots), 1, cap, cap)
+    return (dot(from_x, out_rows) + dot(from_g, row_grad)).astype(B16)
+
+
+def give_kernel(
+    cap, side_ref, own_ref, oth_ref, gate_ref, up_ref, wg_far, wu_far, wd_far,
+    give_ref, hidden_ref, gate_term_ref, up_term_ref, wd_own, wd_oth, wg, wu, sems,
 ):
     rows, half = own_ref.shape
     slots = rows // 2
     _, here, there = halves(side_ref, half)
+    copies = fetch(
+        [
+            (wd_far.at[:, here], wd_own),
+            (wd_far.at[:, there], wd_oth),
+            (wg_far.at[there], wg),
+            (wu_far.at[there], wu),
+        ],
+        sems,
+    )
     to_g = pick((slots, rows), 0, cap, cap)
     g_own, g_oth = dot(to_g, own_ref[...]).astype(B16), dot(to_g, oth_ref[...]).astype(B16)
     gate, up = gate_ref[...], up_ref[...]
     sig = 1.0 / (1.0 + jnp.exp(-gate))
     act = gate * sig
     hidden = (act * up).astype(B16)
-    hidden_grad = dot(g_own, wd_ref[:, here], COLS1) + dot(g_oth, wd_ref[:, there], COLS1)
+    copies[0].wait()
+    copies[1].wait()
+    hidden_grad = dot(g_own, wd_own[...], COLS1) + dot(g_oth, wd_oth[...], COLS1)
     gate_term = (hidden_grad * up * sig * (1.0 + gate * (1.0 - sig))).astype(B16)
     up_term = (hidden_grad * act).astype(B16)
-    from_x = pick((rows, slots), 1, cap, 0)
-    from_g = pick((rows, slots), 1, cap, cap)
-    for part, out in ((there, give_ref), (here, keep_ref)):
-        out_rows = dot(hidden, wd_ref[:, part]).astype(B16)
-        row_grad = dot(gate_term, wg_ref[part, :], COLS1) + dot(up_term, wu_ref[part, :], COLS1)
-        out[...] = (dot(from_x, out_rows) + dot(from_g, row_grad.astype(B16))).astype(B16)
+    hidden_ref[...] = hidden
+    gate_term_ref[...] = gate_term
+    up_term_ref[...] = up_term
+    copies[2].wait()
+    copies[3].wait()
+    give_ref[...] = results(cap, hidden, gate_term, up_term, wd_oth, wg, wu)
+
+
+def keep_kernel(
+    cap, side_ref, hidden_ref, gate_term_ref, up_term_ref, wg_far, wu_far, wd_far,
+    keep_ref, wd, wg, wu, sems,
+):
+    _, here, _ = halves(side_ref, wd.shape[1])
+    copies = fetch(
+        [(wd_far.at[:, here], wd), (wg_far.at[here], wg), (wu_far.at[here], wu)], sems
+    )
+    for c in copies:
+        c.wait()
+    keep_ref[...] = results(cap, hidden_ref[...], gate_term_ref[...], up_term_ref[...], wd, wg, wu)
 
 
 def down_kernel(bit_ref, packs_ref, cols_ref, keep_ref, give_ref):
@@ -291,7 +326,7 @@
     )
     gate, up, pack = fused(
         functools.partial(rest_kernel, cap),
-        [pltpu.HBM((slots, ff), F32)] * 2 + [pltpu.HBM((NX, slots, half // NX + ff), B16)],
+        [floats, floats, pltpu.HBM((NX, slots, half // NX + ff), B16)],
         side,
         oth,
         gate,
@@ -304,24 +339,40 @@
         mib=12,
         far=(6,),
         scratch=halfway,
+        alias={2: 0, 3: 1},
     )
     packs = trade(pack, "x", *pack.shape)
-    keep, give = fused(
-        functools.partial(backward_kernel, cap),
-        [bf(2 * slots, half)] * 2,
+    weights = [hbm(w[0]) for w in (gate_weight, up_weight, down_weight)]
+    down_half, in_half = bf(ff, half), bf(half, ff)
+    give, *terms = fused(
+        functools.partial(give_kernel, cap),
+        [bf(2 * slots, half)] + [bf(slots, ff)] * 3,
         side,
         own,
         oth,
         gate,
         up,
-        hbm(gate_weight[0]),
-        hbm(up_weight[0]),
-        hbm(down_weight[0]),
-        scalars=1,
-        flops=slots * half * 2 * ff * 8 + slots * 2 * slots * half * 12,
-        mib=24,
-    )
-    total = (keep.astype(F32) + swap(give).astype(F32)).astype(B16)
+        *weights,
+        scalars=1,
+        flops=slots * half * 2 * ff * 5 + slots * 2 * slots * half * 8,
+        mib=16,
+        far=(5, 6, 7),
+        scratch=landing(down_half, down_half, in_half, in_half),
+    )
+    got = swap(give)
+    (keep,) = fused(
+        functools.partial(keep_kernel, cap),
+        [bf(2 * slots, half)],
+        side,
+        *terms,
+        *weights,
+        scalars=1,
+        flops=slots * half * 2 * ff * 3 + slots * 2 * slots * half * 4,
+        mib=12,
+        far=(4, 5, 6),
+        scratch=landing(down_half, in_half, in_half),
+    )
+    total = (keep.astype(F32) + got.astype(F32)).astype(B16)
     back = trade(total, "expert", *chunks).reshape(2 * slots, half)
     keep, give = fused(
         down_kernel,

time: 110 us -> 107 us (0.973)
  waiting for transfers between devices: 10.9 us -> 8.05 us
  local copies, waits for them, and re-layouts: 1.89 us -> 0.03 us
  Pallas kernels: 14.8 us -> 16.1 us
    all_to_all x2, waiting for transfers between devices: 10.9 us -> 8.04 us  [trade(): lax.all_to_all(rows.reshape(shape), axis, split_axis=0, concat_axis=0, ti...]
    unnamed x6 -> x2, local copies, waits for them, and re-layouts: 1.87 us -> 0.01 us
    pallas_call x9 -> x10, Pallas kernels: 14.8 us -> 16.1 us  [fused(): pl.pallas_call(kernel, out_shape=outs, in_specs=specs, out_specs=[pl.Bloc...]
  transfers between devices with their start and end apart: 4 -> 4, of which waited for: 1 -> 1; matrix products, arithmetic and copies ran while one was open for 1% -> 1% of each run, Pallas kernels for 4% -> 6%
where the time goes in v5:
time: 107 us; the launch traced here: 106 us
  blocking collectives  68 us (64%)
  Pallas kernels  16.1 us (15%)
  starting transfers between devices  12.2 us (11%)
  waiting for transfers between devices  8.05 us (8%)
  other arithmetic  1.07 us (1%)
    all_to_all x1, blocking collectives, trade(): lax.all_to_all(rows.reshape(shape), axis, split_axis=0, concat_axis=0, ti...  41.8 us
    all_gather x4, blocking collectives, pair(): return lax.all_gather(v, axis, axis=1, tiled=True)  26.2 us
    pallas_call x10, Pallas kernels, fused(): pl.pallas_call(kernel, out_shape=outs, in_specs=specs, out_specs=[pl.Bloc...  16.1 us
    all_to_all x2, waiting for transfers between devices, trade(): lax.all_to_all(rows.reshape(shape), axis, split_axis=0, concat_axis=0, ti...  8.04 us
    all_to_all x2, starting transfers between devices, trade(): lax.all_to_all(rows.reshape(shape), axis, split_axis=0, concat_axis=0, ti...  7.92 us
    ppermute x2, starting transfers between devices, swap(): return lax.ppermute(v, 'tensor', [(0, 1), (1, 0)])  4.31 us
  transfers between devices with their start and end apart: 4, of which 1 were waited for; matrix products, arithmetic and copies ran while one was open for 1% of the time, Pallas kernels for 6%

profile of v5, /device:TPU:32, one launch (start us, length us, event | category | flops | bytes accessed | tf_op | source)
XLA Modules:
  0.0 106.2 jit_solution(17035047343974154831)
XLA Ops:
  0.6 0.0 copy-start
  0.6 1.7 %shard_map.95 = bf16[288,1024]{1,0:T(8,128)(2,1)S(1)} custom-call(s32[8,128]{1,0:T(8,128)} %bitcast.31, f32[8,128]{1,0:T(8,128)} %bitcast.33, bf16[128,1024]{1,0:T(8,128)(2,1)} %refs_2_.1, bf16[128,1024]{1,0:T(8,128)(2,1)} %refs_3_.1), custom_call_target="tpu_custom_call" | custom-call | flops 150994944 | bytes 1122304 | tf_op jit(solution)/shard_map/pallas_call | solution.py:37
  2.3 41.8 %all_to_all.15 = bf16[12,24,1024]{2,1,0:T(8,128)(2,1)S(1)} all-to-all(bf16[12,24,1024]{2,1,0:T(8,128)(2,1)S(1)} %bitcast.24), channel_id=1, replica_groups=mesh['y4'=2,'y2'=2,'y1'=2,'x'=4,'expert'=12,'tensor'=2] {'expert'}, dimensions={0} | all-to-all | bytes 1179648 | tf_op jit(solution)/shard_map/all_to_all | solution.py:301
  44.2 1.9 %collective-permute-start = (bf16[288,1024]{1,0:T(8,128)(2,1)S(1)}, bf16[288,1024]{1,0:T(8,128)(2,1)S(1)}, u32[]{:S(2)}, u32[]{:S(2)}) collective-permute-start(bf16[288,1024]{1,0:T(8,128)(2,1)S(1)} %bitcast.20), channel_id=1, source_target_pairs={{0,1},{1,0},{2,3},{3,2},{4,5},{5,4},{6,7},{7,6},{8,9},{9,8},{10,11... | collective-permute-start | bytes 1769480 | tf_op jit(solution)/shard_map/ppermute | solution.py:304
  46.1 2.0 %shard_map.96 = (f32[144,384]{1,0:T(8,128)S(1)}, f32[144,384]{1,0:T(8,128)S(1)}, bf16[4,144,256]{2,1,0:T(8,128)(2,1)S(1)}) custom-call(s32[1]{0:T(128)} %bitcast.3.side_ref, bf16[288,1024]{1,0:T(8,128)(2,1)S(1)} %bitcast.21, bf16[2048,384]{1,0:T(8,128)(2,1)S(1)} %bitcast.18, bf16[2048,384]{1,0:T(8,128)(2,1)} %bitcast.25), custom_call_target="tpu_custom_call" | custom-call | flops 396361728 | bytes 4472836 | tf_op jit(solution)/shard_map/pallas_call | solution.py:37
  48.1 0.0 collective-permute-done.oth_ref
  48.1 2.7 %shard_map.97 = (f32[144,384]{1,0:T(8,128)S(1)}, f32[144,384]{1,0:T(8,128)S(1)}, bf16[4,144,640]{2,1,0:T(8,128)(2,1)}) custom-call(s32[1]{0:T(128)} %bitcast.3.side_ref, bf16[288,1024]{1,0:T(8,128)(2,1)S(1)} %collective-permute-done.oth_ref, f32[144,384]{1,0:T(8,128)S(1)} %get-tuple-element.28.gate_in, ...), custom_call_target="tpu_custom_call", output_to_operand_aliasing={{0}: (2, {}), {1}: (3, {})} | custom-call | flops 311427072 | bytes 5652484 | tf_op jit(solution)/shard_map/pallas_call | solution.py:37
  50.9 3.7 %shard_map.98 = (bf16[288,1024]{1,0:T(8,128)(2,1)S(1)}, bf16[144,384]{1,0:T(8,128)(2,1)S(1)}, bf16[144,384]{1,0:T(8,128)(2,1)S(1)}, bf16[144,384]{1,0:T(8,128)(2,1)S(1)}) custom-call(s32[1]{0:T(128)} %bitcast.3.side_ref, bf16[288,1024]{1,0:T(8,128)(2,1)S(1)} %bitcast.22, bf16[288,1024]{1,0:T(8,128)(2,1)S(1)} %collective-permute-done.oth_ref, ...), custom_call_target="tpu_custom_call" | custom-call | flops 905969664 | bytes 7262212 | tf_op jit(solution)/shard_map/pallas_call | solution.py:37
  54.6 2.4 %collective-permute-start.1 = (bf16[288,1024]{1,0:T(8,128)(2,1)S(1)}, bf16[288,1024]{1,0:T(8,128)(2,1)S(1)}, u32[]{:S(2)}, u32[]{:S(2)}) collective-permute-start(bf16[288,1024]{1,0:T(8,128)(2,1)S(1)} %get-tuple-element.36), channel_id=1, source_target_pairs={{0,1},{1,0},{2,3},{3,2},{4,5},{5,4},{6,7},{7,6},{8,9},{9,8},{10,11... | collective-permute-start | bytes 1769480 | tf_op jit(solution)/shard_map/ppermute | solution.py:304
  57.0 4.3 %all-to-all-start.2 = ((bf16[4,144,640]{2,1,0:T(8,128)(2,1)}), bf16[4,144,640]{2,1,0:T(8,128)(2,1)S(1)}, u32[]{:S(2)}, u32[]{:S(2)}) async-start(bf16[4,144,640]{2,1,0:T(8,128)(2,1)} %get-tuple-element.37), calls=%async_computation.2 | async-start | bytes 1474560 | tf_op jit(solution)/shard_map/all_to_all | solution.py:301
  61.3 2.8 %shard_map.99 = bf16[288,1024]{1,0:T(8,128)(2,1)S(1)} custom-call(s32[1]{0:T(128)} %bitcast.3.side_ref, bf16[144,384]{1,0:T(8,128)(2,1)S(1)} %get-tuple-element.33.hidden_ref, bf16[144,384]{1,0:T(8,128)(2,1)S(1)} %get-tuple-element.34.gate_term_ref, bf16[144,384]{1,0:T(8,128)(2,1)S(1)} %get-tuple-element.35.up_term_ref, bf16[2048,384]{1,0:T(8,128)(2,1)} %bitcast.17, ...), custom_call_target="tpu_custom_call" | custom-call | flops 509607936 | bytes 5640196 | tf_op jit(solution)/shard_map/pallas_call | solution.py:37
  64.1 0.0 collective-permute-done.1
  64.2 1.1 %add_convert_fusion = bf16[288,1024]{1,0:T(8,128)(2,1)} fusion(bf16[288,1024]{1,0:T(8,128)(2,1)S(1)} %collective-permute-done.1, bf16[288,1024]{1,0:T(8,128)(2,1)S(1)} %shard_map.99), kind=kLoop, calls=%fused_computation | loop fusion | flops 1179648 | bytes 1769472 | tf_op jit(solution)/shard_map/convert_element_type | solution.py:375
  65.2 8.0 %all-to-all-done.2.packs_ref = bf16[4,144,640]{2,1,0:T(8,128)(2,1)S(1)} async-done(((bf16[4,144,640]{2,1,0:T(8,128)(2,1)}), bf16[4,144,640]{2,1,0:T(8,128)(2,1)S(1)}, u32[]{:S(2)}, u32[]{:S(2)}) %all-to-all-start.2) | async-done | bytes 737312 | tf_op jit(solution)/shard_map/all_to_all | solution.py:301
  73.3 3.6 %all-to-all-start.1 = ((bf16[12,24,1024]{2,1,0:T(8,128)(2,1)}), bf16[12,24,1024]{2,1,0:T(8,128)(2,1)S(1)}, u32[]{:S(2)}, u32[]{:S(2)}) async-start(bf16[12,24,1024]{2,1,0:T(8,128)(2,1)} %bitcast.9), calls=%async_computation.1 | async-start | bytes 1179648 | tf_op jit(solution)/shard_map/all_to_all | solution.py:301
  76.9 1.0 shard_map.94
  77.9 2.2 %all_gather.12.cols_ref = bf16[4,288,256]{2,1,0:T(8,128)(2,1)S(1)} all-gather(bf16[4,144,256]{2,1,0:T(8,128)(2,1)S(1)} %slice.4), channel_id=1, replica_groups=mesh['y4'=2,'y2'=2,'y1'=2,'x'=4,'expert'=12,'tensor'=2] {'tensor'}, dimensions={1}, use_global_device_ids=true | all-gather | bytes 884736 | tf_op jit(solution)/shard_map/all_gather | solution.py:307
  80.2 0.8 shard_map.100
  80.9 7.6 %all_gather.13.pair_ref = bf16[2,256,384]{2,1,0:T(8,128)(2,1)S(1)} all-gather(bf16[2,128,384]{2,1,0:T(8,128)(2,1)S(1)} %get-tuple-element.39), channel_id=1, replica_groups=mesh['y4'=2,'y2'=2,'y1'=2,'x'=4,'expert'=12,'tensor'=2] {'y1'}, dimensions={1}, use_global_device_ids=true | all-gather | bytes 589824 | tf_op jit(solution)/shard_map/all_gather | solution.py:307
  88.6 0.1 shard_map.101
  88.6 7.6 %all_gather.14.pair_ref = bf16[2,128,384]{2,1,0:T(8,128)(2,1)S(1)} all-gather(bf16[2,64,384]{2,1,0:T(8,128)(2,1)S(1)} %get-tuple-element.41), channel_id=1, replica_groups=mesh['y4'=2,'y2'=2,'y1'=2,'x'=4,'expert'=12,'tensor'=2] {'y2'}, dimensions={1}, use_global_device_ids=true | all-gather | bytes 294912 | tf_op jit(solution)/shard_map/all_gather | solution.py:307
  96.3 8.7 %all_gather.15.pair_ref = bf16[2,64,384]{2,1,0:T(8,128)(2,1)S(1)} all-gather(bf16[2,32,384]{2,1,0:T(8,128)(2,1)S(1)} %get-tuple-element.43), channel_id=1, replica_groups=mesh['y4'=2,'y2'=2,'y1'=2,'x'=4,'expert'=12,'tensor'=2] {'y4'}, dimensions={1}, use_global_device_ids=true | all-gather | bytes 147456 | tf_op jit(solution)/shard_map/all_gather | solution.py:307
  104.9 0.0 all-to-all-done.1
  105.0 1.3 %shard_map.103 = (bf16[128,1024]{1,0:T(8,128)(2,1)}, bf16[128,1024]{1,0:T(8,128)(2,1)}, bf16[64,384]{1,0:T(8,128)(2,1)}) custom-call(s32[1]{0:T(128)} %bitcast.bit_ref, bf16[128,288]{1,0:T(8,128)(2,1)S(1)} %get-tuple-element.25.high_ref, bf16[128,288]{1,0:T(8,128)(2,1)S(1)} %get-tuple-element.26.low_ref, bf16[128,288]{1,0:T(8,128)(2,1)S(1)} %get-tuple-element.27.right_ref, ...), custom_call_target="tpu_custom_call" | custom-call | flops 226492416 | bytes 1531908 | tf_op jit(solution)/shard_map/pallas_call | solution.py:37
  (3 shorter events, 0.1 us)
Async XLA Ops:
  0.6 45.5 %copy-start = (bf16[1,2048,384]{2,1,0:T(8,128)(2,1)S(1)}, bf16[1,2048,384]{2,1,0:T(8,128)(2,1)}, u32[]{:S(2)}) copy-start(bf16[1,2048,384]{2,1,0:T(8,128)(2,1)} %param.10) | copy-start | bytes 4718596
  44.2 4.0 %collective-permute-start = (bf16[288,1024]{1,0:T(8,128)(2,1)S(1)}, bf16[288,1024]{1,0:T(8,128)(2,1)S(1)}, u32[]{:S(2)}, u32[]{:S(2)}) collective-permute-start(bf16[288,1024]{1,0:T(8,128)(2,1)S(1)} %bitcast.20), channel_id=1, source_target_pairs={{0,1},{1,0},{2,3},{3,2},{4,5},{5,4},{6,7},{7,6},{8,9},{9,8},{10,11... | collective-permute-start | bytes 1769480 | tf_op jit(solution)/shard_map/ppermute | solution.py:304
  54.6 9.5 %collective-permute-start.1 = (bf16[288,1024]{1,0:T(8,128)(2,1)S(1)}, bf16[288,1024]{1,0:T(8,128)(2,1)S(1)}, u32[]{:S(2)}, u32[]{:S(2)}) collective-permute-start(bf16[288,1024]{1,0:T(8,128)(2,1)S(1)} %get-tuple-element.36), channel_id=1, source_target_pairs={{0,1},{1,0},{2,3},{3,2},{4,5},{5,4},{6,7},{7,6},{8,9},{9,8},{10,11... | collective-permute-start | bytes 1769480 | tf_op jit(solution)/shard_map/ppermute | solution.py:304
  57.0 16.3 %all-to-all-start.2 = ((bf16[4,144,640]{2,1,0:T(8,128)(2,1)}), bf16[4,144,640]{2,1,0:T(8,128)(2,1)S(1)}, u32[]{:S(2)}, u32[]{:S(2)}) async-start(bf16[4,144,640]{2,1,0:T(8,128)(2,1)} %get-tuple-element.37), calls=%async_computation.2 | async-start | bytes 1474560 | tf_op jit(solution)/shard_map/all_to_all | solution.py:301
  73.3 31.7 %all-to-all-start.1 = ((bf16[12,24,1024]{2,1,0:T(8,128)(2,1)}), bf16[12,24,1024]{2,1,0:T(8,128)(2,1)S(1)}, u32[]{:S(2)}, u32[]{:S(2)}) async-start(bf16[12,24,1024]{2,1,0:T(8,128)(2,1)} %bitcast.9), calls=%async_computation.1 | async-start | bytes 1179648 | tf_op jit(solution)/shard_map/all_to_all | solution.py:301

commit v6 on v5

--- a/solution.py
+++ b/solution.py
@@ -140,11 +140,10 @@
     own = own_ref[...]
     x = dot(pick((slots, rows), 0, cap, 0), own).astype(B16)
     g = dot(pick((slots, rows), 0, cap, cap), own).astype(B16)
-    wide = half // NX
-    for xd in range(NX):
-        cols = [g[:, (y * NX + xd) * 64 : (y * NX + xd) * 64 + 64] for y in range(wide // 64)]
-        cols_ref[xd, :, 0 : wide // 2] = jnp.concatenate(cols[0::2], axis=1)
-        cols_ref[xd, :, wide // 2 : wide] = jnp.concatenate(cols[1::2], axis=1)
+    wide = cols_ref.shape[2]
+    for way in range(2 * NX):
+        starts = [(y * NX + way % NX) * 64 for y in range(way // NX, wide // 32, 2)]
+        cols_ref[way] = jnp.concatenate([g[:, at : at + 64] for at in starts], axis=1)
     gate_ref[...] = dot(x, wg_ref[here, :])
     copies[0].wait()
     up_ref[...] = dot(x, wu[...])
@@ -166,8 +165,8 @@
     hidden = (gate * (1.0 / (1.0 + jnp.exp(-gate))) * up).astype(B16)
     gate_ref[...] = gate
     up_ref[...] = up
-    for xd in range(NX):
-        pack_ref[xd, :, wide:] = hidden
+    for way in range(2 * NX):
+        pack_ref[way, :, wide:] = hidden
 
 
 def results(cap, hidden, gate_term, up_term, wd, wg, wu):
@@ -227,34 +226,25 @@
     keep_ref[...] = results(cap, hidden_ref[...], gate_term_ref[...], up_term_ref[...], wd, wg, wu)
 
 
-def down_kernel(bit_ref, packs_ref, cols_ref, keep_ref, give_ref):
+def down_kernel(bit_ref, packs_ref, cols_ref, keep_ref, give_ref, sum_ref):
     n = keep_ref.shape[1]
     slots = packs_ref.shape[1]
     wide = cols_ref.shape[2]
     bit = bit_ref[0]
-    for at, out in ((1 - bit, give_ref), (bit, keep_ref)):
-        cols = pl.ds(pl.multiple_of(at * n, n), n)
-        for h in range(2):
-            total = None
-            for k in range(NX):
-                rows = cols_ref[k, h * slots : (h + 1) * slots, cols]
-                part = dot(rows, packs_ref[k, :, wide:], ROWS0)
-                total = part if total is None else total + part
-            out[h] = total.astype(B16)
+    for h in range(2):
+        total = None
+        for k in range(2 * NX):
+            rows = cols_ref[k, h * slots : (h + 1) * slots, :]
+            part = dot(rows, packs_ref[k, :, wide:], ROWS0)
+            total = part if total is None else total + part
+        sum_ref[...] = total
+        give_ref[h] = sum_ref[pl.ds(pl.multiple_of((1 - bit) * n, n), n), :].astype(B16)
+        keep_ref[h] = sum_ref[pl.ds(pl.multiple_of(bit * n, n), n), :].astype(B16)
 
 
 def partner(bit_ref, pair_ref, h, at, n):
     start = (1 - bit_ref[0]) * (pair_ref.shape[1] // 2) + at
     return pair_ref[h, pl.ds(pl.multiple_of(start, n), n), :].astype(F32)
-
-
-def halve_rows_kernel(last_ref, bit_ref, mine_ref, pair_ref, keep_ref, give_ref):
-    n = keep_ref.shape[1]
-    bit = bit_ref[0]
-    for side, out in ((1 - bit, give_ref), (bit, keep_ref)):
-        for h in range(2):
-            mine = mine_ref[h, pl.ds(pl.multiple_of(side * n, n), n), :].astype(F32)
-            out[h] = (mine + partner(last_ref, pair_ref, h, side * n, n)).astype(B16)
 
 
 def halve_sides_kernel(last_ref, bit_ref, mine_ref, pair_ref, keep_ref, give_ref):
@@ -313,7 +303,7 @@
     halfway = landing(bf(half, ff))
     gate, up, cols = fused(
         functools.partial(own_kernel, cap),
-        [floats, floats, bf(NX, slots, half // NX)],
+        [floats, floats, bf(2 * NX, slots, half // (2 * NX))],
         side,
         own,
         gate_weight[0],
@@ -326,7 +316,7 @@
     )
     gate, up, pack = fused(
         functools.partial(rest_kernel, cap),
-        [floats, floats, pltpu.HBM((NX, slots, half // NX + ff), B16)],
+        [floats, floats, pltpu.HBM((2 * NX, slots, half // (2 * NX) + ff), B16)],
         side,
         oth,
         gate,
@@ -341,7 +331,7 @@
         scratch=halfway,
         alias={2: 0, 3: 1},
     )
-    packs = trade(pack, "x", *pack.shape)
+    packs = trade(pack, ("y1", "x"), *pack.shape)
     weights = [hbm(w[0]) for w in (gate_weight, up_weight, down_weight)]
     down_half, in_half = bf(ff, half), bf(half, ff)
     give, *terms = fused(
@@ -376,23 +366,23 @@
     back = trade(total, "expert", *chunks).reshape(2 * slots, half)
     keep, give = fused(
         down_kernel,
-        [bf(2, half // 8, ff)] * 2,
-        bits[0],
+        [bf(2, half // 16, ff)] * 2,
+        bits[1],
         packs,
-        pair(packs[:, :, : half // NX], "tensor"),
-        scalars=1,
-        flops=half // 2 * ff * slots * 2 * NX,
-    )
-    for step, kernel in ((1, halve_rows_kernel), (2, halve_sides_kernel)):
-        keep, give = fused(
-            kernel,
-            [bf(2, keep.shape[1] // 2, ff)] * 2,
-            bits[step - 1],
-            bits[step],
-            keep,
-            pair(give, ("y1", "y2")[step - 1]),
-            scalars=2,
-        )
+        pair(packs[:, :, : half // (2 * NX)], "tensor"),
+        scalars=1,
+        flops=half // 4 * ff * slots * 4 * NX,
+        scratch=[pltpu.VMEM((half // 8, ff), F32)],
+    )
+    keep, give = fused(
+        halve_sides_kernel,
+        [bf(2, half // 32, ff)] * 2,
+        bits[1],
+        bits[2],
+        keep,
+        pair(give, "y2"),
+        scalars=2,
+    )
     mixed, token_grad, down_grad = fused(
         combine_kernel,
         [bf(tok_rows, half)] * 2 + [bf(half // 16, ff)],

time: 107 us -> 106 us (level)
  the two profiles are of different devices: /device:TPU:32 before, /device:TPU:16 now
where the time goes in v6:
time: 106 us
  blocking collectives  59.8 us (56%)
  Pallas kernels  16.2 us (15%)
  waiting for transfers between devices  15 us (14%)
  starting transfers between devices  13 us (12%)
  other arithmetic  1.06 us (1%)
    all_to_all x1, blocking collectives, trade(): lax.all_to_all(rows.reshape(shape), axis, split_axis=0, concat_axis=0, ti...  41.8 us
    all_gather x3, blocking collectives, pair(): return lax.all_gather(v, axis, axis=1, tiled=True)  17.9 us
    pallas_call x9, Pallas kernels, fused(): pl.pallas_call(kernel, out_shape=outs, in_specs=specs, out_specs=[pl.Bloc...  16.2 us
    all_to_all x2, waiting for transfers between devices, trade(): lax.all_to_all(rows.reshape(shape), axis, split_axis=0, concat_axis=0, ti...  14.9 us
    all_to_all x2, starting transfers between devices, trade(): lax.all_to_all(rows.reshape(shape), axis, split_axis=0, concat_axis=0, ti...  8.95 us
    ppermute x2, starting transfers between devices, swap(): return lax.ppermute(v, 'tensor', [(0, 1), (1, 0)])  4.03 us
  transfers between devices with their start and end apart: 4, of which 2 were waited for; matrix products, arithmetic and copies ran while one was open for 1% of the time, Pallas kernels for 10%

profile of v6, /device:TPU:16, one launch (start us, length us, event | category | flops | bytes accessed | tf_op | source)
XLA Modules:
  0.0 105.8 jit_solution(13539817472416969270)
XLA Ops:
  0.6 0.0 copy-start
  0.6 1.7 %shard_map.95 = bf16[288,1024]{1,0:T(8,128)(2,1)S(1)} custom-call(s32[8,128]{1,0:T(8,128)} %bitcast.30, f32[8,128]{1,0:T(8,128)} %bitcast.32, bf16[128,1024]{1,0:T(8,128)(2,1)} %refs_2_.1, bf16[128,1024]{1,0:T(8,128)(2,1)} %refs_3_.1), custom_call_target="tpu_custom_call" | custom-call | flops 150994944 | bytes 1122304 | tf_op jit(solution)/shard_map/pallas_call | solution.py:37
  2.3 41.8 %all_to_all.15 = bf16[12,24,1024]{2,1,0:T(8,128)(2,1)S(1)} all-to-all(bf16[12,24,1024]{2,1,0:T(8,128)(2,1)S(1)} %bitcast.23), channel_id=1, replica_groups=mesh['y4'=2,'y2'=2,'y1'=2,'x'=4,'expert'=12,'tensor'=2] {'expert'}, dimensions={0} | all-to-all | bytes 1179648 | tf_op jit(solution)/shard_map/all_to_all | solution.py:291
  44.2 1.9 %collective-permute-start = (bf16[288,1024]{1,0:T(8,128)(2,1)S(1)}, bf16[288,1024]{1,0:T(8,128)(2,1)S(1)}, u32[]{:S(2)}, u32[]{:S(2)}) collective-permute-start(bf16[288,1024]{1,0:T(8,128)(2,1)S(1)} %bitcast.19), channel_id=1, source_target_pairs={{0,1},{1,0},{2,3},{3,2},{4,5},{5,4},{6,7},{7,6},{8,9},{9,8},{10,11... | collective-permute-start | bytes 1769480 | tf_op jit(solution)/shard_map/ppermute | solution.py:294
  46.1 0.0 copy-done
  46.1 2.0 %shard_map.96 = (f32[144,384]{1,0:T(8,128)S(1)}, f32[144,384]{1,0:T(8,128)S(1)}, bf16[8,144,128]{2,1,0:T(8,128)(2,1)S(1)}) custom-call(s32[1]{0:T(128)} %bitcast.3.side_ref, bf16[288,1024]{1,0:T(8,128)(2,1)S(1)} %bitcast.20, bf16[2048,384]{1,0:T(8,128)(2,1)S(1)} %bitcast.17, bf16[2048,384]{1,0:T(8,128)(2,1)} %bitcast.24), custom_call_target="tpu_custom_call" | custom-call | flops 396361728 | bytes 4472836 | tf_op jit(solution)/shard_map/pallas_call | solution.py:37
  48.1 0.0 collective-permute-done.oth_ref
  48.1 2.9 %shard_map.97 = (f32[144,384]{1,0:T(8,128)S(1)}, f32[144,384]{1,0:T(8,128)S(1)}, bf16[8,144,512]{2,1,0:T(8,128)(2,1)}) custom-call(s32[1]{0:T(128)} %bitcast.3.side_ref, bf16[288,1024]{1,0:T(8,128)(2,1)S(1)} %collective-permute-done.oth_ref, f32[144,384]{1,0:T(8,128)S(1)} %get-tuple-element.26.gate_in, ...), custom_call_target="tpu_custom_call", output_to_operand_aliasing={{0}: (2, {}), {1}: (3, {})} | custom-call | flops 311427072 | bytes 6094852 | tf_op jit(solution)/shard_map/pallas_call | solution.py:37
  51.0 5.3 %all-to-all-start.2 = ((bf16[8,144,512]{2,1,0:T(8,128)(2,1)}), bf16[8,144,512]{2,1,0:T(8,128)(2,1)S(1)}, u32[]{:S(2)}, u32[]{:S(2)}) async-start(bf16[8,144,512]{2,1,0:T(8,128)(2,1)} %get-tuple-element.35), calls=%async_computation.2 | async-start | bytes 2359296 | tf_op jit(solution)/shard_map/all_to_all | solution.py:291
  56.4 3.7 %shard_map.98 = (bf16[288,1024]{1,0:T(8,128)(2,1)S(1)}, bf16[144,384]{1,0:T(8,128)(2,1)S(1)}, bf16[144,384]{1,0:T(8,128)(2,1)S(1)}, bf16[144,384]{1,0:T(8,128)(2,1)S(1)}) custom-call(s32[1]{0:T(128)} %bitcast.3.side_ref, bf16[288,1024]{1,0:T(8,128)(2,1)S(1)} %bitcast.21, bf16[288,1024]{1,0:T(8,128)(2,1)S(1)} %collective-permute-done.oth_ref, ...), custom_call_target="tpu_custom_call" | custom-call | flops 905969664 | bytes 7262212 | tf_op jit(solution)/shard_map/pallas_call | solution.py:37
  60.1 2.1 %collective-permute-start.1 = (bf16[288,1024]{1,0:T(8,128)(2,1)S(1)}, bf16[288,1024]{1,0:T(8,128)(2,1)S(1)}, u32[]{:S(2)}, u32[]{:S(2)}) collective-permute-start(bf16[288,1024]{1,0:T(8,128)(2,1)S(1)} %get-tuple-element.34), channel_id=1, source_target_pairs={{0,1},{1,0},{2,3},{3,2},{4,5},{5,4},{6,7},{7,6},{8,9},{9,8},{10,11... | collective-permute-start | bytes 1769480 | tf_op jit(solution)/shard_map/ppermute | solution.py:294
  62.2 2.8 %shard_map.99 = bf16[288,1024]{1,0:T(8,128)(2,1)S(1)} custom-call(s32[1]{0:T(128)} %bitcast.3.side_ref, bf16[144,384]{1,0:T(8,128)(2,1)S(1)} %get-tuple-element.31.hidden_ref, bf16[144,384]{1,0:T(8,128)(2,1)S(1)} %get-tuple-element.32.gate_term_ref, bf16[144,384]{1,0:T(8,128)(2,1)S(1)} %get-tuple-element.33.up_term_ref, bf16[2048,384]{1,0:T(8,128)(2,1)} %bitcast.16, ...), custom_call_target="tpu_custom_call" | custom-call | flops 509607936 | bytes 5640196 | tf_op jit(solution)/shard_map/pallas_call | solution.py:37
  65.1 0.0 collective-permute-done.1
  65.1 1.1 %add_convert_fusion = bf16[288,1024]{1,0:T(8,128)(2,1)} fusion(bf16[288,1024]{1,0:T(8,128)(2,1)S(1)} %collective-permute-done.1, bf16[288,1024]{1,0:T(8,128)(2,1)S(1)} %shard_map.99), kind=kLoop, calls=%fused_computation | loop fusion | flops 1179648 | bytes 1769472 | tf_op jit(solution)/shard_map/convert_element_type | solution.py:365
  66.1 7.1 %all-to-all-done.2.packs_ref = bf16[8,144,512]{2,1,0:T(8,128)(2,1)S(1)} async-done(((bf16[8,144,512]{2,1,0:T(8,128)(2,1)}), bf16[8,144,512]{2,1,0:T(8,128)(2,1)S(1)}, u32[]{:S(2)}, u32[]{:S(2)}) %all-to-all-start.2) | async-done | bytes 1179680 | tf_op jit(solution)/shard_map/all_to_all | solution.py:291
  73.2 3.6 %all-to-all-start.1 = ((bf16[12,24,1024]{2,1,0:T(8,128)(2,1)}), bf16[12,24,1024]{2,1,0:T(8,128)(2,1)S(1)}, u32[]{:S(2)}, u32[]{:S(2)}) async-start(bf16[12,24,1024]{2,1,0:T(8,128)(2,1)} %bitcast.9), calls=%async_computation.1 | async-start | bytes 1179648 | tf_op jit(solution)/shard_map/all_to_all | solution.py:291
  76.9 1.0 shard_map.94
  77.9 0.1 slice.4
  77.9 2.2 %all_gather.9.cols_ref = bf16[8,288,128]{2,1,0:T(8,128)(2,1)S(1)} all-gather(bf16[8,144,128]{2,1,0:T(8,128)(2,1)S(1)} %slice.4), channel_id=1, replica_groups=mesh['y4'=2,'y2'=2,'y1'=2,'x'=4,'expert'=12,'tensor'=2] {'tensor'}, dimensions={1}, use_global_device_ids=true | all-gather | bytes 884736 | tf_op jit(solution)/shard_map/all_gather | solution.py:297
  80.2 0.8 shard_map.100
  80.9 6.5 %all_gather.10.pair_ref = bf16[2,128,384]{2,1,0:T(8,128)(2,1)S(1)} all-gather(bf16[2,64,384]{2,1,0:T(8,128)(2,1)S(1)} %get-tuple-element.37), channel_id=1, replica_groups=mesh['y4'=2,'y2'=2,'y1'=2,'x'=4,'expert'=12,'tensor'=2] {'y2'}, dimensions={1}, use_global_device_ids=true | all-gather | bytes 294912 | tf_op jit(solution)/shard_map/all_gather | solution.py:297
  87.5 9.2 %all_gather.11.pair_ref = bf16[2,64,384]{2,1,0:T(8,128)(2,1)S(1)} all-gather(bf16[2,32,384]{2,1,0:T(8,128)(2,1)S(1)} %get-tuple-element.39), channel_id=1, replica_groups=mesh['y4'=2,'y2'=2,'y1'=2,'x'=4,'expert'=12,'tensor'=2] {'y4'}, dimensions={1}, use_global_device_ids=true | all-gather | bytes 147456 | tf_op jit(solution)/shard_map/all_gather | solution.py:297
  96.7 7.8 %all-to-all-done.1 = bf16[12,24,1024]{2,1,0:T(8,128)(2,1)S(1)} async-done(((bf16[12,24,1024]{2,1,0:T(8,128)(2,1)}), bf16[12,24,1024]{2,1,0:T(8,128)(2,1)S(1)}, u32[]{:S(2)}, u32[]{:S(2)}) %all-to-all-start.1) | async-done | bytes 589856 | tf_op jit(solution)/shard_map/all_to_all | solution.py:291
  104.5 1.3 %shard_map.102 = (bf16[128,1024]{1,0:T(8,128)(2,1)}, bf16[128,1024]{1,0:T(8,128)(2,1)}, bf16[64,384]{1,0:T(8,128)(2,1)}) custom-call(s32[1]{0:T(128)} %bitcast.bit_ref, bf16[128,288]{1,0:T(8,128)(2,1)S(1)} %get-tuple-element.23.high_ref, bf16[128,288]{1,0:T(8,128)(2,1)S(1)} %get-tuple-element.24.low_ref, bf16[128,288]{1,0:T(8,128)(2,1)S(1)} %get-tuple-element.25.right_ref, ...), custom_call_target="tpu_custom_call" | custom-call | flops 226492416 | bytes 1531908 | tf_op jit(solution)/shard_map/pallas_call | solution.py:37
  (1 shorter events, 0.0 us)
Async XLA Ops:
  0.6 45.5 %copy-start = (bf16[1,2048,384]{2,1,0:T(8,128)(2,1)S(1)}, bf16[1,2048,384]{2,1,0:T(8,128)(2,1)}, u32[]{:S(2)}) copy-start(bf16[1,2048,384]{2,1,0:T(8,128)(2,1)} %param.10) | copy-start | bytes 4718596
  44.2 4.0 %collective-permute-start = (bf16[288,1024]{1,0:T(8,128)(2,1)S(1)}, bf16[288,1024]{1,0:T(8,128)(2,1)S(1)}, u32[]{:S(2)}, u32[]{:S(2)}) collective-permute-start(bf16[288,1024]{1,0:T(8,128)(2,1)S(1)} %bitcast.19), channel_id=1, source_target_pairs={{0,1},{1,0},{2,3},{3,2},{4,5},{5,4},{6,7},{7,6},{8,9},{9,8},{10,11... | collective-permute-start | bytes 1769480 | tf_op jit(solution)/shard_map/ppermute | solution.py:294
  51.0 22.2 %all-to-all-start.2 = ((bf16[8,144,512]{2,1,0:T(8,128)(2,1)}), bf16[8,144,512]{2,1,0:T(8,128)(2,1)S(1)}, u32[]{:S(2)}, u32[]{:S(2)}) async-start(bf16[8,144,512]{2,1,0:T(8,128)(2,1)} %get-tuple-element.35), calls=%async_computation.2 | async-start | bytes 2359296 | tf_op jit(solution)/shard_map/all_to_all | solution.py:291
  60.1 4.9 %collective-permute-start.1 = (bf16[288,1024]{1,0:T(8,128)(2,1)S(1)}, bf16[288,1024]{1,0:T(8,128)(2,1)S(1)}, u32[]{:S(2)}, u32[]{:S(2)}) collective-permute-start(bf16[288,1024]{1,0:T(8,128)(2,1)S(1)} %get-tuple-element.34), channel_id=1, source_target_pairs={{0,1},{1,0},{2,3},{3,2},{4,5},{5,4},{6,7},{7,6},{8,9},{9,8},{10,11... | collective-permute-start | bytes 1769480 | tf_op jit(solution)/shard_map/ppermute | solution.py:294
  73.2 31.3 %all-to-all-start.1 = ((bf16[12,24,1024]{2,1,0:T(8,128)(2,1)}), bf16[12,24,1024]{2,1,0:T(8,128)(2,1)S(1)}, u32[]{:S(2)}, u32[]{:S(2)}) async-start(bf16[12,24,1024]{2,1,0:T(8,128)(2,1)} %bitcast.9), calls=%async_computation.1 | async-start | bytes 1179648 | tf_op jit(solution)/shard_map/all_to_all | solution.py:291

commit v7 on v5

--- a/solution.py
+++ b/solution.py
@@ -132,11 +132,21 @@
     return side, here, there
 
 
-def own_kernel(cap, side_ref, own_ref, wg_ref, wu_far, gate_ref, up_ref, cols_ref, wu, sems):
+def own_kernel(
+    cap, side_ref, own_ref, wg_far, wu_far, gate_ref, up_ref, cols_ref, wg_oth, wu_oth, wg, wu, sems
+):
     rows, half = own_ref.shape
     slots = rows // 2
-    _, here, _ = halves(side_ref, half)
-    copies = fetch([(wu_far.at[here], wu)], sems)
+    _, here, there = halves(side_ref, half)
+    copies = fetch(
+        [
+            (wg_far.at[here], wg),
+            (wu_far.at[here], wu),
+            (wg_far.at[there], wg_oth),
+            (wu_far.at[there], wu_oth),
+        ],
+        sems,
+    )
     own = own_ref[...]
     x = dot(pick((slots, rows), 0, cap, 0), own).astype(B16)
     g = dot(pick((slots, rows), 0, cap, cap), own).astype(B16)
@@ -145,27 +155,25 @@
         cols = [g[:, (y * NX + xd) * 64 : (y * NX + xd) * 64 + 64] for y in range(wide // 64)]
         cols_ref[xd, :, 0 : wide // 2] = jnp.concatenate(cols[0::2], axis=1)
         cols_ref[xd, :, wide // 2 : wide] = jnp.concatenate(cols[1::2], axis=1)
-    gate_ref[...] = dot(x, wg_ref[here, :])
     copies[0].wait()
+    gate_ref[...] = dot(x, wg[...])
+    copies[1].wait()
     up_ref[...] = dot(x, wu[...])
-
-
-def rest_kernel(
-    cap, side_ref, oth_ref, gate_in, up_in, cols_ref, wg_ref, wu_far, gate_ref, up_ref, pack_ref, wu, sems
-):
-    rows, half = oth_ref.shape
+    copies[2].wait()
+    copies[3].wait()
+
+
+def rest_kernel(cap, oth_ref, gate_in, up_in, cols_ref, wg_ref, wu_ref, gate_ref, up_ref, pack_ref):
+    rows = oth_ref.shape[0]
     slots = rows // 2
-    _, _, there = halves(side_ref, half)
-    copies = fetch([(wu_far.at[there], wu)], sems)
     wide = cols_ref.shape[2]
     x = dot(pick((slots, rows), 0, cap, 0), oth_ref[...]).astype(B16)
-    pack_ref[:, :, 0:wide] = cols_ref[...]
-    gate = gate_in[...] + dot(x, wg_ref[there, :])
-    copies[0].wait()
-    up = up_in[...] + dot(x, wu[...])
+    gate = gate_in[...] + dot(x, wg_ref[...])
+    up = up_in[...] + dot(x, wu_ref[...])
     hidden = (gate * (1.0 / (1.0 + jnp.exp(-gate))) * up).astype(B16)
     gate_ref[...] = gate
     up_ref[...] = up
+    pack_ref[:, :, 0:wide] = cols_ref[...]
     for xd in range(NX):
         pack_ref[xd, :, wide:] = hidden
 
@@ -227,20 +235,18 @@
     keep_ref[...] = results(cap, hidden_ref[...], gate_term_ref[...], up_term_ref[...], wd, wg, wu)
 
 
-def down_kernel(bit_ref, packs_ref, cols_ref, keep_ref, give_ref):
+def down_kernel(bit_ref, side_ref, packs_ref, oth_ref, keep_ref, give_ref):
     n = keep_ref.shape[1]
-    slots = packs_ref.shape[1]
-    wide = cols_ref.shape[2]
-    bit = bit_ref[0]
+    wide = oth_ref.shape[2]
+    bit, side = bit_ref[0], side_ref[0]
     for at, out in ((1 - bit, give_ref), (bit, keep_ref)):
         cols = pl.ds(pl.multiple_of(at * n, n), n)
-        for h in range(2):
+        for place, ref in ((side, packs_ref), (1 - side, oth_ref)):
             total = None
             for k in range(NX):
-                rows = cols_ref[k, h * slots : (h + 1) * slots, cols]
-                part = dot(rows, packs_ref[k, :, wide:], ROWS0)
+                part = dot(ref[k, :, cols], packs_ref[k, :, wide:], ROWS0)
                 total = part if total is None else total + part
-            out[h] = total.astype(B16)
+            out[place] = total.astype(B16)
 
 
 def partner(bit_ref, pair_ref, h, at, n):
@@ -310,40 +316,34 @@
     own = trade(send, "expert", *chunks).reshape(2 * slots, half)
     oth = swap(own)
     floats = jax.ShapeDtypeStruct((slots, ff), F32)
-    halfway = landing(bf(half, ff))
-    gate, up, cols = fused(
+    down_half, in_half = bf(ff, half), bf(half, ff)
+    weights = [hbm(w[0]) for w in (gate_weight, up_weight, down_weight)]
+    gate, up, cols, wg_oth, wu_oth = fused(
         functools.partial(own_kernel, cap),
-        [floats, floats, bf(NX, slots, half // NX)],
+        [floats, floats, bf(NX, slots, half // NX), in_half, in_half],
         side,
         own,
-        gate_weight[0],
-        hbm(up_weight[0]),
+        *weights[:2],
         scalars=1,
         flops=slots * half * 2 * ff * 2 + slots * 2 * slots * half * 4,
         mib=12,
-        far=(3,),
-        scratch=halfway,
+        far=(2, 3),
+        scratch=[pltpu.VMEM(in_half.shape, B16)] * 2 + [pltpu.SemaphoreType.DMA((4,))],
     )
     gate, up, pack = fused(
         functools.partial(rest_kernel, cap),
         [floats, floats, pltpu.HBM((NX, slots, half // NX + ff), B16)],
-        side,
         oth,
         gate,
         up,
         cols,
-        gate_weight[0],
-        hbm(up_weight[0]),
-        scalars=1,
+        wg_oth,
+        wu_oth,
         flops=slots * half * 2 * ff * 2 + slots * 2 * slots * half * 2,
         mib=12,
-        far=(6,),
-        scratch=halfway,
-        alias={2: 0, 3: 1},
+        alias={1: 0, 2: 1},
     )
     packs = trade(pack, "x", *pack.shape)
-    weights = [hbm(w[0]) for w in (gate_weight, up_weight, down_weight)]
-    down_half, in_half = bf(ff, half), bf(half, ff)
     give, *terms = fused(
         functools.partial(give_kernel, cap),
         [bf(2 * slots, half)] + [bf(slots, ff)] * 3,
@@ -373,14 +373,16 @@
         scratch=landing(down_half, in_half, in_half),
     )
     total = (keep.astype(F32) + got.astype(F32)).astype(B16)
+    cols_oth = swap(packs[:, :, : half // NX])
     back = trade(total, "expert", *chunks).reshape(2 * slots, half)
     keep, give = fused(
         down_kernel,
         [bf(2, half // 8, ff)] * 2,
         bits[0],
+        side,
         packs,
-        pair(packs[:, :, : half // NX], "tensor"),
-        scalars=1,
+        cols_oth,
+        scalars=2,
         flops=half // 2 * ff * slots * 2 * NX,
     )
     for step, kernel in ((1, halve_rows_kernel), (2, halve_sides_kernel)):

time: 107 us -> 106 us (level)
  blocking collectives: 68 us -> 65.8 us
  starting transfers between devices: 12.2 us -> 14.1 us
  Pallas kernels: 16.1 us -> 14.9 us
    all_gather x4 -> x3, blocking collectives: 26.2 us -> 23.9 us  [pair(): return lax.all_gather(v, axis, axis=1, tiled=True)]
    ppermute x2 -> x3, starting transfers between devices: 4.31 us -> 6.24 us  [swap(): return lax.ppermute(v, 'tensor', [(0, 1), (1, 0)])]
    pallas_call x10, Pallas kernels: 16.1 us -> 14.9 us  [fused(): pl.pallas_call(kernel, out_shape=outs, in_specs=specs, out_specs=[pl.Bloc...]
  transfers between devices with their start and end apart: 4 -> 5, of which waited for: 1 -> 2; matrix products, arithmetic and copies ran while one was open for 1% -> 1% of each run, Pallas kernels for 6% -> 6%
where the time goes in v7:
time: 106 us; the launch traced here: 105 us
  blocking collectives  65.8 us (62%)
  Pallas kernels  14.9 us (14%)
  starting transfers between devices  14.1 us (13%)
  waiting for transfers between devices  8.57 us (8%)
  other arithmetic  1.07 us (1%)
    all_to_all x1, blocking collectives, trade(): lax.all_to_all(rows.reshape(shape), axis, split_axis=0, concat_axis=0, ti...  41.8 us
    all_gather x3, blocking collectives, pair(): return lax.all_gather(v, axis, axis=1, tiled=True)  23.9 us
    pallas_call x10, Pallas kernels, fused(): pl.pallas_call(kernel, out_shape=outs, in_specs=specs, out_specs=[pl.Bloc...  14.9 us
    all_to_all x2, waiting for transfers between devices, trade(): lax.all_to_all(rows.reshape(shape), axis, split_axis=0, concat_axis=0, ti...  8.05 us
    all_to_all x2, starting transfers between devices, trade(): lax.all_to_all(rows.reshape(shape), axis, split_axis=0, concat_axis=0, ti...  7.91 us
    ppermute x3, starting transfers between devices, swap(): return lax.ppermute(v, 'tensor', [(0, 1), (1, 0)])  6.24 us
  transfers between devices with their start and end apart: 5, of which 2 were waited for; matrix products, arithmetic and copies ran while one was open for 1% of the time, Pallas kernels for 6%

profile of v7, /device:TPU:32, one launch (start us, length us, event | category | flops | bytes accessed | tf_op | source)
XLA Modules:
  0.0 105.2 jit_solution(8963316742490580145)
XLA Ops:
  0.6 1.6 %shard_map.95 = bf16[288,1024]{1,0:T(8,128)(2,1)S(1)} custom-call(s32[8,128]{1,0:T(8,128)} %bitcast.29, f32[8,128]{1,0:T(8,128)} %bitcast.31, bf16[128,1024]{1,0:T(8,128)(2,1)} %refs_2_.1, bf16[128,1024]{1,0:T(8,128)(2,1)} %refs_3_.1), custom_call_target="tpu_custom_call" | custom-call | flops 150994944 | bytes 1122304 | tf_op jit(solution)/shard_map/pallas_call | solution.py:37
  2.2 41.8 %all_to_all.15 = bf16[12,24,1024]{2,1,0:T(8,128)(2,1)S(1)} all-to-all(bf16[12,24,1024]{2,1,0:T(8,128)(2,1)S(1)} %bitcast.20), channel_id=1, replica_groups=mesh['y4'=2,'y2'=2,'y1'=2,'x'=4,'expert'=12,'tensor'=2] {'expert'}, dimensions={0} | all-to-all | bytes 1179648 | tf_op jit(solution)/shard_map/all_to_all | solution.py:307
  44.1 1.9 %collective-permute-start = (bf16[288,1024]{1,0:T(8,128)(2,1)S(1)}, bf16[288,1024]{1,0:T(8,128)(2,1)S(1)}, u32[]{:S(2)}, u32[]{:S(2)}) collective-permute-start(bf16[288,1024]{1,0:T(8,128)(2,1)S(1)} %bitcast.16), channel_id=1, source_target_pairs={{0,1},{1,0},{2,3},{3,2},{4,5},{5,4},{6,7},{7,6},{8,9},{9,8},{10,11... | collective-permute-start | bytes 1769480 | tf_op jit(solution)/shard_map/ppermute | solution.py:310
  46.0 2.0 %shard_map.96 = (f32[144,384]{1,0:T(8,128)S(1)}, f32[144,384]{1,0:T(8,128)S(1)}, bf16[4,144,256]{2,1,0:T(8,128)(2,1)S(1)}, bf16[1024,384]{1,0:T(8,128)(2,1)S(1)}, bf16[1024,384]{1,0:T(8,128)(2,1)S(1)}) custom-call(s32[1]{0:T(128)} %bitcast.3.side_ref, bf16[288,1024]{1,0:T(8,128)(2,1)S(1)} %bitcast.17, bf16[2048,384]{1,0:T(8,128)(2,1)} %bitcast.21, ...), custom_call_target="tpu_custom_call" | custom-call | flops 396361728 | bytes 6045700 | tf_op jit(solution)/shard_map/pallas_call | solution.py:37
  48.0 0.0 collective-permute-done.oth_ref
  48.0 1.6 %shard_map.97 = (f32[144,384]{1,0:T(8,128)S(1)}, f32[144,384]{1,0:T(8,128)S(1)}, bf16[4,144,640]{2,1,0:T(8,128)(2,1)}) custom-call(bf16[288,1024]{1,0:T(8,128)(2,1)S(1)} %collective-permute-done.oth_ref, f32[144,384]{1,0:T(8,128)S(1)} %get-tuple-element.30.gate_in, ...), custom_call_target="tpu_custom_call", output_to_operand_aliasing={{0}: (1, {}), {1}: (2, {})} | custom-call | flops 311427072 | bytes 4079616 | tf_op jit(solution)/shard_map/pallas_call | solution.py:37
  49.6 3.7 %shard_map.98 = (bf16[288,1024]{1,0:T(8,128)(2,1)S(1)}, bf16[144,384]{1,0:T(8,128)(2,1)S(1)}, bf16[144,384]{1,0:T(8,128)(2,1)S(1)}, bf16[144,384]{1,0:T(8,128)(2,1)S(1)}) custom-call(s32[1]{0:T(128)} %bitcast.3.side_ref, bf16[288,1024]{1,0:T(8,128)(2,1)S(1)} %bitcast.18, bf16[288,1024]{1,0:T(8,128)(2,1)S(1)} %collective-permute-done.oth_ref, ...), custom_call_target="tpu_custom_call" | custom-call | flops 905969664 | bytes 7262212 | tf_op jit(solution)/shard_map/pallas_call | solution.py:37
  53.4 2.4 %collective-permute-start.1 = (bf16[288,1024]{1,0:T(8,128)(2,1)S(1)}, bf16[288,1024]{1,0:T(8,128)(2,1)S(1)}, u32[]{:S(2)}, u32[]{:S(2)}) collective-permute-start(bf16[288,1024]{1,0:T(8,128)(2,1)S(1)} %get-tuple-element.40), channel_id=1, source_target_pairs={{0,1},{1,0},{2,3},{3,2},{4,5},{5,4},{6,7},{7,6},{8,9},{9,8},{10,11... | collective-permute-start | bytes 1769480 | tf_op jit(solution)/shard_map/ppermute | solution.py:310
  55.8 4.3 %all-to-all-start.2 = ((bf16[4,144,640]{2,1,0:T(8,128)(2,1)}), bf16[4,144,640]{2,1,0:T(8,128)(2,1)S(1)}, u32[]{:S(2)}, u32[]{:S(2)}) async-start(bf16[4,144,640]{2,1,0:T(8,128)(2,1)} %get-tuple-element.41), calls=%async_computation.2 | async-start | bytes 1474560 | tf_op jit(solution)/shard_map/all_to_all | solution.py:307
  60.1 2.8 %shard_map.99 = bf16[288,1024]{1,0:T(8,128)(2,1)S(1)} custom-call(s32[1]{0:T(128)} %bitcast.3.side_ref, bf16[144,384]{1,0:T(8,128)(2,1)S(1)} %get-tuple-element.37.hidden_ref, bf16[144,384]{1,0:T(8,128)(2,1)S(1)} %get-tuple-element.38.gate_term_ref, bf16[144,384]{1,0:T(8,128)(2,1)S(1)} %get-tuple-element.39.up_term_ref, bf16[2048,384]{1,0:T(8,128)(2,1)} %bitcast.23, ...), custom_call_target="tpu_custom_call" | custom-call | flops 509607936 | bytes 5640196 | tf_op jit(solution)/shard_map/pallas_call | solution.py:37
  62.9 0.0 collective-permute-done.1
  62.9 1.1 %add_convert_fusion = bf16[288,1024]{1,0:T(8,128)(2,1)} fusion(bf16[288,1024]{1,0:T(8,128)(2,1)S(1)} %collective-permute-done.1, bf16[288,1024]{1,0:T(8,128)(2,1)S(1)} %shard_map.99), kind=kLoop, calls=%fused_computation | loop fusion | flops 1179648 | bytes 1769472 | tf_op jit(solution)/shard_map/convert_element_type | solution.py:375
  64.0 8.0 %all-to-all-done.2.packs_ref = bf16[4,144,640]{2,1,0:T(8,128)(2,1)S(1)} async-done(((bf16[4,144,640]{2,1,0:T(8,128)(2,1)}), bf16[4,144,640]{2,1,0:T(8,128)(2,1)S(1)}, u32[]{:S(2)}, u32[]{:S(2)}) %all-to-all-start.2) | async-done | bytes 737312 | tf_op jit(solution)/shard_map/all_to_all | solution.py:307
  72.0 3.6 %all-to-all-start.1 = ((bf16[12,24,1024]{2,1,0:T(8,128)(2,1)}), bf16[12,24,1024]{2,1,0:T(8,128)(2,1)S(1)}, u32[]{:S(2)}, u32[]{:S(2)}) async-start(bf16[12,24,1024]{2,1,0:T(8,128)(2,1)} %bitcast.9), calls=%async_computation.1 | async-start | bytes 1179648 | tf_op jit(solution)/shard_map/all_to_all | solution.py:307
  75.7 1.9 %collective-permute-start.2 = (bf16[4,144,256]{2,1,0:T(8,128)(2,1)S(1)}, bf16[4,144,256]{2,1,0:T(8,128)(2,1)S(1)}, u32[]{:S(2)}, u32[]{:S(2)}) collective-permute-start(bf16[4,144,256]{2,1,0:T(8,128)(2,1)S(1)} %slice.4), channel_id=1, source_target_pairs={{0,1},{1,0},{2,3},{3,2},{4,5},{5,4},{6,7},{7,6},{8,9},{9,8},{10,11... | collective-permute-start | bytes 884744 | tf_op jit(solution)/shard_map/ppermute | solution.py:310
  77.6 1.0 shard_map.94
  78.6 0.5 collective-permute-done.2.oth_ref
  79.1 0.8 shard_map.100
  79.9 7.6 %all_gather.9.pair_ref = bf16[2,256,384]{2,1,0:T(8,128)(2,1)S(1)} all-gather(bf16[2,128,384]{2,1,0:T(8,128)(2,1)S(1)} %get-tuple-element.43), channel_id=1, replica_groups=mesh['y4'=2,'y2'=2,'y1'=2,'x'=4,'expert'=12,'tensor'=2] {'y1'}, dimensions={1}, use_global_device_ids=true | all-gather | bytes 589824 | tf_op jit(solution)/shard_map/all_gather | solution.py:313
  87.5 0.1 shard_map.101
  87.6 7.6 %all_gather.10.pair_ref = bf16[2,128,384]{2,1,0:T(8,128)(2,1)S(1)} all-gather(bf16[2,64,384]{2,1,0:T(8,128)(2,1)S(1)} %get-tuple-element.45), channel_id=1, replica_groups=mesh['y4'=2,'y2'=2,'y1'=2,'x'=4,'expert'=12,'tensor'=2] {'y2'}, dimensions={1}, use_global_device_ids=true | all-gather | bytes 294912 | tf_op jit(solution)/shard_map/all_gather | solution.py:313
  95.3 8.7 %all_gather.11.pair_ref = bf16[2,64,384]{2,1,0:T(8,128)(2,1)S(1)} all-gather(bf16[2,32,384]{2,1,0:T(8,128)(2,1)S(1)} %get-tuple-element.47), channel_id=1, replica_groups=mesh['y4'=2,'y2'=2,'y1'=2,'x'=4,'expert'=12,'tensor'=2] {'y4'}, dimensions={1}, use_global_device_ids=true | all-gather | bytes 147456 | tf_op jit(solution)/shard_map/all_gather | solution.py:313
  103.9 0.0 all-to-all-done.1
  103.9 1.3 %shard_map.103 = (bf16[128,1024]{1,0:T(8,128)(2,1)}, bf16[128,1024]{1,0:T(8,128)(2,1)}, bf16[64,384]{1,0:T(8,128)(2,1)}) custom-call(s32[1]{0:T(128)} %bitcast.bit_ref, bf16[128,288]{1,0:T(8,128)(2,1)S(1)} %get-tuple-element.27.high_ref, bf16[128,288]{1,0:T(8,128)(2,1)S(1)} %get-tuple-element.28.low_ref, bf16[128,288]{1,0:T(8,128)(2,1)S(1)} %get-tuple-element.29.right_ref, ...), custom_call_target="tpu_custom_call" | custom-call | flops 226492416 | bytes 1531908 | tf_op jit(solution)/shard_map/pallas_call | solution.py:37
  (2 shorter events, 0.1 us)
Async XLA Ops:
  44.1 3.9 %collective-permute-start = (bf16[288,1024]{1,0:T(8,128)(2,1)S(1)}, bf16[288,1024]{1,0:T(8,128)(2,1)S(1)}, u32[]{:S(2)}, u32[]{:S(2)}) collective-permute-start(bf16[288,1024]{1,0:T(8,128)(2,1)S(1)} %bitcast.16), channel_id=1, source_target_pairs={{0,1},{1,0},{2,3},{3,2},{4,5},{5,4},{6,7},{7,6},{8,9},{9,8},{10,11... | collective-permute-start | bytes 1769480 | tf_op jit(solution)/shard_map/ppermute | solution.py:310
  53.4 9.5 %collective-permute-start.1 = (bf16[288,1024]{1,0:T(8,128)(2,1)S(1)}, bf16[288,1024]{1,0:T(8,128)(2,1)S(1)}, u32[]{:S(2)}, u32[]{:S(2)}) collective-permute-start(bf16[288,1024]{1,0:T(8,128)(2,1)S(1)} %get-tuple-element.40), channel_id=1, source_target_pairs={{0,1},{1,0},{2,3},{3,2},{4,5},{5,4},{6,7},{7,6},{8,9},{9,8},{10,11... | collective-permute-start | bytes 1769480 | tf_op jit(solution)/shard_map/ppermute | solution.py:310
  55.8 16.2 %all-to-all-start.2 = ((bf16[4,144,640]{2,1,0:T(8,128)(2,1)}), bf16[4,144,640]{2,1,0:T(8,128)(2,1)S(1)}, u32[]{:S(2)}, u32[]{:S(2)}) async-start(bf16[4,144,640]{2,1,0:T(8,128)(2,1)} %get-tuple-element.41), calls=%async_computation.2 | async-start | bytes 1474560 | tf_op jit(solution)/shard_map/all_to_all | solution.py:307
  72.0 31.9 %all-to-all-start.1 = ((bf16[12,24,1024]{2,1,0:T(8,128)(2,1)}), bf16[12,24,1024]{2,1,0:T(8,128)(2,1)S(1)}, u32[]{:S(2)}, u32[]{:S(2)}) async-start(bf16[12,24,1024]{2,1,0:T(8,128)(2,1)} %bitcast.9), calls=%async_computation.1 | async-start | bytes 1179648 | tf_op jit(solution)/shard_map/all_to_all | solution.py:307
  75.7 3.5 %collective-permute-start.2 = (bf16[4,144,256]{2,1,0:T(8,128)(2,1)S(1)}, bf16[4,144,256]{2,1,0:T(8,128)(2,1)S(1)}, u32[]{:S(2)}, u32[]{:S(2)}) collective-permute-start(bf16[4,144,256]{2,1,0:T(8,128)(2,1)S(1)} %slice.4), channel_id=1, source_target_pairs={{0,1},{1,0},{2,3},{3,2},{4,5},{5,4},{6,7},{7,6},{8,9},{9,8},{10,11... | collective-permute-start | bytes 884744 | tf_op jit(solution)/shard_map/ppermute | solution.py:310

commit v8 on v7

--- a/solution.py
+++ b/solution.py
@@ -235,18 +235,20 @@
     keep_ref[...] = results(cap, hidden_ref[...], gate_term_ref[...], up_term_ref[...], wd, wg, wu)
 
 
-def down_kernel(bit_ref, side_ref, packs_ref, oth_ref, keep_ref, give_ref):
+def down_kernel(bit_ref, packs_ref, cols_ref, keep_ref, give_ref):
     n = keep_ref.shape[1]
-    wide = oth_ref.shape[2]
-    bit, side = bit_ref[0], side_ref[0]
+    slots = packs_ref.shape[1]
+    wide = cols_ref.shape[2]
+    bit = bit_ref[0]
     for at, out in ((1 - bit, give_ref), (bit, keep_ref)):
         cols = pl.ds(pl.multiple_of(at * n, n), n)
-        for place, ref in ((side, packs_ref), (1 - side, oth_ref)):
+        for h in range(2):
             total = None
             for k in range(NX):
-                part = dot(ref[k, :, cols], packs_ref[k, :, wide:], ROWS0)
+                rows = cols_ref[k, h * slots : (h + 1) * slots, cols]
+                part = dot(rows, packs_ref[k, :, wide:], ROWS0)
                 total = part if total is None else total + part
-            out[place] = total.astype(B16)
+            out[h] = total.astype(B16)
 
 
 def partner(bit_ref, pair_ref, h, at, n):
@@ -373,16 +375,14 @@
         scratch=landing(down_half, in_half, in_half),
     )
     total = (keep.astype(F32) + got.astype(F32)).astype(B16)
-    cols_oth = swap(packs[:, :, : half // NX])
     back = trade(total, "expert", *chunks).reshape(2 * slots, half)
     keep, give = fused(
         down_kernel,
         [bf(2, half // 8, ff)] * 2,
         bits[0],
-        side,
         packs,
-        cols_oth,
-        scalars=2,
+        pair(packs[:, :, : half // NX], "tensor"),
+        scalars=1,
         flops=half // 2 * ff * slots * 2 * NX,
     )
     for step, kernel in ((1, halve_rows_kernel), (2, halve_sides_kernel)):

time: 106 us -> 105 us (level)
  blocking collectives: 65.8 us -> 68 us
  starting transfers between devices: 14.1 us -> 12.2 us
    all_gather x3 -> x4, blocking collectives: 23.9 us -> 26.1 us  [pair(): return lax.all_gather(v, axis, axis=1, tiled=True)]
    ppermute x3 -> x2, starting transfers between devices: 6.24 us -> 4.31 us  [swap(): return lax.ppermute(v, 'tensor', [(0, 1), (1, 0)])]
  transfers between devices with their start and end apart: 5 -> 4, of which waited for: 2 -> 1; matrix products, arithmetic and copies ran while one was open for 1% -> 1% of each run, Pallas kernels for 6% -> 6%
where the time goes in v8:
time: 105 us
  blocking collectives  68 us (65%)
  Pallas kernels  14.9 us (14%)
  starting transfers between devices  12.2 us (12%)
  waiting for transfers between devices  8.07 us (8%)
  other arithmetic  1.06 us (1%)
    all_to_all x1, blocking collectives, trade(): lax.all_to_all(rows.reshape(shape), axis, split_axis=0, concat_axis=0, ti...  41.8 us
    all_gather x4, blocking collectives, pair(): return lax.all_gather(v, axis, axis=1, tiled=True)  26.1 us
    pallas_call x10, Pallas kernels, fused(): pl.pallas_call(kernel, out_shape=outs, in_specs=specs, out_specs=[pl.Bloc...  14.9 us
    all_to_all x2, waiting for transfers between devices, trade(): lax.all_to_all(rows.reshape(shape), axis, split_axis=0, concat_axis=0, ti...  8.06 us
    all_to_all x2, starting transfers between devices, trade(): lax.all_to_all(rows.reshape(shape), axis, split_axis=0, concat_axis=0, ti...  7.91 us
    ppermute x2, starting transfers between devices, swap(): return lax.ppermute(v, 'tensor', [(0, 1), (1, 0)])  4.31 us
  transfers between devices with their start and end apart: 4, of which 1 were waited for; matrix products, arithmetic and copies ran while one was open for 1% of the time, Pallas kernels for 6%

profile of v8, /device:TPU:32, one launch (start us, length us, event | category | flops | bytes accessed | tf_op | source)
XLA Modules:
  0.0 105.0 jit_solution(9258928435765289680)
XLA Ops:
  0.6 1.6 %shard_map.95 = bf16[288,1024]{1,0:T(8,128)(2,1)S(1)} custom-call(s32[8,128]{1,0:T(8,128)} %bitcast.29, f32[8,128]{1,0:T(8,128)} %bitcast.31, bf16[128,1024]{1,0:T(8,128)(2,1)} %refs_2_.1, bf16[128,1024]{1,0:T(8,128)(2,1)} %refs_3_.1), custom_call_target="tpu_custom_call" | custom-call | flops 150994944 | bytes 1122304 | tf_op jit(solution)/shard_map/pallas_call | solution.py:37
  2.2 41.8 %all_to_all.15 = bf16[12,24,1024]{2,1,0:T(8,128)(2,1)S(1)} all-to-all(bf16[12,24,1024]{2,1,0:T(8,128)(2,1)S(1)} %bitcast.20), channel_id=1, replica_groups=mesh['y4'=2,'y2'=2,'y1'=2,'x'=4,'expert'=12,'tensor'=2] {'expert'}, dimensions={0} | all-to-all | bytes 1179648 | tf_op jit(solution)/shard_map/all_to_all | solution.py:309
  44.1 1.9 %collective-permute-start = (bf16[288,1024]{1,0:T(8,128)(2,1)S(1)}, bf16[288,1024]{1,0:T(8,128)(2,1)S(1)}, u32[]{:S(2)}, u32[]{:S(2)}) collective-permute-start(bf16[288,1024]{1,0:T(8,128)(2,1)S(1)} %bitcast.16), channel_id=1, source_target_pairs={{0,1},{1,0},{2,3},{3,2},{4,5},{5,4},{6,7},{7,6},{8,9},{9,8},{10,11... | collective-permute-start | bytes 1769480 | tf_op jit(solution)/shard_map/ppermute | solution.py:312
  46.0 2.0 %shard_map.96 = (f32[144,384]{1,0:T(8,128)S(1)}, f32[144,384]{1,0:T(8,128)S(1)}, bf16[4,144,256]{2,1,0:T(8,128)(2,1)S(1)}, bf16[1024,384]{1,0:T(8,128)(2,1)S(1)}, bf16[1024,384]{1,0:T(8,128)(2,1)S(1)}) custom-call(s32[1]{0:T(128)} %bitcast.3.side_ref, bf16[288,1024]{1,0:T(8,128)(2,1)S(1)} %bitcast.17, bf16[2048,384]{1,0:T(8,128)(2,1)} %bitcast.21, ...), custom_call_target="tpu_custom_call" | custom-call | flops 396361728 | bytes 6045700 | tf_op jit(solution)/shard_map/pallas_call | solution.py:37
  48.0 0.0 collective-permute-done.oth_ref
  48.0 1.6 %shard_map.97 = (f32[144,384]{1,0:T(8,128)S(1)}, f32[144,384]{1,0:T(8,128)S(1)}, bf16[4,144,640]{2,1,0:T(8,128)(2,1)}) custom-call(bf16[288,1024]{1,0:T(8,128)(2,1)S(1)} %collective-permute-done.oth_ref, f32[144,384]{1,0:T(8,128)S(1)} %get-tuple-element.30.gate_in, ...), custom_call_target="tpu_custom_call", output_to_operand_aliasing={{0}: (1, {}), {1}: (2, {})} | custom-call | flops 311427072 | bytes 4079616 | tf_op jit(solution)/shard_map/pallas_call | solution.py:37
  49.6 3.7 %shard_map.98 = (bf16[288,1024]{1,0:T(8,128)(2,1)S(1)}, bf16[144,384]{1,0:T(8,128)(2,1)S(1)}, bf16[144,384]{1,0:T(8,128)(2,1)S(1)}, bf16[144,384]{1,0:T(8,128)(2,1)S(1)}) custom-call(s32[1]{0:T(128)} %bitcast.3.side_ref, bf16[288,1024]{1,0:T(8,128)(2,1)S(1)} %bitcast.18, bf16[288,1024]{1,0:T(8,128)(2,1)S(1)} %collective-permute-done.oth_ref, ...), custom_call_target="tpu_custom_call" | custom-call | flops 905969664 | bytes 7262212 | tf_op jit(solution)/shard_map/pallas_call | solution.py:37
  53.4 2.4 %collective-permute-start.1 = (bf16[288,1024]{1,0:T(8,128)(2,1)S(1)}, bf16[288,1024]{1,0:T(8,128)(2,1)S(1)}, u32[]{:S(2)}, u32[]{:S(2)}) collective-permute-start(bf16[288,1024]{1,0:T(8,128)(2,1)S(1)} %get-tuple-element.40), channel_id=1, source_target_pairs={{0,1},{1,0},{2,3},{3,2},{4,5},{5,4},{6,7},{7,6},{8,9},{9,8},{10,11... | collective-permute-start | bytes 1769480 | tf_op jit(solution)/shard_map/ppermute | solution.py:312
  55.8 4.3 %all-to-all-start.2 = ((bf16[4,144,640]{2,1,0:T(8,128)(2,1)}), bf16[4,144,640]{2,1,0:T(8,128)(2,1)S(1)}, u32[]{:S(2)}, u32[]{:S(2)}) async-start(bf16[4,144,640]{2,1,0:T(8,128)(2,1)} %get-tuple-element.41), calls=%async_computation.2 | async-start | bytes 1474560 | tf_op jit(solution)/shard_map/all_to_all | solution.py:309
  60.1 2.8 %shard_map.99 = bf16[288,1024]{1,0:T(8,128)(2,1)S(1)} custom-call(s32[1]{0:T(128)} %bitcast.3.side_ref, bf16[144,384]{1,0:T(8,128)(2,1)S(1)} %get-tuple-element.37.hidden_ref, bf16[144,384]{1,0:T(8,128)(2,1)S(1)} %get-tuple-element.38.gate_term_ref, bf16[144,384]{1,0:T(8,128)(2,1)S(1)} %get-tuple-element.39.up_term_ref, bf16[2048,384]{1,0:T(8,128)(2,1)} %bitcast.23, ...), custom_call_target="tpu_custom_call" | custom-call | flops 509607936 | bytes 5640196 | tf_op jit(solution)/shard_map/pallas_call | solution.py:37
  62.9 0.0 collective-permute-done.1
  62.9 1.1 %add_convert_fusion = bf16[288,1024]{1,0:T(8,128)(2,1)} fusion(bf16[288,1024]{1,0:T(8,128)(2,1)S(1)} %collective-permute-done.1, bf16[288,1024]{1,0:T(8,128)(2,1)S(1)} %shard_map.99), kind=kLoop, calls=%fused_computation | loop fusion | flops 1179648 | bytes 1769472 | tf_op jit(solution)/shard_map/convert_element_type | solution.py:377
  64.0 8.1 %all-to-all-done.2.packs_ref = bf16[4,144,640]{2,1,0:T(8,128)(2,1)S(1)} async-done(((bf16[4,144,640]{2,1,0:T(8,128)(2,1)}), bf16[4,144,640]{2,1,0:T(8,128)(2,1)S(1)}, u32[]{:S(2)}, u32[]{:S(2)}) %all-to-all-start.2) | async-done | bytes 737312 | tf_op jit(solution)/shard_map/all_to_all | solution.py:309
  72.0 3.6 %all-to-all-start.1 = ((bf16[12,24,1024]{2,1,0:T(8,128)(2,1)}), bf16[12,24,1024]{2,1,0:T(8,128)(2,1)S(1)}, u32[]{:S(2)}, u32[]{:S(2)}) async-start(bf16[12,24,1024]{2,1,0:T(8,128)(2,1)} %bitcast.9), calls=%async_computation.1 | async-start | bytes 1179648 | tf_op jit(solution)/shard_map/all_to_all | solution.py:309
  75.6 1.0 shard_map.94
  76.7 2.2 %all_gather.12.cols_ref = bf16[4,288,256]{2,1,0:T(8,128)(2,1)S(1)} all-gather(bf16[4,144,256]{2,1,0:T(8,128)(2,1)S(1)} %slice.4), channel_id=1, replica_groups=mesh['y4'=2,'y2'=2,'y1'=2,'x'=4,'expert'=12,'tensor'=2] {'tensor'}, dimensions={1}, use_global_device_ids=true | all-gather | bytes 884736 | tf_op jit(solution)/shard_map/all_gather | solution.py:315
  78.9 0.8 shard_map.100
  79.7 7.6 %all_gather.13.pair_ref = bf16[2,256,384]{2,1,0:T(8,128)(2,1)S(1)} all-gather(bf16[2,128,384]{2,1,0:T(8,128)(2,1)S(1)} %get-tuple-element.43), channel_id=1, replica_groups=mesh['y4'=2,'y2'=2,'y1'=2,'x'=4,'expert'=12,'tensor'=2] {'y1'}, dimensions={1}, use_global_device_ids=true | all-gather | bytes 589824 | tf_op jit(solution)/shard_map/all_gather | solution.py:315
  87.3 0.1 shard_map.101
  87.3 7.6 %all_gather.14.pair_ref = bf16[2,128,384]{2,1,0:T(8,128)(2,1)S(1)} all-gather(bf16[2,64,384]{2,1,0:T(8,128)(2,1)S(1)} %get-tuple-element.45), channel_id=1, replica_groups=mesh['y4'=2,'y2'=2,'y1'=2,'x'=4,'expert'=12,'tensor'=2] {'y2'}, dimensions={1}, use_global_device_ids=true | all-gather | bytes 294912 | tf_op jit(solution)/shard_map/all_gather | solution.py:315
  95.0 8.7 %all_gather.15.pair_ref = bf16[2,64,384]{2,1,0:T(8,128)(2,1)S(1)} all-gather(bf16[2,32,384]{2,1,0:T(8,128)(2,1)S(1)} %get-tuple-element.47), channel_id=1, replica_groups=mesh['y4'=2,'y2'=2,'y1'=2,'x'=4,'expert'=12,'tensor'=2] {'y4'}, dimensions={1}, use_global_device_ids=true | all-gather | bytes 147456 | tf_op jit(solution)/shard_map/all_gather | solution.py:315
  103.7 0.0 all-to-all-done.1
  103.7 1.3 %shard_map.103 = (bf16[128,1024]{1,0:T(8,128)(2,1)}, bf16[128,1024]{1,0:T(8,128)(2,1)}, bf16[64,384]{1,0:T(8,128)(2,1)}) custom-call(s32[1]{0:T(128)} %bitcast.bit_ref, bf16[128,288]{1,0:T(8,128)(2,1)S(1)} %get-tuple-element.27.high_ref, bf16[128,288]{1,0:T(8,128)(2,1)S(1)} %get-tuple-element.28.low_ref, bf16[128,288]{1,0:T(8,128)(2,1)S(1)} %get-tuple-element.29.right_ref, ...), custom_call_target="tpu_custom_call" | custom-call | flops 226492416 | bytes 1531908 | tf_op jit(solution)/shard_map/pallas_call | solution.py:37
  (2 shorter events, 0.1 us)
Async XLA Ops:
  44.1 3.9 %collective-permute-start = (bf16[288,1024]{1,0:T(8,128)(2,1)S(1)}, bf16[288,1024]{1,0:T(8,128)(2,1)S(1)}, u32[]{:S(2)}, u32[]{:S(2)}) collective-permute-start(bf16[288,1024]{1,0:T(8,128)(2,1)S(1)} %bitcast.16), channel_id=1, source_target_pairs={{0,1},{1,0},{2,3},{3,2},{4,5},{5,4},{6,7},{7,6},{8,9},{9,8},{10,11... | collective-permute-start | bytes 1769480 | tf_op jit(solution)/shard_map/ppermute | solution.py:312
  53.4 9.5 %collective-permute-start.1 = (bf16[288,1024]{1,0:T(8,128)(2,1)S(1)}, bf16[288,1024]{1,0:T(8,128)(2,1)S(1)}, u32[]{:S(2)}, u32[]{:S(2)}) collective-permute-start(bf16[288,1024]{1,0:T(8,128)(2,1)S(1)} %get-tuple-element.40), channel_id=1, source_target_pairs={{0,1},{1,0},{2,3},{3,2},{4,5},{5,4},{6,7},{7,6},{8,9},{9,8},{10,11... | collective-permute-start | bytes 1769480 | tf_op jit(solution)/shard_map/ppermute | solution.py:312
  55.8 16.3 %all-to-all-start.2 = ((bf16[4,144,640]{2,1,0:T(8,128)(2,1)}), bf16[4,144,640]{2,1,0:T(8,128)(2,1)S(1)}, u32[]{:S(2)}, u32[]{:S(2)}) async-start(bf16[4,144,640]{2,1,0:T(8,128)(2,1)} %get-tuple-element.41), calls=%async_computation.2 | async-start | bytes 1474560 | tf_op jit(solution)/shard_map/all_to_all | solution.py:309
  72.0 31.7 %all-to-all-start.1 = ((bf16[12,24,1024]{2,1,0:T(8,128)(2,1)}), bf16[12,24,1024]{2,1,0:T(8,128)(2,1)S(1)}, u32[]{:S(2)}, u32[]{:S(2)}) async-start(bf16[12,24,1024]{2,1,0:T(8,128)(2,1)} %bitcast.9), calls=%async_computation.1 | async-start | bytes 1179648 | tf_op jit(solution)/shard_map/all_to_all | solution.py:309

commit v9 on v8

--- a/solution.py
+++ b/solution.py
@@ -26,7 +26,7 @@
     return pltpu.with_memory_space_constraint(v, pltpu.HBM)
 
 
-def fused(kernel, outs, *args, scalars=0, flops=0, mib=8, far=(), scratch=(), alias=None):
+def fused(kernel, outs, *args, scalars=0, flops=0, mib=8, far=(), scratch=(), alias=None, blocks=None):
     specs = [
         pl.BlockSpec(
             memory_space=pltpu.SMEM if i < scalars else pltpu.HBM if i in far else pltpu.VMEM
@@ -37,8 +37,11 @@
     return pl.pallas_call(
         kernel,
         out_shape=outs,
+        grid=(1,) if blocks else (),
         in_specs=specs,
-        out_specs=[pl.BlockSpec(memory_space=pltpu.VMEM)] * len(outs),
+        out_specs=[
+            (blocks or {}).get(i, pl.BlockSpec(memory_space=pltpu.VMEM)) for i in range(len(outs))
+        ],
         scratch_shapes=scratch,
         input_output_aliases=alias or {},
         compiler_params=pltpu.CompilerParams(vmem_limit_bytes=mib << 20),
@@ -163,19 +166,17 @@
     copies[3].wait()
 
 
-def rest_kernel(cap, oth_ref, gate_in, up_in, cols_ref, wg_ref, wu_ref, gate_ref, up_ref, pack_ref):
+def rest_kernel(cap, oth_ref, gate_in, up_in, _, wg_ref, wu_ref, gate_ref, up_ref, pack_ref):
     rows = oth_ref.shape[0]
     slots = rows // 2
-    wide = cols_ref.shape[2]
     x = dot(pick((slots, rows), 0, cap, 0), oth_ref[...]).astype(B16)
     gate = gate_in[...] + dot(x, wg_ref[...])
     up = up_in[...] + dot(x, wu_ref[...])
     hidden = (gate * (1.0 / (1.0 + jnp.exp(-gate))) * up).astype(B16)
     gate_ref[...] = gate
     up_ref[...] = up
-    pack_ref[:, :, 0:wide] = cols_ref[...]
     for xd in range(NX):
-        pack_ref[xd, :, wide:] = hidden
+        pack_ref[xd] = hidden
 
 
 def results(cap, hidden, gate_term, up_term, wd, wg, wu):
@@ -320,9 +321,12 @@
     floats = jax.ShapeDtypeStruct((slots, ff), F32)
     down_half, in_half = bf(ff, half), bf(half, ff)
     weights = [hbm(w[0]) for w in (gate_weight, up_weight, down_weight)]
-    gate, up, cols, wg_oth, wu_oth = fused(
+    wide = half // NX
+    pack_shape = pltpu.HBM((NX, slots, wide + ff), B16)
+    whole = (pl.Element(NX), pl.Element(slots))
+    gate, up, pack, wg_oth, wu_oth = fused(
         functools.partial(own_kernel, cap),
-        [floats, floats, bf(NX, slots, half // NX), in_half, in_half],
+        [floats, floats, pack_shape, in_half, in_half],
         side,
         own,
         *weights[:2],
@@ -331,19 +335,22 @@
         mib=12,
         far=(2, 3),
         scratch=[pltpu.VMEM(in_half.shape, B16)] * 2 + [pltpu.SemaphoreType.DMA((4,))],
+        blocks={2: pl.BlockSpec((*whole, pl.Element(wide)), lambda i: (0, 0, 0))},
     )
     gate, up, pack = fused(
         functools.partial(rest_kernel, cap),
-        [floats, floats, pltpu.HBM((NX, slots, half // NX + ff), B16)],
+        [floats, floats, pack_shape],
         oth,
         gate,
         up,
-        cols,
+        pack,
         wg_oth,
         wu_oth,
         flops=slots * half * 2 * ff * 2 + slots * 2 * slots * half * 2,
         mib=12,
-        alias={1: 0, 2: 1},
+        far=(3,),
+        alias={1: 0, 2: 1, 3: 2},
+        blocks={2: pl.BlockSpec((*whole, pl.Element(ff)), lambda i: (0, 0, wide))},
     )
     packs = trade(pack, "x", *pack.shape)
     give, *terms = fused(

time: 105 us -> 106 us (level)
  the two profiles are of different devices: /device:TPU:32 before, /device:TPU:56 now
where the time goes in v9:
time: 106 us
  blocking collectives  68 us (64%)
  Pallas kernels  15.6 us (15%)
  starting transfers between devices  12.2 us (12%)
  waiting for transfers between devices  8.05 us (8%)
  other arithmetic  1.06 us (1%)
    all_to_all x1, blocking collectives, trade(): lax.all_to_all(rows.reshape(shape), axis, split_axis=0, concat_axis=0, ti...  41.8 us
    all_gather x4, blocking collectives, pair(): return lax.all_gather(v, axis, axis=1, tiled=True)  26.1 us
    pallas_call x10, Pallas kernels, fused(): pl.pallas_call(kernel, out_shape=outs, grid=(1,) if blocks else (), in_sp...  15.6 us
    all_to_all x2, waiting for transfers between devices, trade(): lax.all_to_all(rows.reshape(shape), axis, split_axis=0, concat_axis=0, ti...  8.05 us
    all_to_all x2, starting transfers between devices, trade(): lax.all_to_all(rows.reshape(shape), axis, split_axis=0, concat_axis=0, ti...  7.92 us
    ppermute x2, starting transfers between devices, swap(): return lax.ppermute(v, 'tensor', [(0, 1), (1, 0)])  4.32 us
  transfers between devices with their start and end apart: 4, of which 1 were waited for; matrix products, arithmetic and copies ran while one was open for 1% of the time, Pallas kernels for 7%

profile of v9, /device:TPU:56, one launch (start us, length us, event | category | flops | bytes accessed | tf_op | source)
XLA Modules:
  0.0 105.7 jit_solution(11926043491374389555)
XLA Ops:
  0.6 1.6 %shard_map.95 = bf16[288,1024]{1,0:T(8,128)(2,1)S(1)} custom-call(s32[8,128]{1,0:T(8,128)} %bitcast.29, f32[8,128]{1,0:T(8,128)} %bitcast.31, bf16[128,1024]{1,0:T(8,128)(2,1)} %refs_2_.1, bf16[128,1024]{1,0:T(8,128)(2,1)} %refs_3_.1), custom_call_target="tpu_custom_call" | custom-call | flops 150994944 | bytes 1122304 | tf_op jit(solution)/shard_map/pallas_call | solution.py:37
  2.2 41.8 %all_to_all.15 = bf16[12,24,1024]{2,1,0:T(8,128)(2,1)S(1)} all-to-all(bf16[12,24,1024]{2,1,0:T(8,128)(2,1)S(1)} %bitcast.20), channel_id=1, replica_groups=mesh['y4'=2,'y2'=2,'y1'=2,'x'=4,'expert'=12,'tensor'=2] {'expert'}, dimensions={0} | all-to-all | bytes 1179648 | tf_op jit(solution)/shard_map/all_to_all | solution.py:310
  44.0 1.9 %collective-permute-start = (bf16[288,1024]{1,0:T(8,128)(2,1)S(1)}, bf16[288,1024]{1,0:T(8,128)(2,1)S(1)}, u32[]{:S(2)}, u32[]{:S(2)}) collective-permute-start(bf16[288,1024]{1,0:T(8,128)(2,1)S(1)} %bitcast.16), channel_id=1, source_target_pairs={{0,1},{1,0},{2,3},{3,2},{4,5},{5,4},{6,7},{7,6},{8,9},{9,8},{10,11... | collective-permute-start | bytes 1769480 | tf_op jit(solution)/shard_map/ppermute | solution.py:313
  46.0 2.8 %shard_map.96 = (f32[144,384]{1,0:T(8,128)S(1)}, f32[144,384]{1,0:T(8,128)S(1)}, bf16[4,144,640]{2,1,0:T(8,128)(2,1)}, bf16[1024,384]{1,0:T(8,128)(2,1)S(1)}, bf16[1024,384]{1,0:T(8,128)(2,1)S(1)}) custom-call(s32[1]{0:T(128)} %bitcast.3.side_ref, bf16[288,1024]{1,0:T(8,128)(2,1)S(1)} %bitcast.17, bf16[2048,384]{1,0:T(8,128)(2,1)} %bitcast.21, ...), custom_call_target="tpu_custom_call" | custom-call | flops 396361728 | bytes 6488068 | tf_op jit(solution)/shard_map/pallas_call | solution.py:37
  48.8 0.0 collective-permute-done.oth_ref
  48.8 1.6 %shard_map.97 = (f32[144,384]{1,0:T(8,128)S(1)}, f32[144,384]{1,0:T(8,128)S(1)}, bf16[4,144,640]{2,1,0:T(8,128)(2,1)}) custom-call(bf16[288,1024]{1,0:T(8,128)(2,1)S(1)} %collective-permute-done.oth_ref, f32[144,384]{1,0:T(8,128)S(1)} %get-tuple-element.30.gate_in, ...), custom_call_target="tpu_custom_call", output_to_operand_aliasing={{0}: (1, {}), {1}: (2, {}), {2}: (3, {})} | custom-call | flops 311427072 | bytes 4521984 | tf_op jit(solution)/shard_map/pallas_call | solution.py:37
  50.3 3.7 %shard_map.98 = (bf16[288,1024]{1,0:T(8,128)(2,1)S(1)}, bf16[144,384]{1,0:T(8,128)(2,1)S(1)}, bf16[144,384]{1,0:T(8,128)(2,1)S(1)}, bf16[144,384]{1,0:T(8,128)(2,1)S(1)}) custom-call(s32[1]{0:T(128)} %bitcast.3.side_ref, bf16[288,1024]{1,0:T(8,128)(2,1)S(1)} %bitcast.18, bf16[288,1024]{1,0:T(8,128)(2,1)S(1)} %collective-permute-done.oth_ref, ...), custom_call_target="tpu_custom_call" | custom-call | flops 905969664 | bytes 7262212 | tf_op jit(solution)/shard_map/pallas_call | solution.py:37
  54.1 2.4 %collective-permute-start.1 = (bf16[288,1024]{1,0:T(8,128)(2,1)S(1)}, bf16[288,1024]{1,0:T(8,128)(2,1)S(1)}, u32[]{:S(2)}, u32[]{:S(2)}) collective-permute-start(bf16[288,1024]{1,0:T(8,128)(2,1)S(1)} %get-tuple-element.40), channel_id=1, source_target_pairs={{0,1},{1,0},{2,3},{3,2},{4,5},{5,4},{6,7},{7,6},{8,9},{9,8},{10,11... | collective-permute-start | bytes 1769480 | tf_op jit(solution)/shard_map/ppermute | solution.py:313
  56.5 4.3 %all-to-all-start.2 = ((bf16[4,144,640]{2,1,0:T(8,128)(2,1)}), bf16[4,144,640]{2,1,0:T(8,128)(2,1)S(1)}, u32[]{:S(2)}, u32[]{:S(2)}) async-start(bf16[4,144,640]{2,1,0:T(8,128)(2,1)} %get-tuple-element.41), calls=%async_computation.2 | async-start | bytes 1474560 | tf_op jit(solution)/shard_map/all_to_all | solution.py:310
  60.8 2.8 %shard_map.99 = bf16[288,1024]{1,0:T(8,128)(2,1)S(1)} custom-call(s32[1]{0:T(128)} %bitcast.3.side_ref, bf16[144,384]{1,0:T(8,128)(2,1)S(1)} %get-tuple-element.37.hidden_ref, bf16[144,384]{1,0:T(8,128)(2,1)S(1)} %get-tuple-element.38.gate_term_ref, bf16[144,384]{1,0:T(8,128)(2,1)S(1)} %get-tuple-element.39.up_term_ref, bf16[2048,384]{1,0:T(8,128)(2,1)} %bitcast.23, ...), custom_call_target="tpu_custom_call" | custom-call | flops 509607936 | bytes 5640196 | tf_op jit(solution)/shard_map/pallas_call | solution.py:37
  63.6 0.0 collective-permute-done.1
  63.6 1.1 %add_convert_fusion = bf16[288,1024]{1,0:T(8,128)(2,1)} fusion(bf16[288,1024]{1,0:T(8,128)(2,1)S(1)} %collective-permute-done.1, bf16[288,1024]{1,0:T(8,128)(2,1)S(1)} %shard_map.99), kind=kLoop, calls=%fused_computation | loop fusion | flops 1179648 | bytes 1769472 | tf_op jit(solution)/shard_map/convert_element_type | solution.py:384
  64.7 8.0 %all-to-all-done.2.packs_ref = bf16[4,144,640]{2,1,0:T(8,128)(2,1)S(1)} async-done(((bf16[4,144,640]{2,1,0:T(8,128)(2,1)}), bf16[4,144,640]{2,1,0:T(8,128)(2,1)S(1)}, u32[]{:S(2)}, u32[]{:S(2)}) %all-to-all-start.2) | async-done | bytes 737312 | tf_op jit(solution)/shard_map/all_to_all | solution.py:310
  72.7 3.6 %all-to-all-start.1 = ((bf16[12,24,1024]{2,1,0:T(8,128)(2,1)}), bf16[12,24,1024]{2,1,0:T(8,128)(2,1)S(1)}, u32[]{:S(2)}, u32[]{:S(2)}) async-start(bf16[12,24,1024]{2,1,0:T(8,128)(2,1)} %bitcast.9), calls=%async_computation.1 | async-start | bytes 1179648 | tf_op jit(solution)/shard_map/all_to_all | solution.py:310
  76.4 1.0 shard_map.94
  77.4 2.2 %all_gather.12.cols_ref = bf16[4,288,256]{2,1,0:T(8,128)(2,1)S(1)} all-gather(bf16[4,144,256]{2,1,0:T(8,128)(2,1)S(1)} %slice.4), channel_id=1, replica_groups=mesh['y4'=2,'y2'=2,'y1'=2,'x'=4,'expert'=12,'tensor'=2] {'tensor'}, dimensions={1}, use_global_device_ids=true | all-gather | bytes 884736 | tf_op jit(solution)/shard_map/all_gather | solution.py:316
  79.6 0.8 shard_map.100
  80.4 7.6 %all_gather.13.pair_ref = bf16[2,256,384]{2,1,0:T(8,128)(2,1)S(1)} all-gather(bf16[2,128,384]{2,1,0:T(8,128)(2,1)S(1)} %get-tuple-element.43), channel_id=1, replica_groups=mesh['y4'=2,'y2'=2,'y1'=2,'x'=4,'expert'=12,'tensor'=2] {'y1'}, dimensions={1}, use_global_device_ids=true | all-gather | bytes 589824 | tf_op jit(solution)/shard_map/all_gather | solution.py:316
  88.0 0.1 shard_map.101
  88.1 7.6 %all_gather.14.pair_ref = bf16[2,128,384]{2,1,0:T(8,128)(2,1)S(1)} all-gather(bf16[2,64,384]{2,1,0:T(8,128)(2,1)S(1)} %get-tuple-element.45), channel_id=1, replica_groups=mesh['y4'=2,'y2'=2,'y1'=2,'x'=4,'expert'=12,'tensor'=2] {'y2'}, dimensions={1}, use_global_device_ids=true | all-gather | bytes 294912 | tf_op jit(solution)/shard_map/all_gather | solution.py:316
  95.8 8.7 %all_gather.15.pair_ref = bf16[2,64,384]{2,1,0:T(8,128)(2,1)S(1)} all-gather(bf16[2,32,384]{2,1,0:T(8,128)(2,1)S(1)} %get-tuple-element.47), channel_id=1, replica_groups=mesh['y4'=2,'y2'=2,'y1'=2,'x'=4,'expert'=12,'tensor'=2] {'y4'}, dimensions={1}, use_global_device_ids=true | all-gather | bytes 147456 | tf_op jit(solution)/shard_map/all_gather | solution.py:316
  104.4 0.0 all-to-all-done.1
  104.4 1.3 %shard_map.103 = (bf16[128,1024]{1,0:T(8,128)(2,1)}, bf16[128,1024]{1,0:T(8,128)(2,1)}, bf16[64,384]{1,0:T(8,128)(2,1)}) custom-call(s32[1]{0:T(128)} %bitcast.bit_ref, bf16[128,288]{1,0:T(8,128)(2,1)S(1)} %get-tuple-element.27.high_ref, bf16[128,288]{1,0:T(8,128)(2,1)S(1)} %get-tuple-element.28.low_ref, bf16[128,288]{1,0:T(8,128)(2,1)S(1)} %get-tuple-element.29.right_ref, ...), custom_call_target="tpu_custom_call" | custom-call | flops 226492416 | bytes 1531908 | tf_op jit(solution)/shard_map/pallas_call | solution.py:37
  (2 shorter events, 0.0 us)
Async XLA Ops:
  44.0 4.7 %collective-permute-start = (bf16[288,1024]{1,0:T(8,128)(2,1)S(1)}, bf16[288,1024]{1,0:T(8,128)(2,1)S(1)}, u32[]{:S(2)}, u32[]{:S(2)}) collective-permute-start(bf16[288,1024]{1,0:T(8,128)(2,1)S(1)} %bitcast.16), channel_id=1, source_target_pairs={{0,1},{1,0},{2,3},{3,2},{4,5},{5,4},{6,7},{7,6},{8,9},{9,8},{10,11... | collective-permute-start | bytes 1769480 | tf_op jit(solution)/shard_map/ppermute | solution.py:313
  54.1 9.6 %collective-permute-start.1 = (bf16[288,1024]{1,0:T(8,128)(2,1)S(1)}, bf16[288,1024]{1,0:T(8,128)(2,1)S(1)}, u32[]{:S(2)}, u32[]{:S(2)}) collective-permute-start(bf16[288,1024]{1,0:T(8,128)(2,1)S(1)} %get-tuple-element.40), channel_id=1, source_target_pairs={{0,1},{1,0},{2,3},{3,2},{4,5},{5,4},{6,7},{7,6},{8,9},{9,8},{10,11... | collective-permute-start | bytes 1769480 | tf_op jit(solution)/shard_map/ppermute | solution.py:313
  56.5 16.2 %all-to-all-start.2 = ((bf16[4,144,640]{2,1,0:T(8,128)(2,1)}), bf16[4,144,640]{2,1,0:T(8,128)(2,1)S(1)}, u32[]{:S(2)}, u32[]{:S(2)}) async-start(bf16[4,144,640]{2,1,0:T(8,128)(2,1)} %get-tuple-element.41), calls=%async_computation.2 | async-start | bytes 1474560 | tf_op jit(solution)/shard_map/all_to_all | solution.py:310
  72.7 31.7 %all-to-all-start.1 = ((bf16[12,24,1024]{2,1,0:T(8,128)(2,1)}), bf16[12,24,1024]{2,1,0:T(8,128)(2,1)S(1)}, u32[]{:S(2)}, u32[]{:S(2)}) async-start(bf16[12,24,1024]{2,1,0:T(8,128)(2,1)} %bitcast.9), calls=%async_computation.1 | async-start | bytes 1179648 | tf_op jit(solution)/shard_map/all_to_all | solution.py:310
